TPU v7x, 32 devices: a whole 2x2x4 slice. The times are simulated.
32 devices in a mesh: rows: 8 (over y, x, core), blk: 4 (over z).
Axes of the slice: x: 2, y: 2, z: 4, core: 2. Of those that a mesh axis runs over, the one named last changes fastest.
Arguments:
- vectors: float32 [6144, 128], P('blk'), may hold values from -6 to 6
- left_intersection: float32 [256, 128, 128], P(('rows', 'blk')), may hold values from -0.5 to 0.5
- right_intersection: float32 [48, 128, 128], P('blk'), may hold values from -0.5 to 0.5
- tiles: float32 [512, 128, 128], P('rows'), may hold values from -0.09375 to 0.09375
- pair_cols: int32 [256, 32], P(('rows', 'blk')), may hold values from 0 to 47, all different within a row
- pair_owner: int32 [256, 32], P(('rows', 'blk')), may hold values from 0 to 7, as said below
- pair_slot: int32 [256, 32], P(('rows', 'blk')), may hold values from 0 to 63
- pair_counts: int32 [256], P(('rows', 'blk')), may hold values from 1 to 32, as said below
Outputs:
- product: float32 [32768, 128], P(('rows', 'blk'))
Inputs may be any that keep to these rules, and one draw needn't show every extreme that they name: `pair_owner`: among the 256 entries of each aligned block of 8 row blocks, every rows index appears exactly 32 times. `pair_cols`: the column blocks listed for one row block are distinct. `pair_counts`: some row block has all 32 entries live.
All inputs are finite; a program needn't handle non-finite values.
Results may differ from a plain program's by a relative error of at most 0.0003.
Values sent between devices are 32-bit elements; how exact they have to be, the bound alone decides.
No kernel may reach another device: no remote copies, remote signals or barrier semaphores. Data moves between devices by JAX's collectives and lax.ppermute only.
A program may use at most 128 MiB of HBM per device.

v0:
```python
import functools

import jax
import jax.numpy as jnp
from jax import lax
from jax.experimental import pallas as pl
from jax.experimental.pallas import tpu as pltpu
from jax.sharding import PartitionSpec as P


F32 = jnp.float32
BF16 = jnp.bfloat16
I32 = jnp.int32
UNROLL = 8
MIB = 1 << 20


VMEM = pl.BlockSpec(memory_space=pltpu.VMEM)
HBM = pl.BlockSpec(memory_space=pltpu.HBM)
SMEM = pl.BlockSpec(memory_space=pltpu.SMEM)


def in_hbm(x):
    return pltpu.with_memory_space_constraint(x, pltpu.HBM)


def cost(flops, nbytes):
    return pl.CostEstimate(flops=flops, bytes_accessed=nbytes, transcendentals=0)


def split(x):
    hi = x.astype(BF16)
    return hi, (x - hi.astype(F32)).astype(BF16)


def lanes(shape):
    return lax.broadcasted_iota(I32, shape, len(shape) - 1)


def triple(a, b, dims):
    a_hi, a_lo = split(a)
    b_hi, b_lo = split(b)

    def dot(x, y):
        return lax.dot_general(x, y, (dims, ((), ())), preferred_element_type=F32)

    return dot(a_hi, b_hi) + dot(a_hi, b_lo) + dot(a_lo, b_hi)


def fold_halves(x):
    half = x.shape[0] // 2
    top, bottom = x[:half], x[half:]
    low = lanes(top.shape) < half
    first = jnp.where(low, top, pltpu.roll(bottom, half, 1))
    second = jnp.where(low, pltpu.roll(top, half, 1), bottom)
    return first, second


def unfold_halves(first, second):
    half = first.shape[0]
    low = lanes(first.shape) < half
    top = jnp.where(low, first, pltpu.roll(second, half, 1))
    bottom = jnp.where(low, pltpu.roll(first, half, 1), second)
    return top, bottom


def send_kernel(place, v_ref, r_ref, out_ref, v_buf, r_buf, sems):
    part = place[1]
    count = v_buf.shape[0]
    first_block = place[0] * count
    copies = [
        pltpu.make_async_copy(ref.at[pl.ds(first_block, count)], buf, sems.at[i])
        for i, (ref, buf) in enumerate(((v_ref, v_buf), (r_ref, r_buf)))
    ]
    for copy in copies:
        copy.start()
    for copy in copies:
        copy.wait()
    for i in range(count):
        first, second = fold_halves(triple(r_buf[i], v_buf[i], ((0,), (0,))))
        out_ref[part, i] = first
        out_ref[1 - part, i] = second


def own_kernel(place, v_ref, r_ref, out_ref, v_buf, r_buf, sems):
    keep_first = place[1] == 0
    count = v_buf.shape[0]
    copies = [
        pltpu.make_async_copy(ref, buf, sems.at[i])
        for i, (ref, buf) in enumerate(((v_ref, v_buf), (r_ref, r_buf)))
    ]
    for copy in copies:
        copy.start()
    for copy in copies:
        copy.wait()
    for i in range(count):
        first, second = fold_halves(triple(r_buf[i], v_buf[i], ((0,), (0,))))
        out_ref[i] = jnp.where(keep_first, first, second)


def list_kernel(chips, held, cols, owner, slot, counts, out_ref, words, sems):
    blocks, listed = cols.shape
    span = out_ref.shape[2]
    copies = [
        pltpu.make_async_copy(ref, words.at[i], sems.at[i])
        for i, ref in enumerate((cols, owner, slot))
    ]
    for copy in copies:
        copy.start()
    for copy in copies:
        copy.wait()
    kinds = lax.broadcasted_iota(I32, (16, listed), 0)
    upto = lax.broadcasted_iota(I32, (listed, listed), 0) <= lanes((listed, listed))
    upto = upto.astype(F32).astype(BF16)
    spots = lax.broadcasted_iota(I32, (chips * span, listed), 0).astype(F32)
    offset = jnp.zeros((16, 1), F32)
    total = jnp.zeros((8, chips * span), F32)
    for i in range(blocks):
        col, own, place = words[0, i : i + 1], words[1, i : i + 1], words[2, i : i + 1]
        chip = jnp.where(lanes((1, listed)) < counts[i], own >> 1, chips)
        match = (kinds == chip).astype(F32)
        ranks = jnp.dot(match.astype(BF16), upto, preferred_element_type=F32) + offset
        offset = offset + jnp.sum(match, axis=1, keepdims=True)
        rank = jnp.sum(match * ranks, axis=0, keepdims=True) - 1
        target = jnp.where(chip < chips, chip.astype(F32) * span + rank, -1.0)
        chosen = (spots == target).astype(F32).astype(BF16)
        one = jnp.ones((1, listed), F32)
        fields = jnp.concatenate(
            [
                one,
                ((own & 1) * held + place).astype(F32),
                col.astype(F32),
                one * (i - blocks),
                jnp.zeros((4, listed), F32),
            ],
            axis=0,
        )
        total += lax.dot_general(
            fields.astype(BF16), chosen, (((1,), (1,)), ((), ())), preferred_element_type=F32
        )
    row = lax.broadcasted_iota(I32, (8, span), 0)
    for c in range(chips):
        part = total[:, c * span : (c + 1) * span]
        number = jnp.broadcast_to(offset[c : c + 1], (8, span))
        part = jnp.where(row == 0, number, jnp.where(row == 3, part + blocks, part))
        out_ref[c] = part[:4].astype(I32)


def tile_kernel(core, own_ref, other_ref, out_ref, buf, sems):
    held, _, width = own_ref.shape
    step = buf.shape[1]
    steps = held // step
    mine = core[0]
    refs = (own_ref, other_ref)

    def copy(s):
        ref, at = refs[s // steps], s % steps * step
        return pltpu.make_async_copy(ref.at[pl.ds(at, step)], buf.at[s % 2], sems.at[s % 2])

    copy(0).start()
    for s in range(2 * steps):
        if s + 1 < 2 * steps:
            copy(s + 1).start()
        copy(s).wait()
        whose = mine if s < steps else 1 - mine
        start = whose * held + s % steps * step

        def one(i, _):
            hi, lo = split(buf[s % 2, i])
            out_ref[start + i, :, :width] = hi
            out_ref[start + i, :, width:] = lo
            return 0

        lax.fori_loop(0, step, one, 0, unroll=4)


def gather_kernel(planes, place, own_ref, *refs):
    pieces, out_ref = refs[:-1], refs[-1]
    count, half, width = own_ref.shape
    quarter = count // 4
    blk = place[2]
    low = lanes((half, width)) < half
    zero = jnp.zeros((half, width), F32)

    def put(src, start, n):
        for i in range(n):
            x = src[i]
            hi = x.astype(BF16).astype(F32)
            lo = pltpu.roll(x - hi, half, 1)
            out_ref[start + i, 0 * half : 1 * half] = jnp.where(low, hi, lo).astype(BF16)
            out_ref[start + i, 1 * half : 2 * half] = jnp.where(low, lo, hi).astype(BF16)
            out_ref[start + i, 2 * half : 3 * half] = jnp.where(low, hi, zero).astype(BF16)
            out_ref[start + i, 3 * half : 4 * half] = jnp.where(low, zero, hi).astype(BF16)

    put(own_ref, blk * count, count)
    for k in range(1, planes):
        plane = lax.rem(blk - k + planes, planes)
        for p in range(4):
            put(pieces[(k - 1) * 4 + p], plane * count + place[3 + p] * quarter, quarter)


def entry_kernel(g, lists, tiles_ref, proj_ref, out_ref, acc):
    blocks, half, width = out_ref.shape
    acc[...] = jnp.zeros_like(acc)

    def step(s, _):
        base = s * UNROLL
        terms = [
            jnp.dot(
                tiles_ref[lists[g, 1, base + u]],
                proj_ref[lists[g, 2, base + u]],
                preferred_element_type=F32,
            )
            for u in range(UNROLL)
        ]
        for u in range(UNROLL):
            acc[lists[g, 3, base + u]] += terms[u]
        return 0

    lax.fori_loop(0, (lists[g, 0, 0] + UNROLL - 1) // UNROLL, step, 0)
    low = lanes((half, width)) < half
    for i in range(blocks):
        top, bottom = acc[i, :half], acc[i, half:]
        a, b = jnp.where(low, top, bottom), jnp.where(low, bottom, top)
        out_ref[i] = a + pltpu.roll(b, half, 1)


def final_kernel(place, left_ref, own_a, own_b, own_c, other, out_ref):
    blocks, _, _ = own_a.shape
    keep_first = place[1] == 0
    for i in range(blocks):
        own = own_a[i] + own_b[i] + own_c[i]
        first = jnp.where(keep_first, own, other[i])
        second = jnp.where(keep_first, other[i], own)
        top, bottom = unfold_halves(first, second)
        summed = jnp.concatenate([top, bottom], axis=0)
        out_ref[i] = triple(left_ref[i], summed, ((1,), (0,)))


def call(kernel, prefetch, ins, out, scratch, args, estimate, limit, grid=(), out_spec=VMEM):
    return pl.pallas_call(
        kernel,
        out_shape=out,
        grid_spec=pltpu.PrefetchScalarGridSpec(
            num_scalar_prefetch=prefetch,
            grid=grid,
            in_specs=ins,
            out_specs=out_spec,
            scratch_shapes=scratch,
        ),
        compiler_params=pltpu.CompilerParams(vmem_limit_bytes=limit),
        cost_estimate=estimate,
    )(*args)


def work(
    vectors, left, right, tiles, pair_cols, pair_owner, pair_slot, pair_counts
):
    rows, planes = lax.axis_size("rows"), lax.axis_size("blk")
    row, blk = lax.axis_index("rows"), lax.axis_index("blk")
    blocks, fine, coarse = left.shape
    vecs = vectors.shape[1]
    count = right.shape[0]
    held = tiles.shape[0]
    listed = pair_cols.shape[1]
    chips = rows // 2
    bits = chips.bit_length() - 1
    cap = blocks * listed // chips
    half = coarse // 2
    quarter = count // 4
    core, chip = row & 1, row >> 1
    b0, b1 = chip & 1, (chip >> 1) & 1
    part = blk & 1

    def physical(mask, core_at):
        return mask if core_at == 0 else (mask & ~3) | ((mask & 1) << 1) | ((mask >> 1) & 1)

    def across(mask):
        return [(r, r ^ (physical(mask, r % 2) << 1)) for r in range(rows)]

    def swap(x):
        return lax.ppermute(x, "rows", [(r, r ^ 1) for r in range(rows)])

    def turn(x, k):
        return lax.ppermute(x, "blk", [(b, (b + k) % planes) for b in range(planes)])

    def mate(x):
        return lax.ppermute(x, "blk", [(b, b ^ 1) for b in range(planes)])

    mine = jnp.where(core == 0, b0, 2 + b1)
    theirs = jnp.where(core == 0, 2 + b1, b0)
    place = jnp.stack([mine, part, blk, mine, mine ^ 1, theirs, theirs ^ 1]).astype(I32)

    v = vectors.reshape(count, fine, vecs)
    v, right = in_hbm(v), in_hbm(right)

    def blocks_of(n):
        return [pltpu.VMEM((n, fine, vecs), F32)] * 2 + [pltpu.SemaphoreType.DMA((2,))]

    sent = call(
        send_kernel, 1, [HBM, HBM],
        jax.ShapeDtypeStruct((2, quarter, half, vecs), F32),
        blocks_of(quarter), (place, v, right),
        cost(2 * quarter * 128**3 * 3, 2 * quarter * 65536), 8 * MIB,
    )
    arrived = {k: turn(sent[k % 2], k) for k in range(1, planes)}
    other_tiles = swap(tiles)

    span = pl.cdiv(cap, 128) * 128
    lists = call(
        functools.partial(list_kernel, chips, held), 0, [HBM] * 3 + [SMEM],
        jax.ShapeDtypeStruct((chips, 4, span), I32),
        [pltpu.VMEM((3, blocks, listed), I32), pltpu.SemaphoreType.DMA((3,))],
        (in_hbm(pair_cols), in_hbm(pair_owner), in_hbm(pair_slot), pair_counts),
        cost(10**8, 16384), 8 * MIB,
    )
    gathered = jnp.stack([lists, mate(lists)], axis=1)
    tables = {}
    for m in range(chips):
        to_chip = chip ^ jnp.where(core == 0, physical(m, 0), physical(m, 1))
        chosen = lax.dynamic_index_in_dim(gathered, to_chip, 0, keepdims=False)
        tables[m] = chosen if m == 0 else lax.ppermute(chosen, "rows", across(m))

    own = call(
        own_kernel, 1, [HBM, HBM],
        jax.ShapeDtypeStruct((count, half, vecs), F32),
        blocks_of(count), (place, v, right), cost(2 * count * 128**3 * 3, 2 * count * 65536), 8 * MIB,
    )
    packed = call(
        tile_kernel, 1, [HBM, HBM],
        jax.ShapeDtypeStruct((2 * held, coarse, 2 * coarse), BF16),
        [pltpu.VMEM((2, 16, coarse, coarse), F32), pltpu.SemaphoreType.DMA((2,))],
        (core.reshape(1).astype(I32), in_hbm(tiles), in_hbm(other_tiles)),
        cost(held * 65536 * 4, held * 65536 * 4), 12 * MIB,
    )

    pieces = []
    for k in range(1, planes):
        z = arrived[k]
        x = lax.ppermute(z, "rows", across(1))
        pieces += [z, x, swap(z), swap(x)]
    proj = call(
        functools.partial(gather_kernel, planes), 1, [VMEM] * (1 + len(pieces)),
        jax.ShapeDtypeStruct((planes * count, 2 * coarse, vecs), BF16),
        [], (place, own, *pieces), cost(10**6, 3 * planes * count * 32768), 16 * MIB,
    )

    def partial_sum(m, g):
        return call(
            functools.partial(entry_kernel, g), 1, [VMEM, VMEM],
            jax.ShapeDtypeStruct((blocks, half, vecs), F32),
            [pltpu.VMEM((blocks + 1, coarse, vecs), F32)],
            (tables[m], packed, proj),
            cost(cap * 128**3 * 4, 4 * MIB), 12 * MIB,
        )

    def reduce_over_chips(g):
        total = {m: [partial_sum(m, g)] for m in range(chips)}
        for j in range(bits):
            bit = 1 << j
            for m in sorted((m for m in range(chips) if m & bit and not m & (bit - 1)), reverse=True):
                value = functools.reduce(jnp.add, total[m])
                total[m ^ bit].append(lax.ppermute(value, "rows", across(bit)))
        return total[0]

    other = mate(functools.reduce(jnp.add, reduce_over_chips(1)))
    sums = reduce_over_chips(0)
    while len(sums) > 3:
        sums = [sums[0] + sums[1]] + sums[2:]
    result = call(
        final_kernel, 1, [VMEM] * 5,
        jax.ShapeDtypeStruct((blocks, fine, vecs), F32),
        [], (place, left, *sums, other), cost(2 * blocks * 128**3 * 3, 2 * MIB), 8 * MIB,
    )
    return result.reshape(blocks * fine, vecs)


def solution(mesh):
    return jax.shard_map(
        work,
        mesh=mesh,
        in_specs=(
            P("blk", None),
            P(("rows", "blk"), None, None),
            P("blk", None, None),
            P("rows", None, None),
            P(("rows", "blk"), None),
            P(("rows", "blk"), None),
            P(("rows", "blk"), None),
            P(("rows", "blk")),
        ),
        out_specs=P(("rows", "blk"), None),
        check_vma=False,
    )
```

profile of v0, /device:TPU:16, one launch (start us, length us, event | category | flops | bytes accessed | tf_op | source)
XLA Modules:
  0.0 74.9 jit_solution(3974445903052979172)
XLA Ops:
  0.0 0.1 stack.37.place
  0.1 1.9 %shard_map.85 = f32[2,3,64,128]{3,2,1,0:T(8,128)S(1)} custom-call(s32[7]{0:T(128)S(1)} %stack.37.place, f32[12,128,128]{2,1,0:T(8,128)} %bitcast.24, f32[12,128,128]{2,1,0:T(8,128)} %r_ref.3), custom_call_target="tpu_custom_call" | custom-call | flops 37748736 | bytes 393216 | tf_op jit(solution)/shard_map/pallas_call | solution.py:241
  2.0 1.6 %collective-permute-start.2 = (f32[3,64,128]{2,1,0:T(8,128)S(1)}, f32[3,64,128]{2,1,0:T(8,128)S(1)}, u32[]{:S(2)}, u32[]{:S(2)}) collective-permute-start(f32[3,64,128]{2,1,0:T(8,128)S(1)} %get-tuple-element.6), channel_id=1, source_target_pairs={{0,1},{1,2},{2,3},{3,0},{4,5},{5,6},{6,7},{7,4},{8,9},{9,10},{10,1... | collective-permute-start | bytes 294920 | tf_op jit(solution)/shard_map/ppermute | solution.py:285
  3.7 0.3 collective-permute-start.6
  4.0 1.2 %collective-permute-start.10 = (f32[3,64,128]{2,1,0:T(8,128)S(1)}, f32[3,64,128]{2,1,0:T(8,128)S(1)}, u32[]{:S(2)}, u32[]{:S(2)}) collective-permute-start(f32[3,64,128]{2,1,0:T(8,128)S(1)} %get-tuple-element.6), channel_id=1, source_target_pairs={{0,3},{1,0},{2,1},{3,2},{4,7},{5,4},{6,5},{7,6},{8,11},{9,8},{10,9... | collective-permute-start | bytes 294920 | tf_op jit(solution)/shard_map/ppermute | solution.py:285
  5.2 6.8 %collective-permute-done.2.refs_0_ = f32[3,64,128]{2,1,0:T(8,128)S(1)} collective-permute-done((f32[3,64,128]{2,1,0:T(8,128)S(1)}, f32[3,64,128]{2,1,0:T(8,128)S(1)}, u32[]{:S(2)}, u32[]{:S(2)}) %collective-permute-start.2) | collective-permute-done | bytes 98336 | tf_op jit(solution)/shard_map/ppermute | solution.py:285
  12.0 1.5 %collective-permute-start.3 = (f32[3,64,128]{2,1,0:T(8,128)S(1)}, f32[3,64,128]{2,1,0:T(8,128)S(1)}, u32[]{:S(2)}, u32[]{:S(2)}) collective-permute-start(f32[3,64,128]{2,1,0:T(8,128)S(1)} %collective-permute-done.2.refs_0_), channel_id=1, source_target_pairs={{0,8},{4,20},{8,0},{12,28},{16,24},{20,4},{24,16},{28,12},{1,9},{5... | collective-permute-start | bytes 294920 | tf_op jit(solution)/shard_map/ppermute | solution.py:340
  13.5 0.7 copy-done.1
  14.1 2.6 %shard_map.82 = s32[4,4,128]{2,1,0:T(4,128)S(1)} custom-call(s32[8,32]{1,0:T(8,128)} %cols.1, s32[8,32]{1,0:T(8,128)} %owner.1, s32[8,32]{1,0:T(8,128)} %slot.1, s32[8]{0:T(128)S(1)} %copy-done.1), custom_call_target="tpu_custom_call" | custom-call | flops 100000000 | bytes 16384 | tf_op jit(solution)/shard_map/pallas_call | solution.py:241
  16.8 0.1 collective-permute-start
  16.8 3.6 %collective-permute-done = s32[4,4,128]{2,1,0:T(4,128)S(1)} collective-permute-done((s32[4,4,128]{2,1,0:T(4,128)S(1)}, s32[4,4,128]{2,1,0:T(4,128)S(1)}, u32[]{:S(2)}, u32[]{:S(2)}) %collective-permute-start) | collective-permute-done | bytes 8224 | tf_op jit(solution)/shard_map/ppermute | solution.py:288
  20.5 0.5 collective-permute-start.7
  21.0 1.2 %collective-permute-start.8 = (f32[3,64,128]{2,1,0:T(8,128)S(1)}, f32[3,64,128]{2,1,0:T(8,128)S(1)}, u32[]{:S(2)}, u32[]{:S(2)}) collective-permute-start(f32[3,64,128]{2,1,0:T(8,128)S(1)} %collective-permute-done.6.refs_4_), channel_id=1, source_target_pairs={{0,4},{4,0},{8,12},{12,8},{16,20},{20,16},{24,28},{28,24},{1,5},{5... | collective-permute-start | bytes 294920 | tf_op jit(solution)/shard_map/ppermute | solution.py:282
  22.2 0.0 collective-permute-done.3.refs_1_
  22.2 0.5 collective-permute-start.11
  22.8 0.0 collective-permute-done.4.refs_2_
  22.8 0.0 collective-permute-start.12
  22.8 2.3 %collective-permute-done.7.refs_5_ = f32[3,64,128]{2,1,0:T(8,128)S(1)} collective-permute-done((f32[3,64,128]{2,1,0:T(8,128)S(1)}, f32[3,64,128]{2,1,0:T(8,128)S(1)}, u32[]{:S(2)}, u32[]{:S(2)}) %collective-permute-start.7) | collective-permute-done | bytes 98336 | tf_op jit(solution)/shard_map/ppermute | solution.py:340
  25.1 0.5 collective-permute-start.9
  25.6 1.2 %collective-permute-done.11.refs_9_ = f32[3,64,128]{2,1,0:T(8,128)S(1)} collective-permute-done((f32[3,64,128]{2,1,0:T(8,128)S(1)}, f32[3,64,128]{2,1,0:T(8,128)S(1)}, u32[]{:S(2)}, u32[]{:S(2)}) %collective-permute-start.11) | collective-permute-done | bytes 98336 | tf_op jit(solution)/shard_map/ppermute | solution.py:340
  26.9 0.0 collective-permute-done.12.refs_10_
  26.9 1.4 %collective-permute-start.17 = (s32[2,4,128]{2,1,0:T(4,128)S(1)}, s32[2,4,128]{2,1,0:T(4,128)S(1)}, u32[]{:S(2)}, u32[]{:S(2)}) collective-permute-start(s32[2,4,128]{2,1,0:T(4,128)S(1)} %get-tuple-element.7), channel_id=1, source_target_pairs={{0,24},{4,28},{8,16},{12,20},{16,8},{20,12},{24,0},{28,4},{1,25},{... | collective-permute-start | bytes 12296 | tf_op jit(solution)/shard_map/ppermute | solution.py:322
  28.3 2.5 %shard_map.84.own_ref = f32[12,64,128]{2,1,0:T(8,128)S(1)} custom-call(s32[7]{0:T(128)S(1)} %stack.37.place, f32[12,128,128]{2,1,0:T(8,128)} %bitcast.25, f32[12,128,128]{2,1,0:T(8,128)} %r_ref.3), custom_call_target="tpu_custom_call" | custom-call | flops 150994944 | bytes 1572864 | tf_op jit(solution)/shard_map/pallas_call | solution.py:241
  30.8 0.0 collective-permute-done.5.refs_3_
  30.8 0.0 collective-permute-done.9.refs_7_
  30.8 1.1 %shard_map.86.proj_ref = bf16[48,256,128]{2,1,0:T(8,128)(2,1)S(1)} custom-call(s32[7]{0:T(128)S(1)} %stack.37.place, f32[12,64,128]{2,1,0:T(8,128)S(1)} %shard_map.84.own_ref, f32[3,64,128]{2,1,0:T(8,128)S(1)} %collective-permute-done.2.refs_0_, f32[3,64,128]{2,1,0:T(8,128)S(1)} %collective-permute-done.3.refs_1_, ...), custom_call_target="tpu_custom_call" | custom-call | flops 1000000 | bytes 4718592 | tf_op jit(solution)/shard_map/pallas_call | solution.py:241
  31.9 6.1 %shard_map.83.tiles_ref = bf16[128,128,256]{2,1,0:T(8,128)(2,1)S(1)} custom-call(s32[1]{0:T(128)} %bitcast.9.core, f32[64,128,128]{2,1,0:T(8,128)} %own_ref.1, f32[64,128,128]{2,1,0:T(8,128)} %collective-permute-done.1.other_ref), custom_call_target="tpu_custom_call" | custom-call | flops 16777216 | bytes 16777216 | tf_op jit(solution)/shard_map/pallas_call | solution.py:241
  38.1 2.9 %shard_map.94 = f32[8,64,128]{2,1,0:T(8,128)S(1)} custom-call(s32[2,4,128]{2,1,0:T(4,128)S(1)} %collective-permute-done.17.lists, bf16[128,128,256]{2,1,0:T(8,128)(2,1)S(1)} %shard_map.83.tiles_ref, bf16[48,256,128]{2,1,0:T(8,128)(2,1)S(1)} %shard_map.86.proj_ref), custom_call_target="tpu_custom_call" | custom-call | flops 536870912 | bytes 4194304 | tf_op jit(solution)/shard_map/pallas_call | solution.py:241
  41.0 1.0 %collective-permute-start.21 = (f32[8,64,128]{2,1,0:T(8,128)S(1)}, f32[8,64,128]{2,1,0:T(8,128)S(1)}, u32[]{:S(2)}, u32[]{:S(2)}) collective-permute-start(f32[8,64,128]{2,1,0:T(8,128)S(1)} %shard_map.94), channel_id=1, source_target_pairs={{0,8},{4,20},{8,0},{12,28},{16,24},{20,4},{24,16},{28,12},{1,9},{5... | collective-permute-start | bytes 786440 | tf_op jit(solution)/shard_map/ppermute | solution.py:363
  42.0 1.1 %collective-permute-start.14 = (s32[2,4,128]{2,1,0:T(4,128)S(1)}, s32[2,4,128]{2,1,0:T(4,128)S(1)}, u32[]{:S(2)}, u32[]{:S(2)}) collective-permute-start(s32[2,4,128]{2,1,0:T(4,128)S(1)} %get-tuple-element.9), channel_id=1, source_target_pairs={{0,8},{4,20},{8,0},{12,28},{16,24},{20,4},{24,16},{28,12},{1,9},{5... | collective-permute-start | bytes 12296 | tf_op jit(solution)/shard_map/ppermute | solution.py:322
  43.1 0.7 collective-permute-start.16
  43.8 2.6 %shard_map.90 = f32[8,64,128]{2,1,0:T(8,128)S(1)} custom-call(s32[2,4,128]{2,1,0:T(4,128)S(1)} %collective-permute-done.17.lists, bf16[128,128,256]{2,1,0:T(8,128)(2,1)S(1)} %shard_map.83.tiles_ref, bf16[48,256,128]{2,1,0:T(8,128)(2,1)S(1)} %shard_map.86.proj_ref), custom_call_target="tpu_custom_call" | custom-call | flops 536870912 | bytes 4194304 | tf_op jit(solution)/shard_map/pallas_call | solution.py:241
  46.4 1.6 %collective-permute-start.18 = (f32[8,64,128]{2,1,0:T(8,128)S(1)}, f32[8,64,128]{2,1,0:T(8,128)S(1)}, u32[]{:S(2)}, u32[]{:S(2)}) collective-permute-start(f32[8,64,128]{2,1,0:T(8,128)S(1)} %shard_map.90), channel_id=1, source_target_pairs={{0,8},{4,20},{8,0},{12,28},{16,24},{20,4},{24,16},{28,12},{1,9},{5... | collective-permute-start | bytes 786440 | tf_op jit(solution)/shard_map/ppermute | solution.py:363
  47.9 2.6 %shard_map.92 = f32[8,64,128]{2,1,0:T(8,128)S(1)} custom-call(s32[2,4,128]{2,1,0:T(4,128)S(1)} %collective-permute-done.14.lists, bf16[128,128,256]{2,1,0:T(8,128)(2,1)S(1)} %shard_map.83.tiles_ref, bf16[48,256,128]{2,1,0:T(8,128)(2,1)S(1)} %shard_map.86.proj_ref), custom_call_target="tpu_custom_call" | custom-call | flops 536870912 | bytes 4194304 | tf_op jit(solution)/shard_map/pallas_call | solution.py:241
  50.5 0.9 %collective-permute-start.20 = (f32[8,64,128]{2,1,0:T(8,128)S(1)}, f32[8,64,128]{2,1,0:T(8,128)S(1)}, u32[]{:S(2)}, u32[]{:S(2)}) collective-permute-start(f32[8,64,128]{2,1,0:T(8,128)S(1)} %shard_map.92), channel_id=1, source_target_pairs={{0,8},{4,20},{8,0},{12,28},{16,24},{20,4},{24,16},{28,12},{1,9},{5... | collective-permute-start | bytes 786440 | tf_op jit(solution)/shard_map/ppermute | solution.py:363
  51.4 2.9 %shard_map.93 = f32[8,64,128]{2,1,0:T(8,128)S(1)} custom-call(s32[2,4,128]{2,1,0:T(4,128)S(1)} %collective-permute-done.16.lists, bf16[128,128,256]{2,1,0:T(8,128)(2,1)S(1)} %shard_map.83.tiles_ref, bf16[48,256,128]{2,1,0:T(8,128)(2,1)S(1)} %shard_map.86.proj_ref), custom_call_target="tpu_custom_call" | custom-call | flops 536870912 | bytes 4194304 | tf_op jit(solution)/shard_map/pallas_call | solution.py:241
  54.4 0.6 collective-permute-start.22
  55.0 1.7 %shard_map.88 = f32[8,64,128]{2,1,0:T(8,128)S(1)} custom-call(s32[2,4,128]{2,1,0:T(4,128)S(1)} %collective-permute-done.14.lists, bf16[128,128,256]{2,1,0:T(8,128)(2,1)S(1)} %shard_map.83.tiles_ref, bf16[48,256,128]{2,1,0:T(8,128)(2,1)S(1)} %shard_map.86.proj_ref), custom_call_target="tpu_custom_call" | custom-call | flops 536870912 | bytes 4194304 | tf_op jit(solution)/shard_map/pallas_call | solution.py:241
  56.7 3.0 %collective-permute-start.15 = (f32[8,64,128]{2,1,0:T(8,128)S(1)}, f32[8,64,128]{2,1,0:T(8,128)S(1)}, u32[]{:S(2)}, u32[]{:S(2)}) collective-permute-start(f32[8,64,128]{2,1,0:T(8,128)S(1)} %shard_map.88), channel_id=1, source_target_pairs={{0,8},{4,20},{8,0},{12,28},{16,24},{20,4},{24,16},{28,12},{1,9},{5... | collective-permute-start | bytes 786440 | tf_op jit(solution)/shard_map/ppermute | solution.py:363
  59.7 2.6 %shard_map.91 = f32[8,64,128]{2,1,0:T(8,128)S(1)} custom-call(s32[2,4,128]{2,1,0:T(4,128)S(1)} %get-tuple-element.8.lists, bf16[128,128,256]{2,1,0:T(8,128)(2,1)S(1)} %shard_map.83.tiles_ref, bf16[48,256,128]{2,1,0:T(8,128)(2,1)S(1)} %shard_map.86.proj_ref), custom_call_target="tpu_custom_call" | custom-call | flops 536870912 | bytes 4194304 | tf_op jit(solution)/shard_map/pallas_call | solution.py:241
  62.3 2.6 %shard_map.89 = f32[8,64,128]{2,1,0:T(8,128)S(1)} custom-call(s32[2,4,128]{2,1,0:T(4,128)S(1)} %collective-permute-done.16.lists, bf16[128,128,256]{2,1,0:T(8,128)(2,1)S(1)} %shard_map.83.tiles_ref, bf16[48,256,128]{2,1,0:T(8,128)(2,1)S(1)} %shard_map.86.proj_ref), custom_call_target="tpu_custom_call" | custom-call | flops 536870912 | bytes 4194304 | tf_op jit(solution)/shard_map/pallas_call | solution.py:241
  65.0 1.6 %collective-permute-start.19 = (f32[8,64,128]{2,1,0:T(8,128)S(1)}, f32[8,64,128]{2,1,0:T(8,128)S(1)}, u32[]{:S(2)}, u32[]{:S(2)}) collective-permute-start(f32[8,64,128]{2,1,0:T(8,128)S(1)} %add.34), channel_id=1, source_target_pairs={{0,16},{4,12},{8,24},{12,4},{16,0},{20,28},{24,8},{28,20},{1,17},{... | collective-permute-start | bytes 786440 | tf_op jit(solution)/shard_map/ppermute | solution.py:363
  66.6 0.0 copy-start
  66.6 0.1 collective-permute-start.23
  66.7 2.6 %shard_map.87.own_a = f32[8,64,128]{2,1,0:T(8,128)S(1)} custom-call(s32[2,4,128]{2,1,0:T(4,128)S(1)} %get-tuple-element.8.lists, bf16[128,128,256]{2,1,0:T(8,128)(2,1)S(1)} %shard_map.83.tiles_ref, bf16[48,256,128]{2,1,0:T(8,128)(2,1)S(1)} %shard_map.86.proj_ref), custom_call_target="tpu_custom_call" | custom-call | flops 536870912 | bytes 4194304 | tf_op jit(solution)/shard_map/pallas_call | solution.py:241
  69.3 2.1 %collective-permute-done.19.own_c = f32[8,64,128]{2,1,0:T(8,128)S(1)} collective-permute-done((f32[8,64,128]{2,1,0:T(8,128)S(1)}, f32[8,64,128]{2,1,0:T(8,128)S(1)}, u32[]{:S(2)}, u32[]{:S(2)}) %collective-permute-start.19) | collective-permute-done | bytes 262176 | tf_op jit(solution)/shard_map/ppermute | solution.py:363
  71.4 1.6 %collective-permute-done.23.other = f32[8,64,128]{2,1,0:T(8,128)S(1)} collective-permute-done((f32[8,64,128]{2,1,0:T(8,128)S(1)}, f32[8,64,128]{2,1,0:T(8,128)S(1)}, u32[]{:S(2)}, u32[]{:S(2)}) %collective-permute-start.23) | collective-permute-done | bytes 262176 | tf_op jit(solution)/shard_map/ppermute | solution.py:288
  73.1 1.8 %shard_map.95 = f32[8,128,128]{2,1,0:T(8,128)} custom-call(s32[7]{0:T(128)S(1)} %stack.37.place, f32[8,128,128]{2,1,0:T(8,128)S(1)} %copy-done, f32[8,64,128]{2,1,0:T(8,128)S(1)} %shard_map.87.own_a, f32[8,64,128]{2,1,0:T(8,128)S(1)} %collective-permute-done.15.own_b, f32[8,64,128]{2,1,0:T(8,128)S(1)} %collective-permute-done.19.own_c, ...), custom_call_target="tpu_custom_call" | custom-call | flops 100663296 | bytes 2097152 | tf_op jit(solution)/shard_map/pallas_call | solution.py:241
  (24 shorter events, 0.2 us)
Async XLA Ops:
  0.0 31.9 %collective-permute-start.1 = (f32[64,128,128]{2,1,0:T(8,128)}, f32[64,128,128]{2,1,0:T(8,128)}, u32[]{:S(2)}, u32[]{:S(2)}) collective-permute-start(f32[64,128,128]{2,1,0:T(8,128)} %own_ref.1), channel_id=1, source_target_pairs={{0,4},{4,0},{8,12},{12,8},{16,20},{20,16},{24,28},{28,24},{1,5},{5... | collective-permute-start | bytes 12582920 | tf_op jit(solution)/shard_map/ppermute | solution.py:282
  2.0 9.9 %collective-permute-start.2 = (f32[3,64,128]{2,1,0:T(8,128)S(1)}, f32[3,64,128]{2,1,0:T(8,128)S(1)}, u32[]{:S(2)}, u32[]{:S(2)}) collective-permute-start(f32[3,64,128]{2,1,0:T(8,128)S(1)} %get-tuple-element.6), channel_id=1, source_target_pairs={{0,1},{1,2},{2,3},{3,0},{4,5},{5,6},{6,7},{7,4},{8,9},{9,10},{10,1... | collective-permute-start | bytes 294920 | tf_op jit(solution)/shard_map/ppermute | solution.py:285
  3.7 16.8 %collective-permute-start.6 = (f32[3,64,128]{2,1,0:T(8,128)S(1)}, f32[3,64,128]{2,1,0:T(8,128)S(1)}, u32[]{:S(2)}, u32[]{:S(2)}) collective-permute-start(f32[3,64,128]{2,1,0:T(8,128)S(1)} %get-tuple-element.5), channel_id=1, source_target_pairs={{0,2},{1,3},{2,0},{3,1},{4,6},{5,7},{6,4},{7,5},{8,10},{9,11},{10,... | collective-permute-start | bytes 294920 | tf_op jit(solution)/shard_map/ppermute | solution.py:285
  4.0 17.0 %collective-permute-start.10 = (f32[3,64,128]{2,1,0:T(8,128)S(1)}, f32[3,64,128]{2,1,0:T(8,128)S(1)}, u32[]{:S(2)}, u32[]{:S(2)}) collective-permute-start(f32[3,64,128]{2,1,0:T(8,128)S(1)} %get-tuple-element.6), channel_id=1, source_target_pairs={{0,3},{1,0},{2,1},{3,2},{4,7},{5,4},{6,5},{7,6},{8,11},{9,8},{10,9... | collective-permute-start | bytes 294920 | tf_op jit(solution)/shard_map/ppermute | solution.py:285
  12.0 10.3 %collective-permute-start.3 = (f32[3,64,128]{2,1,0:T(8,128)S(1)}, f32[3,64,128]{2,1,0:T(8,128)S(1)}, u32[]{:S(2)}, u32[]{:S(2)}) collective-permute-start(f32[3,64,128]{2,1,0:T(8,128)S(1)} %collective-permute-done.2.refs_0_), channel_id=1, source_target_pairs={{0,8},{4,20},{8,0},{12,28},{16,24},{20,4},{24,16},{28,12},{1,9},{5... | collective-permute-start | bytes 294920 | tf_op jit(solution)/shard_map/ppermute | solution.py:340
  13.5 0.7 copy-start.1
  16.8 3.7 %collective-permute-start = (s32[4,4,128]{2,1,0:T(4,128)S(1)}, s32[4,4,128]{2,1,0:T(4,128)S(1)}, u32[]{:S(2)}, u32[]{:S(2)}) collective-permute-start(s32[4,4,128]{2,1,0:T(4,128)S(1)} %shard_map.82), channel_id=1, source_target_pairs={{0,1},{1,0},{2,3},{3,2},{4,5},{5,4},{6,7},{7,6},{8,9},{9,8},{10,11... | collective-permute-start | bytes 24584 | tf_op jit(solution)/shard_map/ppermute | solution.py:288
  20.5 2.3 %collective-permute-start.4 = (f32[3,64,128]{2,1,0:T(8,128)S(1)}, f32[3,64,128]{2,1,0:T(8,128)S(1)}, u32[]{:S(2)}, u32[]{:S(2)}) collective-permute-start(f32[3,64,128]{2,1,0:T(8,128)S(1)} %collective-permute-done.2.refs_0_), channel_id=1, source_target_pairs={{0,4},{4,0},{8,12},{12,8},{16,20},{20,16},{24,28},{28,24},{1,5},{5... | collective-permute-start | bytes 294920 | tf_op jit(solution)/shard_map/ppermute | solution.py:282
  20.5 4.6 %collective-permute-start.7 = (f32[3,64,128]{2,1,0:T(8,128)S(1)}, f32[3,64,128]{2,1,0:T(8,128)S(1)}, u32[]{:S(2)}, u32[]{:S(2)}) collective-permute-start(f32[3,64,128]{2,1,0:T(8,128)S(1)} %collective-permute-done.6.refs_4_), channel_id=1, source_target_pairs={{0,8},{4,20},{8,0},{12,28},{16,24},{20,4},{24,16},{28,12},{1,9},{5... | collective-permute-start | bytes 294920 | tf_op jit(solution)/shard_map/ppermute | solution.py:340
  21.0 4.1 %collective-permute-start.8 = (f32[3,64,128]{2,1,0:T(8,128)S(1)}, f32[3,64,128]{2,1,0:T(8,128)S(1)}, u32[]{:S(2)}, u32[]{:S(2)}) collective-permute-start(f32[3,64,128]{2,1,0:T(8,128)S(1)} %collective-permute-done.6.refs_4_), channel_id=1, source_target_pairs={{0,4},{4,0},{8,12},{12,8},{16,20},{20,16},{24,28},{28,24},{1,5},{5... | collective-permute-start | bytes 294920 | tf_op jit(solution)/shard_map/ppermute | solution.py:282
  22.2 4.6 %collective-permute-start.11 = (f32[3,64,128]{2,1,0:T(8,128)S(1)}, f32[3,64,128]{2,1,0:T(8,128)S(1)}, u32[]{:S(2)}, u32[]{:S(2)}) collective-permute-start(f32[3,64,128]{2,1,0:T(8,128)S(1)} %collective-permute-done.10.refs_8_), channel_id=1, source_target_pairs={{0,8},{4,20},{8,0},{12,28},{16,24},{20,4},{24,16},{28,12},{1,9},{5... | collective-permute-start | bytes 294920 | tf_op jit(solution)/shard_map/ppermute | solution.py:340
  22.8 4.1 %collective-permute-start.12 = (f32[3,64,128]{2,1,0:T(8,128)S(1)}, f32[3,64,128]{2,1,0:T(8,128)S(1)}, u32[]{:S(2)}, u32[]{:S(2)}) collective-permute-start(f32[3,64,128]{2,1,0:T(8,128)S(1)} %collective-permute-done.10.refs_8_), channel_id=1, source_target_pairs={{0,4},{4,0},{8,12},{12,8},{16,20},{20,16},{24,28},{28,24},{1,5},{5... | collective-permute-start | bytes 294920 | tf_op jit(solution)/shard_map/ppermute | solution.py:282
  25.1 5.7 %collective-permute-start.5 = (f32[3,64,128]{2,1,0:T(8,128)S(1)}, f32[3,64,128]{2,1,0:T(8,128)S(1)}, u32[]{:S(2)}, u32[]{:S(2)}) collective-permute-start(f32[3,64,128]{2,1,0:T(8,128)S(1)} %collective-permute-done.3.refs_1_), channel_id=1, source_target_pairs={{0,4},{4,0},{8,12},{12,8},{16,20},{20,16},{24,28},{28,24},{1,5},{5... | collective-permute-start | bytes 294920 | tf_op jit(solution)/shard_map/ppermute | solution.py:282
  25.1 5.7 %collective-permute-start.9 = (f32[3,64,128]{2,1,0:T(8,128)S(1)}, f32[3,64,128]{2,1,0:T(8,128)S(1)}, u32[]{:S(2)}, u32[]{:S(2)}) collective-permute-start(f32[3,64,128]{2,1,0:T(8,128)S(1)} %collective-permute-done.7.refs_5_), channel_id=1, source_target_pairs={{0,4},{4,0},{8,12},{12,8},{16,20},{20,16},{24,28},{28,24},{1,5},{5... | collective-permute-start | bytes 294920 | tf_op jit(solution)/shard_map/ppermute | solution.py:282
  26.9 3.9 %collective-permute-start.13 = (f32[3,64,128]{2,1,0:T(8,128)S(1)}, f32[3,64,128]{2,1,0:T(8,128)S(1)}, u32[]{:S(2)}, u32[]{:S(2)}) collective-permute-start(f32[3,64,128]{2,1,0:T(8,128)S(1)} %collective-permute-done.11.refs_9_), channel_id=1, source_target_pairs={{0,4},{4,0},{8,12},{12,8},{16,20},{20,16},{24,28},{28,24},{1,5},{5... | collective-permute-start | bytes 294920 | tf_op jit(solution)/shard_map/ppermute | solution.py:282
  26.9 11.2 %collective-permute-start.17 = (s32[2,4,128]{2,1,0:T(4,128)S(1)}, s32[2,4,128]{2,1,0:T(4,128)S(1)}, u32[]{:S(2)}, u32[]{:S(2)}) collective-permute-start(s32[2,4,128]{2,1,0:T(4,128)S(1)} %get-tuple-element.7), channel_id=1, source_target_pairs={{0,24},{4,28},{8,16},{12,20},{16,8},{20,12},{24,0},{28,4},{1,25},{... | collective-permute-start | bytes 12296 | tf_op jit(solution)/shard_map/ppermute | solution.py:322
  41.0 13.3 %collective-permute-start.21 = (f32[8,64,128]{2,1,0:T(8,128)S(1)}, f32[8,64,128]{2,1,0:T(8,128)S(1)}, u32[]{:S(2)}, u32[]{:S(2)}) collective-permute-start(f32[8,64,128]{2,1,0:T(8,128)S(1)} %shard_map.94), channel_id=1, source_target_pairs={{0,8},{4,20},{8,0},{12,28},{16,24},{20,4},{24,16},{28,12},{1,9},{5... | collective-permute-start | bytes 786440 | tf_op jit(solution)/shard_map/ppermute | solution.py:363
  42.0 5.9 %collective-permute-start.14 = (s32[2,4,128]{2,1,0:T(4,128)S(1)}, s32[2,4,128]{2,1,0:T(4,128)S(1)}, u32[]{:S(2)}, u32[]{:S(2)}) collective-permute-start(s32[2,4,128]{2,1,0:T(4,128)S(1)} %get-tuple-element.9), channel_id=1, source_target_pairs={{0,8},{4,20},{8,0},{12,28},{16,24},{20,4},{24,16},{28,12},{1,9},{5... | collective-permute-start | bytes 12296 | tf_op jit(solution)/shard_map/ppermute | solution.py:322
  43.1 8.3 %collective-permute-start.16 = (s32[2,4,128]{2,1,0:T(4,128)S(1)}, s32[2,4,128]{2,1,0:T(4,128)S(1)}, u32[]{:S(2)}, u32[]{:S(2)}) collective-permute-start(s32[2,4,128]{2,1,0:T(4,128)S(1)} %get-tuple-element.10), channel_id=1, source_target_pairs={{0,16},{4,12},{8,24},{12,4},{16,0},{20,28},{24,8},{28,20},{1,17},{... | collective-permute-start | bytes 12296 | tf_op jit(solution)/shard_map/ppermute | solution.py:322
  46.4 18.6 %collective-permute-start.18 = (f32[8,64,128]{2,1,0:T(8,128)S(1)}, f32[8,64,128]{2,1,0:T(8,128)S(1)}, u32[]{:S(2)}, u32[]{:S(2)}) collective-permute-start(f32[8,64,128]{2,1,0:T(8,128)S(1)} %shard_map.90), channel_id=1, source_target_pairs={{0,8},{4,20},{8,0},{12,28},{16,24},{20,4},{24,16},{28,12},{1,9},{5... | collective-permute-start | bytes 786440 | tf_op jit(solution)/shard_map/ppermute | solution.py:363
  50.5 16.0 %collective-permute-start.20 = (f32[8,64,128]{2,1,0:T(8,128)S(1)}, f32[8,64,128]{2,1,0:T(8,128)S(1)}, u32[]{:S(2)}, u32[]{:S(2)}) collective-permute-start(f32[8,64,128]{2,1,0:T(8,128)S(1)} %shard_map.92), channel_id=1, source_target_pairs={{0,8},{4,20},{8,0},{12,28},{16,24},{20,4},{24,16},{28,12},{1,9},{5... | collective-permute-start | bytes 786440 | tf_op jit(solution)/shard_map/ppermute | solution.py:363
  54.4 12.2 %collective-permute-start.22 = (f32[8,64,128]{2,1,0:T(8,128)S(1)}, f32[8,64,128]{2,1,0:T(8,128)S(1)}, u32[]{:S(2)}, u32[]{:S(2)}) collective-permute-start(f32[8,64,128]{2,1,0:T(8,128)S(1)} %add.36), channel_id=1, source_target_pairs={{0,16},{4,12},{8,24},{12,4},{16,0},{20,28},{24,8},{28,20},{1,17},{... | collective-permute-start | bytes 786440 | tf_op jit(solution)/shard_map/ppermute | solution.py:363
  56.7 12.6 %collective-permute-start.15 = (f32[8,64,128]{2,1,0:T(8,128)S(1)}, f32[8,64,128]{2,1,0:T(8,128)S(1)}, u32[]{:S(2)}, u32[]{:S(2)}) collective-permute-start(f32[8,64,128]{2,1,0:T(8,128)S(1)} %shard_map.88), channel_id=1, source_target_pairs={{0,8},{4,20},{8,0},{12,28},{16,24},{20,4},{24,16},{28,12},{1,9},{5... | collective-permute-start | bytes 786440 | tf_op jit(solution)/shard_map/ppermute | solution.py:363
  65.0 6.4 %collective-permute-start.19 = (f32[8,64,128]{2,1,0:T(8,128)S(1)}, f32[8,64,128]{2,1,0:T(8,128)S(1)}, u32[]{:S(2)}, u32[]{:S(2)}) collective-permute-start(f32[8,64,128]{2,1,0:T(8,128)S(1)} %add.34), channel_id=1, source_target_pairs={{0,16},{4,12},{8,24},{12,4},{16,0},{20,28},{24,8},{28,20},{1,17},{... | collective-permute-start | bytes 786440 | tf_op jit(solution)/shard_map/ppermute | solution.py:363
  66.6 6.5 %copy-start = (f32[8,128,128]{2,1,0:T(8,128)S(1)}, f32[8,128,128]{2,1,0:T(8,128)}, u32[]{:S(2)}) copy-start(f32[8,128,128]{2,1,0:T(8,128)} %left_ref.1) | copy-start | bytes 1572868
  66.6 6.4 %collective-permute-start.23 = (f32[8,64,128]{2,1,0:T(8,128)S(1)}, f32[8,64,128]{2,1,0:T(8,128)S(1)}, u32[]{:S(2)}, u32[]{:S(2)}) collective-permute-start(f32[8,64,128]{2,1,0:T(8,128)S(1)} %add_add_fusion), channel_id=1, source_target_pairs={{0,1},{1,0},{2,3},{3,2},{4,5},{5,4},{6,7},{7,6},{8,9},{9,8},{10,11... | collective-permute-start | bytes 786440 | tf_op jit(solution)/shard_map/ppermute | solution.py:288
where the time goes:
time: 75.2 us; the launch traced here: 74.9 us
  Pallas kernels  36.6 us (49%)
  starting transfers between devices  19.4 us (26%)
  waiting for transfers between devices  17.8 us (24%)
  local copies, waits for them, and re-layouts  0.76 us (1%)
    pallas_call x14, Pallas kernels, call(): pl.pallas_call(kernel, out_shape=out, grid_spec=pltpu.PrefetchScalarGridS...  36.6 us
    ppermute x6, starting transfers between devices, reduce_over_chips(): total[m ^ bit].append(lax.ppermute(value, 'rows', across(bit)))  8.71 us
    ppermute x3, waiting for transfers between devices, turn(): lax.ppermute(x, 'blk', [(b, (b + k) % planes) for b in range(planes)])  6.77 us
    ppermute x2, waiting for transfers between devices, mate(): return lax.ppermute(x, 'blk', [(b, b ^ 1) for b in range(planes)])  5.27 us
    ppermute x3, waiting for transfers between devices, work(): x = lax.ppermute(z, 'rows', across(1))  3.56 us
    ppermute x3, starting transfers between devices, turn(): lax.ppermute(x, 'blk', [(b, (b + k) % planes) for b in range(planes)])  3.17 us
    ppermute x3, starting transfers between devices, work(): tables[m] = chosen if m == 0 else lax.ppermute(chosen, 'rows', across(m))  3.11 us
    ppermute x3, starting transfers between devices, work(): x = lax.ppermute(z, 'rows', across(1))  2.56 us
  transfers between devices with their start and end apart: 24, of which 6 were waited for; matrix products, arithmetic and copies ran while one was open for 0% of the time, Pallas kernels for 43%

commit v1 on v0

--- a/solution.py
+++ b/solution.py
@@ -11,13 +11,12 @@
 F32 = jnp.float32
 BF16 = jnp.bfloat16
 I32 = jnp.int32
-UNROLL = 8
+UNROLL = 16
 MIB = 1 << 20
 
 
 VMEM = pl.BlockSpec(memory_space=pltpu.VMEM)
 HBM = pl.BlockSpec(memory_space=pltpu.HBM)
-SMEM = pl.BlockSpec(memory_space=pltpu.SMEM)
 
 
 def in_hbm(x):
@@ -98,13 +97,14 @@
         out_ref[i] = jnp.where(keep_first, first, second)
 
 
-def list_kernel(chips, held, cols, owner, slot, counts, out_ref, words, sems):
+def list_kernel(chips, held, cols, owner, slot, number, out_ref, words, counts, sems):
     blocks, listed = cols.shape
     span = out_ref.shape[2]
     copies = [
         pltpu.make_async_copy(ref, words.at[i], sems.at[i])
         for i, ref in enumerate((cols, owner, slot))
     ]
+    copies += [pltpu.make_async_copy(number, counts, sems.at[3])]
     for copy in copies:
         copy.start()
     for copy in copies:
@@ -148,25 +148,25 @@
 
 def tile_kernel(core, own_ref, other_ref, out_ref, buf, sems):
     held, _, width = own_ref.shape
-    step = buf.shape[1]
-    steps = held // step
+    steps, step = buf.shape[:2]
+    half = steps // 2
     mine = core[0]
-    refs = (own_ref, other_ref)
-
-    def copy(s):
-        ref, at = refs[s // steps], s % steps * step
-        return pltpu.make_async_copy(ref.at[pl.ds(at, step)], buf.at[s % 2], sems.at[s % 2])
-
-    copy(0).start()
-    for s in range(2 * steps):
-        if s + 1 < 2 * steps:
-            copy(s + 1).start()
-        copy(s).wait()
-        whose = mine if s < steps else 1 - mine
-        start = whose * held + s % steps * step
+    copies = [
+        pltpu.make_async_copy(
+            (own_ref if s < half else other_ref).at[pl.ds(s % half * step, step)],
+            buf.at[s],
+            sems.at[s],
+        )
+        for s in range(steps)
+    ]
+    for copy in copies:
+        copy.start()
+    for s in range(steps):
+        copies[s].wait()
+        start = (mine if s < half else 1 - mine) * held + s % half * step
 
         def one(i, _):
-            hi, lo = split(buf[s % 2, i])
+            hi, lo = split(buf[s, i])
             out_ref[start + i, :, :width] = hi
             out_ref[start + i, :, width:] = lo
             return 0
@@ -203,21 +203,30 @@
     blocks, half, width = out_ref.shape
     acc[...] = jnp.zeros_like(acc)
 
-    def step(s, _):
-        base = s * UNROLL
+    def multiply(base, n):
         terms = [
             jnp.dot(
                 tiles_ref[lists[g, 1, base + u]],
                 proj_ref[lists[g, 2, base + u]],
                 preferred_element_type=F32,
             )
-            for u in range(UNROLL)
+            for u in range(n)
         ]
-        for u in range(UNROLL):
+        for u in range(n):
             acc[lists[g, 3, base + u]] += terms[u]
+
+    def step(s, _):
+        multiply(s * UNROLL, UNROLL)
         return 0
 
-    lax.fori_loop(0, (lists[g, 0, 0] + UNROLL - 1) // UNROLL, step, 0)
+    number = lists[g, 0, 0]
+    steps = (number + UNROLL // 2 - 1) // UNROLL
+    lax.fori_loop(0, steps, step, 0)
+
+    @pl.when(number > steps * UNROLL)
+    def _():
+        multiply(steps * UNROLL, UNROLL // 2)
+
     low = lanes((half, width)) < half
     for i in range(blocks):
         top, bottom = acc[i, :half], acc[i, half:]
@@ -308,10 +317,14 @@
 
     span = pl.cdiv(cap, 128) * 128
     lists = call(
-        functools.partial(list_kernel, chips, held), 0, [HBM] * 3 + [SMEM],
+        functools.partial(list_kernel, chips, held), 0, [HBM] * 4,
         jax.ShapeDtypeStruct((chips, 4, span), I32),
-        [pltpu.VMEM((3, blocks, listed), I32), pltpu.SemaphoreType.DMA((3,))],
-        (in_hbm(pair_cols), in_hbm(pair_owner), in_hbm(pair_slot), pair_counts),
+        [
+            pltpu.VMEM((3, blocks, listed), I32),
+            pltpu.SMEM((blocks,), I32),
+            pltpu.SemaphoreType.DMA((4,)),
+        ],
+        (in_hbm(pair_cols), in_hbm(pair_owner), in_hbm(pair_slot), in_hbm(pair_counts)),
         cost(10**8, 16384), 8 * MIB,
     )
     gathered = jnp.stack([lists, mate(lists)], axis=1)
@@ -329,9 +342,9 @@
     packed = call(
         tile_kernel, 1, [HBM, HBM],
         jax.ShapeDtypeStruct((2 * held, coarse, 2 * coarse), BF16),
-        [pltpu.VMEM((2, 16, coarse, coarse), F32), pltpu.SemaphoreType.DMA((2,))],
+        [pltpu.VMEM((held // 4, 8, coarse, coarse), F32), pltpu.SemaphoreType.DMA((held // 4,))],
         (core.reshape(1).astype(I32), in_hbm(tiles), in_hbm(other_tiles)),
-        cost(held * 65536 * 4, held * 65536 * 4), 12 * MIB,
+        cost(held * 65536 * 4, held * 65536 * 4), 2 * held * 65536 + 4 * MIB,
     )
 
     pieces = []
@@ -363,7 +376,8 @@
                 total[m ^ bit].append(lax.ppermute(value, "rows", across(bit)))
         return total[0]
 
-    other = mate(functools.reduce(jnp.add, reduce_over_chips(1)))
+    other = functools.reduce(jnp.add, reduce_over_chips(1))
+    other = mate(other)
     sums = reduce_over_chips(0)
     while len(sums) > 3:
         sums = [sums[0] + sums[1]] + sums[2:]

time: 75.2 us -> 68.2 us (0.907)
  Pallas kernels: 36.6 us -> 30.1 us
    pallas_call x14, Pallas kernels: 36.6 us -> 30.1 us  [call(): pl.pallas_call(kernel, out_shape=out, grid_spec=pltpu.PrefetchScalarGridS...]
  transfers between devices with their start and end apart: 24 -> 24, of which waited for: 6 -> 7; matrix products, arithmetic and copies ran while one was open for 0% -> 0% of each run, Pallas kernels for 43% -> 38%
where the time goes in v1:
time: 68.2 us; the launch traced here: 68 us
  Pallas kernels  30.1 us (44%)
  starting transfers between devices  19.1 us (28%)
  waiting for transfers between devices  18.3 us (27%)
    pallas_call x14, Pallas kernels, call(): pl.pallas_call(kernel, out_shape=out, grid_spec=pltpu.PrefetchScalarGridS...  30.1 us
    ppermute x6, starting transfers between devices, reduce_over_chips(): total[m ^ bit].append(lax.ppermute(value, 'rows', across(bit)))  8.41 us
    ppermute x3, waiting for transfers between devices, turn(): lax.ppermute(x, 'blk', [(b, (b + k) % planes) for b in range(planes)])  6.77 us
    ppermute x2, waiting for transfers between devices, mate(): return lax.ppermute(x, 'blk', [(b, b ^ 1) for b in range(planes)])  5.34 us
    ppermute x3, waiting for transfers between devices, work(): x = lax.ppermute(z, 'rows', across(1))  3.56 us
    ppermute x3, starting transfers between devices, turn(): lax.ppermute(x, 'blk', [(b, (b + k) % planes) for b in range(planes)])  3.17 us
    ppermute x3, starting transfers between devices, work(): tables[m] = chosen if m == 0 else lax.ppermute(chosen, 'rows', across(m))  3.11 us
    ppermute x3, starting transfers between devices, work(): x = lax.ppermute(z, 'rows', across(1))  2.56 us
  transfers between devices with their start and end apart: 24, of which 7 were waited for; matrix products, arithmetic and copies ran while one was open for 0% of the time, Pallas kernels for 38%

profile of v1, /device:TPU:16, one launch (start us, length us, event | category | flops | bytes accessed | tf_op | source)
XLA Modules:
  0.0 68.0 jit_solution(14794175156177376365)
XLA Ops:
  0.0 0.1 stack.37.place
  0.1 1.9 %shard_map.85 = f32[2,3,64,128]{3,2,1,0:T(8,128)S(1)} custom-call(s32[7]{0:T(128)S(1)} %stack.37.place, f32[12,128,128]{2,1,0:T(8,128)} %bitcast.24, f32[12,128,128]{2,1,0:T(8,128)} %r_ref.3), custom_call_target="tpu_custom_call" | custom-call | flops 37748736 | bytes 393216 | tf_op jit(solution)/shard_map/pallas_call | solution.py:250
  2.0 1.6 %collective-permute-start.2 = (f32[3,64,128]{2,1,0:T(8,128)S(1)}, f32[3,64,128]{2,1,0:T(8,128)S(1)}, u32[]{:S(2)}, u32[]{:S(2)}) collective-permute-start(f32[3,64,128]{2,1,0:T(8,128)S(1)} %get-tuple-element.6), channel_id=1, source_target_pairs={{0,1},{1,2},{2,3},{3,0},{4,5},{5,6},{6,7},{7,4},{8,9},{9,10},{10,1... | collective-permute-start | bytes 294920 | tf_op jit(solution)/shard_map/ppermute | solution.py:294
  3.7 0.3 collective-permute-start.6
  4.0 1.2 %collective-permute-start.10 = (f32[3,64,128]{2,1,0:T(8,128)S(1)}, f32[3,64,128]{2,1,0:T(8,128)S(1)}, u32[]{:S(2)}, u32[]{:S(2)}) collective-permute-start(f32[3,64,128]{2,1,0:T(8,128)S(1)} %get-tuple-element.6), channel_id=1, source_target_pairs={{0,3},{1,0},{2,1},{3,2},{4,7},{5,4},{6,5},{7,6},{8,11},{9,8},{10,9... | collective-permute-start | bytes 294920 | tf_op jit(solution)/shard_map/ppermute | solution.py:294
  5.2 6.8 %collective-permute-done.2.refs_0_ = f32[3,64,128]{2,1,0:T(8,128)S(1)} collective-permute-done((f32[3,64,128]{2,1,0:T(8,128)S(1)}, f32[3,64,128]{2,1,0:T(8,128)S(1)}, u32[]{:S(2)}, u32[]{:S(2)}) %collective-permute-start.2) | collective-permute-done | bytes 98336 | tf_op jit(solution)/shard_map/ppermute | solution.py:294
  12.0 1.5 %collective-permute-start.3 = (f32[3,64,128]{2,1,0:T(8,128)S(1)}, f32[3,64,128]{2,1,0:T(8,128)S(1)}, u32[]{:S(2)}, u32[]{:S(2)}) collective-permute-start(f32[3,64,128]{2,1,0:T(8,128)S(1)} %collective-permute-done.2.refs_0_), channel_id=1, source_target_pairs={{0,8},{4,20},{8,0},{12,28},{16,24},{20,4},{24,16},{28,12},{1,9},{5... | collective-permute-start | bytes 294920 | tf_op jit(solution)/shard_map/ppermute | solution.py:353
  13.5 2.2 %shard_map.82 = s32[4,4,128]{2,1,0:T(4,128)S(1)} custom-call(s32[8,32]{1,0:T(8,128)} %cols.1, s32[8,32]{1,0:T(8,128)} %owner.1, s32[8,32]{1,0:T(8,128)} %slot.1, s32[8]{0:T(128)} %number.1), custom_call_target="tpu_custom_call" | custom-call | flops 100000000 | bytes 16384 | tf_op jit(solution)/shard_map/pallas_call | solution.py:250
  15.7 0.1 collective-permute-start
  15.7 3.6 %collective-permute-done = s32[4,4,128]{2,1,0:T(4,128)S(1)} collective-permute-done((s32[4,4,128]{2,1,0:T(4,128)S(1)}, s32[4,4,128]{2,1,0:T(4,128)S(1)}, u32[]{:S(2)}, u32[]{:S(2)}) %collective-permute-start) | collective-permute-done | bytes 8224 | tf_op jit(solution)/shard_map/ppermute | solution.py:297
  19.4 0.0 collective-permute-start.4
  19.4 0.0 collective-permute-done.6.refs_4_
  19.4 0.5 collective-permute-start.7
  19.9 0.0 collective-permute-done.10.refs_8_
  19.9 1.2 %collective-permute-start.8 = (f32[3,64,128]{2,1,0:T(8,128)S(1)}, f32[3,64,128]{2,1,0:T(8,128)S(1)}, u32[]{:S(2)}, u32[]{:S(2)}) collective-permute-start(f32[3,64,128]{2,1,0:T(8,128)S(1)} %collective-permute-done.6.refs_4_), channel_id=1, source_target_pairs={{0,4},{4,0},{8,12},{12,8},{16,20},{20,16},{24,28},{28,24},{1,5},{5... | collective-permute-start | bytes 294920 | tf_op jit(solution)/shard_map/ppermute | solution.py:291
  21.1 0.5 collective-permute-start.11
  21.7 0.0 collective-permute-done.4.refs_2_
  21.7 0.0 collective-permute-start.12
  21.7 2.3 %collective-permute-done.7.refs_5_ = f32[3,64,128]{2,1,0:T(8,128)S(1)} collective-permute-done((f32[3,64,128]{2,1,0:T(8,128)S(1)}, f32[3,64,128]{2,1,0:T(8,128)S(1)}, u32[]{:S(2)}, u32[]{:S(2)}) %collective-permute-start.7) | collective-permute-done | bytes 98336 | tf_op jit(solution)/shard_map/ppermute | solution.py:353
  24.0 0.0 collective-permute-done.8.refs_6_
  24.0 0.5 collective-permute-start.9
  24.5 1.2 %collective-permute-done.11.refs_9_ = f32[3,64,128]{2,1,0:T(8,128)S(1)} collective-permute-done((f32[3,64,128]{2,1,0:T(8,128)S(1)}, f32[3,64,128]{2,1,0:T(8,128)S(1)}, u32[]{:S(2)}, u32[]{:S(2)}) %collective-permute-start.11) | collective-permute-done | bytes 98336 | tf_op jit(solution)/shard_map/ppermute | solution.py:353
  25.8 1.4 %collective-permute-start.17 = (s32[2,4,128]{2,1,0:T(4,128)S(1)}, s32[2,4,128]{2,1,0:T(4,128)S(1)}, u32[]{:S(2)}, u32[]{:S(2)}) collective-permute-start(s32[2,4,128]{2,1,0:T(4,128)S(1)} %get-tuple-element.7), channel_id=1, source_target_pairs={{0,24},{4,28},{8,16},{12,20},{16,8},{20,12},{24,0},{28,4},{1,25},{... | collective-permute-start | bytes 12296 | tf_op jit(solution)/shard_map/ppermute | solution.py:335
  27.1 2.5 %shard_map.84.own_ref = f32[12,64,128]{2,1,0:T(8,128)S(1)} custom-call(s32[7]{0:T(128)S(1)} %stack.37.place, f32[12,128,128]{2,1,0:T(8,128)} %bitcast.25, f32[12,128,128]{2,1,0:T(8,128)} %r_ref.3), custom_call_target="tpu_custom_call" | custom-call | flops 150994944 | bytes 1572864 | tf_op jit(solution)/shard_map/pallas_call | solution.py:250
  29.7 1.1 %shard_map.86.proj_ref = bf16[48,256,128]{2,1,0:T(8,128)(2,1)S(1)} custom-call(s32[7]{0:T(128)S(1)} %stack.37.place, f32[12,64,128]{2,1,0:T(8,128)S(1)} %shard_map.84.own_ref, f32[3,64,128]{2,1,0:T(8,128)S(1)} %collective-permute-done.2.refs_0_, f32[3,64,128]{2,1,0:T(8,128)S(1)} %collective-permute-done.3.refs_1_, ...), custom_call_target="tpu_custom_call" | custom-call | flops 1000000 | bytes 4718592 | tf_op jit(solution)/shard_map/pallas_call | solution.py:250
  30.8 3.6 %shard_map.83.tiles_ref = bf16[128,128,256]{2,1,0:T(8,128)(2,1)S(1)} custom-call(s32[1]{0:T(128)} %bitcast.9.core, f32[64,128,128]{2,1,0:T(8,128)} %own_ref.1, f32[64,128,128]{2,1,0:T(8,128)} %collective-permute-done.1.other_ref), custom_call_target="tpu_custom_call" | custom-call | flops 16777216 | bytes 16777216 | tf_op jit(solution)/shard_map/pallas_call | solution.py:250
  34.5 2.4 %shard_map.94 = f32[8,64,128]{2,1,0:T(8,128)S(1)} custom-call(s32[2,4,128]{2,1,0:T(4,128)S(1)} %collective-permute-done.17.lists, bf16[128,128,256]{2,1,0:T(8,128)(2,1)S(1)} %shard_map.83.tiles_ref, bf16[48,256,128]{2,1,0:T(8,128)(2,1)S(1)} %shard_map.86.proj_ref), custom_call_target="tpu_custom_call" | custom-call | flops 536870912 | bytes 4194304 | tf_op jit(solution)/shard_map/pallas_call | solution.py:250
  36.9 1.0 %collective-permute-start.21 = (f32[8,64,128]{2,1,0:T(8,128)S(1)}, f32[8,64,128]{2,1,0:T(8,128)S(1)}, u32[]{:S(2)}, u32[]{:S(2)}) collective-permute-start(f32[8,64,128]{2,1,0:T(8,128)S(1)} %shard_map.94), channel_id=1, source_target_pairs={{0,8},{4,20},{8,0},{12,28},{16,24},{20,4},{24,16},{28,12},{1,9},{5... | collective-permute-start | bytes 786440 | tf_op jit(solution)/shard_map/ppermute | solution.py:376
  37.9 1.0 %collective-permute-start.14 = (s32[2,4,128]{2,1,0:T(4,128)S(1)}, s32[2,4,128]{2,1,0:T(4,128)S(1)}, u32[]{:S(2)}, u32[]{:S(2)}) collective-permute-start(s32[2,4,128]{2,1,0:T(4,128)S(1)} %get-tuple-element.9), channel_id=1, source_target_pairs={{0,8},{4,20},{8,0},{12,28},{16,24},{20,4},{24,16},{28,12},{1,9},{5... | collective-permute-start | bytes 12296 | tf_op jit(solution)/shard_map/ppermute | solution.py:335
  39.0 0.7 %collective-permute-start.16 = (s32[2,4,128]{2,1,0:T(4,128)S(1)}, s32[2,4,128]{2,1,0:T(4,128)S(1)}, u32[]{:S(2)}, u32[]{:S(2)}) collective-permute-start(s32[2,4,128]{2,1,0:T(4,128)S(1)} %get-tuple-element.10), channel_id=1, source_target_pairs={{0,16},{4,12},{8,24},{12,4},{16,0},{20,28},{24,8},{28,20},{1,17},{... | collective-permute-start | bytes 12296 | tf_op jit(solution)/shard_map/ppermute | solution.py:335
  39.7 2.1 %shard_map.90 = f32[8,64,128]{2,1,0:T(8,128)S(1)} custom-call(s32[2,4,128]{2,1,0:T(4,128)S(1)} %collective-permute-done.17.lists, bf16[128,128,256]{2,1,0:T(8,128)(2,1)S(1)} %shard_map.83.tiles_ref, bf16[48,256,128]{2,1,0:T(8,128)(2,1)S(1)} %shard_map.86.proj_ref), custom_call_target="tpu_custom_call" | custom-call | flops 536870912 | bytes 4194304 | tf_op jit(solution)/shard_map/pallas_call | solution.py:250
  41.8 1.6 %collective-permute-start.18 = (f32[8,64,128]{2,1,0:T(8,128)S(1)}, f32[8,64,128]{2,1,0:T(8,128)S(1)}, u32[]{:S(2)}, u32[]{:S(2)}) collective-permute-start(f32[8,64,128]{2,1,0:T(8,128)S(1)} %shard_map.90), channel_id=1, source_target_pairs={{0,8},{4,20},{8,0},{12,28},{16,24},{20,4},{24,16},{28,12},{1,9},{5... | collective-permute-start | bytes 786440 | tf_op jit(solution)/shard_map/ppermute | solution.py:376
  43.4 0.1 collective-permute-done.14.lists
  43.4 2.1 %shard_map.92 = f32[8,64,128]{2,1,0:T(8,128)S(1)} custom-call(s32[2,4,128]{2,1,0:T(4,128)S(1)} %collective-permute-done.14.lists, bf16[128,128,256]{2,1,0:T(8,128)(2,1)S(1)} %shard_map.83.tiles_ref, bf16[48,256,128]{2,1,0:T(8,128)(2,1)S(1)} %shard_map.86.proj_ref), custom_call_target="tpu_custom_call" | custom-call | flops 536870912 | bytes 4194304 | tf_op jit(solution)/shard_map/pallas_call | solution.py:250
  45.5 1.3 %collective-permute-start.20 = (f32[8,64,128]{2,1,0:T(8,128)S(1)}, f32[8,64,128]{2,1,0:T(8,128)S(1)}, u32[]{:S(2)}, u32[]{:S(2)}) collective-permute-start(f32[8,64,128]{2,1,0:T(8,128)S(1)} %shard_map.92), channel_id=1, source_target_pairs={{0,8},{4,20},{8,0},{12,28},{16,24},{20,4},{24,16},{28,12},{1,9},{5... | collective-permute-start | bytes 786440 | tf_op jit(solution)/shard_map/ppermute | solution.py:376
  46.8 2.4 %shard_map.93 = f32[8,64,128]{2,1,0:T(8,128)S(1)} custom-call(s32[2,4,128]{2,1,0:T(4,128)S(1)} %collective-permute-done.16.lists, bf16[128,128,256]{2,1,0:T(8,128)(2,1)S(1)} %shard_map.83.tiles_ref, bf16[48,256,128]{2,1,0:T(8,128)(2,1)S(1)} %shard_map.86.proj_ref), custom_call_target="tpu_custom_call" | custom-call | flops 536870912 | bytes 4194304 | tf_op jit(solution)/shard_map/pallas_call | solution.py:250
  49.3 0.7 %collective-permute-start.22 = (f32[8,64,128]{2,1,0:T(8,128)S(1)}, f32[8,64,128]{2,1,0:T(8,128)S(1)}, u32[]{:S(2)}, u32[]{:S(2)}) collective-permute-start(f32[8,64,128]{2,1,0:T(8,128)S(1)} %add.36), channel_id=1, source_target_pairs={{0,16},{4,12},{8,24},{12,4},{16,0},{20,28},{24,8},{28,20},{1,17},{... | collective-permute-start | bytes 786440 | tf_op jit(solution)/shard_map/ppermute | solution.py:376
  50.0 1.5 %shard_map.88 = f32[8,64,128]{2,1,0:T(8,128)S(1)} custom-call(s32[2,4,128]{2,1,0:T(4,128)S(1)} %collective-permute-done.14.lists, bf16[128,128,256]{2,1,0:T(8,128)(2,1)S(1)} %shard_map.83.tiles_ref, bf16[48,256,128]{2,1,0:T(8,128)(2,1)S(1)} %shard_map.86.proj_ref), custom_call_target="tpu_custom_call" | custom-call | flops 536870912 | bytes 4194304 | tf_op jit(solution)/shard_map/pallas_call | solution.py:250
  51.6 2.2 %collective-permute-start.15 = (f32[8,64,128]{2,1,0:T(8,128)S(1)}, f32[8,64,128]{2,1,0:T(8,128)S(1)}, u32[]{:S(2)}, u32[]{:S(2)}) collective-permute-start(f32[8,64,128]{2,1,0:T(8,128)S(1)} %shard_map.88), channel_id=1, source_target_pairs={{0,8},{4,20},{8,0},{12,28},{16,24},{20,4},{24,16},{28,12},{1,9},{5... | collective-permute-start | bytes 786440 | tf_op jit(solution)/shard_map/ppermute | solution.py:376
  53.7 2.1 %shard_map.91 = f32[8,64,128]{2,1,0:T(8,128)S(1)} custom-call(s32[2,4,128]{2,1,0:T(4,128)S(1)} %get-tuple-element.8.lists, bf16[128,128,256]{2,1,0:T(8,128)(2,1)S(1)} %shard_map.83.tiles_ref, bf16[48,256,128]{2,1,0:T(8,128)(2,1)S(1)} %shard_map.86.proj_ref), custom_call_target="tpu_custom_call" | custom-call | flops 536870912 | bytes 4194304 | tf_op jit(solution)/shard_map/pallas_call | solution.py:250
  55.8 2.1 %shard_map.89 = f32[8,64,128]{2,1,0:T(8,128)S(1)} custom-call(s32[2,4,128]{2,1,0:T(4,128)S(1)} %collective-permute-done.16.lists, bf16[128,128,256]{2,1,0:T(8,128)(2,1)S(1)} %shard_map.83.tiles_ref, bf16[48,256,128]{2,1,0:T(8,128)(2,1)S(1)} %shard_map.86.proj_ref), custom_call_target="tpu_custom_call" | custom-call | flops 536870912 | bytes 4194304 | tf_op jit(solution)/shard_map/pallas_call | solution.py:250
  58.0 1.6 %collective-permute-start.19 = (f32[8,64,128]{2,1,0:T(8,128)S(1)}, f32[8,64,128]{2,1,0:T(8,128)S(1)}, u32[]{:S(2)}, u32[]{:S(2)}) collective-permute-start(f32[8,64,128]{2,1,0:T(8,128)S(1)} %add.34), channel_id=1, source_target_pairs={{0,16},{4,12},{8,24},{12,4},{16,0},{20,28},{24,8},{28,20},{1,17},{... | collective-permute-start | bytes 786440 | tf_op jit(solution)/shard_map/ppermute | solution.py:376
  59.7 0.0 copy-start
  59.7 0.1 collective-permute-start.23
  59.8 2.1 %shard_map.87.own_a = f32[8,64,128]{2,1,0:T(8,128)S(1)} custom-call(s32[2,4,128]{2,1,0:T(4,128)S(1)} %get-tuple-element.8.lists, bf16[128,128,256]{2,1,0:T(8,128)(2,1)S(1)} %shard_map.83.tiles_ref, bf16[48,256,128]{2,1,0:T(8,128)(2,1)S(1)} %shard_map.86.proj_ref), custom_call_target="tpu_custom_call" | custom-call | flops 536870912 | bytes 4194304 | tf_op jit(solution)/shard_map/pallas_call | solution.py:250
  61.9 2.5 %collective-permute-done.19.own_c = f32[8,64,128]{2,1,0:T(8,128)S(1)} collective-permute-done((f32[8,64,128]{2,1,0:T(8,128)S(1)}, f32[8,64,128]{2,1,0:T(8,128)S(1)}, u32[]{:S(2)}, u32[]{:S(2)}) %collective-permute-start.19) | collective-permute-done | bytes 262176 | tf_op jit(solution)/shard_map/ppermute | solution.py:376
  64.5 1.7 %collective-permute-done.23.other = f32[8,64,128]{2,1,0:T(8,128)S(1)} collective-permute-done((f32[8,64,128]{2,1,0:T(8,128)S(1)}, f32[8,64,128]{2,1,0:T(8,128)S(1)}, u32[]{:S(2)}, u32[]{:S(2)}) %collective-permute-start.23) | collective-permute-done | bytes 262176 | tf_op jit(solution)/shard_map/ppermute | solution.py:297
  66.2 1.8 %shard_map.95 = f32[8,128,128]{2,1,0:T(8,128)} custom-call(s32[7]{0:T(128)S(1)} %stack.37.place, f32[8,128,128]{2,1,0:T(8,128)S(1)} %copy-done, f32[8,64,128]{2,1,0:T(8,128)S(1)} %shard_map.87.own_a, f32[8,64,128]{2,1,0:T(8,128)S(1)} %collective-permute-done.15.own_b, f32[8,64,128]{2,1,0:T(8,128)S(1)} %collective-permute-done.19.own_c, ...), custom_call_target="tpu_custom_call" | custom-call | flops 100663296 | bytes 2097152 | tf_op jit(solution)/shard_map/pallas_call | solution.py:250
  (22 shorter events, 0.2 us)
Async XLA Ops:
  0.0 30.8 %collective-permute-start.1 = (f32[64,128,128]{2,1,0:T(8,128)}, f32[64,128,128]{2,1,0:T(8,128)}, u32[]{:S(2)}, u32[]{:S(2)}) collective-permute-start(f32[64,128,128]{2,1,0:T(8,128)} %own_ref.1), channel_id=1, source_target_pairs={{0,4},{4,0},{8,12},{12,8},{16,20},{20,16},{24,28},{28,24},{1,5},{5... | collective-permute-start | bytes 12582920 | tf_op jit(solution)/shard_map/ppermute | solution.py:291
  2.0 9.9 %collective-permute-start.2 = (f32[3,64,128]{2,1,0:T(8,128)S(1)}, f32[3,64,128]{2,1,0:T(8,128)S(1)}, u32[]{:S(2)}, u32[]{:S(2)}) collective-permute-start(f32[3,64,128]{2,1,0:T(8,128)S(1)} %get-tuple-element.6), channel_id=1, source_target_pairs={{0,1},{1,2},{2,3},{3,0},{4,5},{5,6},{6,7},{7,4},{8,9},{9,10},{10,1... | collective-permute-start | bytes 294920 | tf_op jit(solution)/shard_map/ppermute | solution.py:294
  3.7 15.7 %collective-permute-start.6 = (f32[3,64,128]{2,1,0:T(8,128)S(1)}, f32[3,64,128]{2,1,0:T(8,128)S(1)}, u32[]{:S(2)}, u32[]{:S(2)}) collective-permute-start(f32[3,64,128]{2,1,0:T(8,128)S(1)} %get-tuple-element.5), channel_id=1, source_target_pairs={{0,2},{1,3},{2,0},{3,1},{4,6},{5,7},{6,4},{7,5},{8,10},{9,11},{10,... | collective-permute-start | bytes 294920 | tf_op jit(solution)/shard_map/ppermute | solution.py:294
  4.0 15.9 %collective-permute-start.10 = (f32[3,64,128]{2,1,0:T(8,128)S(1)}, f32[3,64,128]{2,1,0:T(8,128)S(1)}, u32[]{:S(2)}, u32[]{:S(2)}) collective-permute-start(f32[3,64,128]{2,1,0:T(8,128)S(1)} %get-tuple-element.6), channel_id=1, source_target_pairs={{0,3},{1,0},{2,1},{3,2},{4,7},{5,4},{6,5},{7,6},{8,11},{9,8},{10,9... | collective-permute-start | bytes 294920 | tf_op jit(solution)/shard_map/ppermute | solution.py:294
  12.0 9.1 %collective-permute-start.3 = (f32[3,64,128]{2,1,0:T(8,128)S(1)}, f32[3,64,128]{2,1,0:T(8,128)S(1)}, u32[]{:S(2)}, u32[]{:S(2)}) collective-permute-start(f32[3,64,128]{2,1,0:T(8,128)S(1)} %collective-permute-done.2.refs_0_), channel_id=1, source_target_pairs={{0,8},{4,20},{8,0},{12,28},{16,24},{20,4},{24,16},{28,12},{1,9},{5... | collective-permute-start | bytes 294920 | tf_op jit(solution)/shard_map/ppermute | solution.py:353
  15.7 3.7 %collective-permute-start = (s32[4,4,128]{2,1,0:T(4,128)S(1)}, s32[4,4,128]{2,1,0:T(4,128)S(1)}, u32[]{:S(2)}, u32[]{:S(2)}) collective-permute-start(s32[4,4,128]{2,1,0:T(4,128)S(1)} %shard_map.82), channel_id=1, source_target_pairs={{0,1},{1,0},{2,3},{3,2},{4,5},{5,4},{6,7},{7,6},{8,9},{9,8},{10,11... | collective-permute-start | bytes 24584 | tf_op jit(solution)/shard_map/ppermute | solution.py:297
  19.4 2.3 %collective-permute-start.4 = (f32[3,64,128]{2,1,0:T(8,128)S(1)}, f32[3,64,128]{2,1,0:T(8,128)S(1)}, u32[]{:S(2)}, u32[]{:S(2)}) collective-permute-start(f32[3,64,128]{2,1,0:T(8,128)S(1)} %collective-permute-done.2.refs_0_), channel_id=1, source_target_pairs={{0,4},{4,0},{8,12},{12,8},{16,20},{20,16},{24,28},{28,24},{1,5},{5... | collective-permute-start | bytes 294920 | tf_op jit(solution)/shard_map/ppermute | solution.py:291
  19.4 4.6 %collective-permute-start.7 = (f32[3,64,128]{2,1,0:T(8,128)S(1)}, f32[3,64,128]{2,1,0:T(8,128)S(1)}, u32[]{:S(2)}, u32[]{:S(2)}) collective-permute-start(f32[3,64,128]{2,1,0:T(8,128)S(1)} %collective-permute-done.6.refs_4_), channel_id=1, source_target_pairs={{0,8},{4,20},{8,0},{12,28},{16,24},{20,4},{24,16},{28,12},{1,9},{5... | collective-permute-start | bytes 294920 | tf_op jit(solution)/shard_map/ppermute | solution.py:353
  19.9 4.1 %collective-permute-start.8 = (f32[3,64,128]{2,1,0:T(8,128)S(1)}, f32[3,64,128]{2,1,0:T(8,128)S(1)}, u32[]{:S(2)}, u32[]{:S(2)}) collective-permute-start(f32[3,64,128]{2,1,0:T(8,128)S(1)} %collective-permute-done.6.refs_4_), channel_id=1, source_target_pairs={{0,4},{4,0},{8,12},{12,8},{16,20},{20,16},{24,28},{28,24},{1,5},{5... | collective-permute-start | bytes 294920 | tf_op jit(solution)/shard_map/ppermute | solution.py:291
  21.1 4.6 %collective-permute-start.11 = (f32[3,64,128]{2,1,0:T(8,128)S(1)}, f32[3,64,128]{2,1,0:T(8,128)S(1)}, u32[]{:S(2)}, u32[]{:S(2)}) collective-permute-start(f32[3,64,128]{2,1,0:T(8,128)S(1)} %collective-permute-done.10.refs_8_), channel_id=1, source_target_pairs={{0,8},{4,20},{8,0},{12,28},{16,24},{20,4},{24,16},{28,12},{1,9},{5... | collective-permute-start | bytes 294920 | tf_op jit(solution)/shard_map/ppermute | solution.py:353
  21.7 4.1 %collective-permute-start.12 = (f32[3,64,128]{2,1,0:T(8,128)S(1)}, f32[3,64,128]{2,1,0:T(8,128)S(1)}, u32[]{:S(2)}, u32[]{:S(2)}) collective-permute-start(f32[3,64,128]{2,1,0:T(8,128)S(1)} %collective-permute-done.10.refs_8_), channel_id=1, source_target_pairs={{0,4},{4,0},{8,12},{12,8},{16,20},{20,16},{24,28},{28,24},{1,5},{5... | collective-permute-start | bytes 294920 | tf_op jit(solution)/shard_map/ppermute | solution.py:291
  24.0 5.7 %collective-permute-start.5 = (f32[3,64,128]{2,1,0:T(8,128)S(1)}, f32[3,64,128]{2,1,0:T(8,128)S(1)}, u32[]{:S(2)}, u32[]{:S(2)}) collective-permute-start(f32[3,64,128]{2,1,0:T(8,128)S(1)} %collective-permute-done.3.refs_1_), channel_id=1, source_target_pairs={{0,4},{4,0},{8,12},{12,8},{16,20},{20,16},{24,28},{28,24},{1,5},{5... | collective-permute-start | bytes 294920 | tf_op jit(solution)/shard_map/ppermute | solution.py:291
  24.0 5.7 %collective-permute-start.9 = (f32[3,64,128]{2,1,0:T(8,128)S(1)}, f32[3,64,128]{2,1,0:T(8,128)S(1)}, u32[]{:S(2)}, u32[]{:S(2)}) collective-permute-start(f32[3,64,128]{2,1,0:T(8,128)S(1)} %collective-permute-done.7.refs_5_), channel_id=1, source_target_pairs={{0,4},{4,0},{8,12},{12,8},{16,20},{20,16},{24,28},{28,24},{1,5},{5... | collective-permute-start | bytes 294920 | tf_op jit(solution)/shard_map/ppermute | solution.py:291
  25.8 3.9 %collective-permute-start.13 = (f32[3,64,128]{2,1,0:T(8,128)S(1)}, f32[3,64,128]{2,1,0:T(8,128)S(1)}, u32[]{:S(2)}, u32[]{:S(2)}) collective-permute-start(f32[3,64,128]{2,1,0:T(8,128)S(1)} %collective-permute-done.11.refs_9_), channel_id=1, source_target_pairs={{0,4},{4,0},{8,12},{12,8},{16,20},{20,16},{24,28},{28,24},{1,5},{5... | collective-permute-start | bytes 294920 | tf_op jit(solution)/shard_map/ppermute | solution.py:291
  25.8 8.7 %collective-permute-start.17 = (s32[2,4,128]{2,1,0:T(4,128)S(1)}, s32[2,4,128]{2,1,0:T(4,128)S(1)}, u32[]{:S(2)}, u32[]{:S(2)}) collective-permute-start(s32[2,4,128]{2,1,0:T(4,128)S(1)} %get-tuple-element.7), channel_id=1, source_target_pairs={{0,24},{4,28},{8,16},{12,20},{16,8},{20,12},{24,0},{28,4},{1,25},{... | collective-permute-start | bytes 12296 | tf_op jit(solution)/shard_map/ppermute | solution.py:335
  36.9 12.4 %collective-permute-start.21 = (f32[8,64,128]{2,1,0:T(8,128)S(1)}, f32[8,64,128]{2,1,0:T(8,128)S(1)}, u32[]{:S(2)}, u32[]{:S(2)}) collective-permute-start(f32[8,64,128]{2,1,0:T(8,128)S(1)} %shard_map.94), channel_id=1, source_target_pairs={{0,8},{4,20},{8,0},{12,28},{16,24},{20,4},{24,16},{28,12},{1,9},{5... | collective-permute-start | bytes 786440 | tf_op jit(solution)/shard_map/ppermute | solution.py:376
  37.9 5.5 %collective-permute-start.14 = (s32[2,4,128]{2,1,0:T(4,128)S(1)}, s32[2,4,128]{2,1,0:T(4,128)S(1)}, u32[]{:S(2)}, u32[]{:S(2)}) collective-permute-start(s32[2,4,128]{2,1,0:T(4,128)S(1)} %get-tuple-element.9), channel_id=1, source_target_pairs={{0,8},{4,20},{8,0},{12,28},{16,24},{20,4},{24,16},{28,12},{1,9},{5... | collective-permute-start | bytes 12296 | tf_op jit(solution)/shard_map/ppermute | solution.py:335
  39.0 7.9 %collective-permute-start.16 = (s32[2,4,128]{2,1,0:T(4,128)S(1)}, s32[2,4,128]{2,1,0:T(4,128)S(1)}, u32[]{:S(2)}, u32[]{:S(2)}) collective-permute-start(s32[2,4,128]{2,1,0:T(4,128)S(1)} %get-tuple-element.10), channel_id=1, source_target_pairs={{0,16},{4,12},{8,24},{12,4},{16,0},{20,28},{24,8},{28,20},{1,17},{... | collective-permute-start | bytes 12296 | tf_op jit(solution)/shard_map/ppermute | solution.py:335
  41.8 16.2 %collective-permute-start.18 = (f32[8,64,128]{2,1,0:T(8,128)S(1)}, f32[8,64,128]{2,1,0:T(8,128)S(1)}, u32[]{:S(2)}, u32[]{:S(2)}) collective-permute-start(f32[8,64,128]{2,1,0:T(8,128)S(1)} %shard_map.90), channel_id=1, source_target_pairs={{0,8},{4,20},{8,0},{12,28},{16,24},{20,4},{24,16},{28,12},{1,9},{5... | collective-permute-start | bytes 786440 | tf_op jit(solution)/shard_map/ppermute | solution.py:376
  45.5 14.1 %collective-permute-start.20 = (f32[8,64,128]{2,1,0:T(8,128)S(1)}, f32[8,64,128]{2,1,0:T(8,128)S(1)}, u32[]{:S(2)}, u32[]{:S(2)}) collective-permute-start(f32[8,64,128]{2,1,0:T(8,128)S(1)} %shard_map.92), channel_id=1, source_target_pairs={{0,8},{4,20},{8,0},{12,28},{16,24},{20,4},{24,16},{28,12},{1,9},{5... | collective-permute-start | bytes 786440 | tf_op jit(solution)/shard_map/ppermute | solution.py:376
  49.3 10.3 %collective-permute-start.22 = (f32[8,64,128]{2,1,0:T(8,128)S(1)}, f32[8,64,128]{2,1,0:T(8,128)S(1)}, u32[]{:S(2)}, u32[]{:S(2)}) collective-permute-start(f32[8,64,128]{2,1,0:T(8,128)S(1)} %add.36), channel_id=1, source_target_pairs={{0,16},{4,12},{8,24},{12,4},{16,0},{20,28},{24,8},{28,20},{1,17},{... | collective-permute-start | bytes 786440 | tf_op jit(solution)/shard_map/ppermute | solution.py:376
  51.6 10.4 %collective-permute-start.15 = (f32[8,64,128]{2,1,0:T(8,128)S(1)}, f32[8,64,128]{2,1,0:T(8,128)S(1)}, u32[]{:S(2)}, u32[]{:S(2)}) collective-permute-start(f32[8,64,128]{2,1,0:T(8,128)S(1)} %shard_map.88), channel_id=1, source_target_pairs={{0,8},{4,20},{8,0},{12,28},{16,24},{20,4},{24,16},{28,12},{1,9},{5... | collective-permute-start | bytes 786440 | tf_op jit(solution)/shard_map/ppermute | solution.py:376
  58.0 6.4 %collective-permute-start.19 = (f32[8,64,128]{2,1,0:T(8,128)S(1)}, f32[8,64,128]{2,1,0:T(8,128)S(1)}, u32[]{:S(2)}, u32[]{:S(2)}) collective-permute-start(f32[8,64,128]{2,1,0:T(8,128)S(1)} %add.34), channel_id=1, source_target_pairs={{0,16},{4,12},{8,24},{12,4},{16,0},{20,28},{24,8},{28,20},{1,17},{... | collective-permute-start | bytes 786440 | tf_op jit(solution)/shard_map/ppermute | solution.py:376
  59.7 6.5 %copy-start = (f32[8,128,128]{2,1,0:T(8,128)S(1)}, f32[8,128,128]{2,1,0:T(8,128)}, u32[]{:S(2)}) copy-start(f32[8,128,128]{2,1,0:T(8,128)} %left_ref.1) | copy-start | bytes 1572868
  59.7 6.4 %collective-permute-start.23 = (f32[8,64,128]{2,1,0:T(8,128)S(1)}, f32[8,64,128]{2,1,0:T(8,128)S(1)}, u32[]{:S(2)}, u32[]{:S(2)}) collective-permute-start(f32[8,64,128]{2,1,0:T(8,128)S(1)} %add_add_fusion), channel_id=1, source_target_pairs={{0,1},{1,0},{2,3},{3,2},{4,5},{5,4},{6,7},{7,6},{8,9},{9,8},{10,11... | collective-permute-start | bytes 786440 | tf_op jit(solution)/shard_map/ppermute | solution.py:297

commit v2 on v1

v2 whole, which is shorter than its diff:
```python
import functools

import jax
import jax.numpy as jnp
from jax import lax
from jax.experimental import pallas as pl
from jax.experimental.pallas import tpu as pltpu
from jax.sharding import PartitionSpec as P


F32 = jnp.float32
BF16 = jnp.bfloat16
I32 = jnp.int32
UNROLL = 16
MIB = 1 << 20


VMEM = pl.BlockSpec(memory_space=pltpu.VMEM)
HBM = pl.BlockSpec(memory_space=pltpu.HBM)


def in_hbm(x):
    return pltpu.with_memory_space_constraint(x, pltpu.HBM)


def cost(flops, nbytes):
    return pl.CostEstimate(flops=flops, bytes_accessed=nbytes, transcendentals=0)


def split(x):
    hi = x.astype(BF16)
    return hi, (x - hi.astype(F32)).astype(BF16)


def lanes(shape):
    return lax.broadcasted_iota(I32, shape, len(shape) - 1)


def triple(a, b, dims):
    a_hi, a_lo = split(a)
    b_hi, b_lo = split(b)

    def dot(x, y):
        return lax.dot_general(x, y, (dims, ((), ())), preferred_element_type=F32)

    return dot(a_hi, b_hi) + dot(a_hi, b_lo) + dot(a_lo, b_hi)


def project_kernel(place, v_ref, r_ref, out_ref, v_buf, r_buf, sems):
    count = v_buf.shape[0]
    first = place[0] * count if count < v_ref.shape[0] else 0
    copies = [
        pltpu.make_async_copy(ref.at[pl.ds(first, count)], buf, sems.at[i])
        for i, (ref, buf) in enumerate(((v_ref, v_buf), (r_ref, r_buf)))
    ]
    for copy in copies:
        copy.start()
    for copy in copies:
        copy.wait()
    for i in range(count):
        out_ref[i] = triple(r_buf[i], v_buf[i], ((0,), (0,)))


def list_kernel(chips, held, columns, cols, owner, slot, number, out_ref, words, counts, sems):
    blocks, listed = cols.shape
    span = out_ref.shape[2]
    copies = [
        pltpu.make_async_copy(ref, words.at[i], sems.at[i])
        for i, ref in enumerate((cols, owner, slot))
    ]
    copies += [pltpu.make_async_copy(number, counts, sems.at[3])]
    for copy in copies:
        copy.start()
    for copy in copies:
        copy.wait()
    kinds = lax.broadcasted_iota(I32, (16, listed), 0)
    upto = lax.broadcasted_iota(I32, (listed, listed), 0) <= lanes((listed, listed))
    upto = upto.astype(F32).astype(BF16)
    spots = lax.broadcasted_iota(I32, (chips * span, listed), 0).astype(F32)
    offset = jnp.zeros((16, 1), F32)
    total = jnp.zeros((8, chips * span), F32)
    for i in range(blocks):
        col, own, place = words[0, i : i + 1], words[1, i : i + 1], words[2, i : i + 1]
        chip = jnp.where(lanes((1, listed)) < counts[i], own >> 1, chips)
        match = (kinds == chip).astype(F32)
        ranks = jnp.dot(match.astype(BF16), upto, preferred_element_type=F32) + offset
        offset = offset + jnp.sum(match, axis=1, keepdims=True)
        rank = jnp.sum(match * ranks, axis=0, keepdims=True) - 1
        target = jnp.where(chip < chips, chip.astype(F32) * span + rank, -1.0)
        chosen = (spots == target).astype(F32).astype(BF16)
        one = jnp.ones((1, listed), F32)
        fields = jnp.concatenate(
            [
                one,
                ((own & 1) * held + place).astype(F32),
                (col - columns).astype(F32),
                one * i,
                jnp.zeros((4, listed), F32),
            ],
            axis=0,
        )
        total += lax.dot_general(
            fields.astype(BF16), chosen, (((1,), (1,)), ((), ())), preferred_element_type=F32
        )
    row = lax.broadcasted_iota(I32, (8, span), 0)
    for c in range(chips):
        part = total[:, c * span : (c + 1) * span]
        number = jnp.broadcast_to(offset[c : c + 1], (8, span))
        part = jnp.where(row == 0, number, jnp.where(row == 2, part + columns, part))
        out_ref[c] = part[:4].astype(I32)


def tile_kernel(core, own_ref, other_ref, out_ref, buf, sems):
    held, _, width = own_ref.shape
    steps, step = buf.shape[:2]
    half = steps // 2
    mine = core[0]
    copies = [
        pltpu.make_async_copy(
            (own_ref if s < half else other_ref).at[pl.ds(s % half * step, step)],
            buf.at[s],
            sems.at[s],
        )
        for s in range(steps)
    ]
    for copy in copies:
        copy.start()
    for s in range(steps):
        copies[s].wait()
        start = (mine if s < half else 1 - mine) * held + s % half * step

        def one(i, _):
            hi, lo = split(buf[s, i])
            out_ref[start + i, :, :width] = hi
            out_ref[start + i, :, width:] = lo
            return 0

        lax.fori_loop(0, step, one, 0, unroll=4)


def gather_kernel(planes, place, own_ref, *refs):
    pieces, out_ref = refs[:-1], refs[-1]
    count, _, width = own_ref.shape
    quarter = count // 4
    blk = place[1]
    out_ref[planes * count] = jnp.zeros_like(out_ref[planes * count])

    def put(src, start, n):
        for i in range(n):
            hi, lo = split(src[i])
            out_ref[start + i, :, :width] = hi
            out_ref[start + i, :, width:] = lo

    put(own_ref, blk * count, count)
    for k in range(1, planes):
        plane = lax.rem(blk - k + planes, planes)
        for p in range(4):
            put(pieces[(k - 1) * 4 + p], plane * count + place[2 + p] * quarter, quarter)


def entry_kernel(lists, tiles_ref, proj_ref, out_ref):
    _, _, width = out_ref.shape
    out_ref[...] = jnp.zeros_like(out_ref)

    def multiply(base, n):
        terms = []
        for u in range(n):
            proj = proj_ref[lists[2, base + u]]
            d = jnp.dot(
                tiles_ref[lists[1, base + u]],
                jnp.concatenate([proj, proj], axis=0),
                preferred_element_type=F32,
            )
            terms.append(d[:, :width] + d[:, width:])
        for u in range(n):
            out_ref[lists[3, base + u]] += terms[u]

    def step(s, _):
        multiply(s * UNROLL, UNROLL)
        return 0

    number = lists[0, 0]
    steps = (number + UNROLL // 2 - 1) // UNROLL
    lax.fori_loop(0, steps, step, 0)

    @pl.when(number > steps * UNROLL)
    def _():
        multiply(steps * UNROLL, UNROLL // 2)


def final_kernel(left_ref, *refs):
    sums, out_ref = refs[:-1], refs[-1]
    for i in range(out_ref.shape[0]):
        total = functools.reduce(jnp.add, [r[i] for r in sums])
        out_ref[i] = triple(left_ref[i], total, ((1,), (0,)))


def call(kernel, prefetch, ins, out, scratch, args, estimate, limit, grid=(), out_spec=VMEM):
    return pl.pallas_call(
        kernel,
        out_shape=out,
        grid_spec=pltpu.PrefetchScalarGridSpec(
            num_scalar_prefetch=prefetch,
            grid=grid,
            in_specs=ins,
            out_specs=out_spec,
            scratch_shapes=scratch,
        ),
        compiler_params=pltpu.CompilerParams(vmem_limit_bytes=limit),
        cost_estimate=estimate,
    )(*args)


def work(
    vectors, left, right, tiles, pair_cols, pair_owner, pair_slot, pair_counts
):
    rows, planes = lax.axis_size("rows"), lax.axis_size("blk")
    row, blk = lax.axis_index("rows"), lax.axis_index("blk")
    blocks, fine, coarse = left.shape
    vecs = vectors.shape[1]
    count = right.shape[0]
    held = tiles.shape[0]
    listed = pair_cols.shape[1]
    chips = rows // 2
    cap = blocks * listed // chips
    quarter = count // 4
    core, chip = row & 1, row >> 1
    b0, b1 = chip & 1, (chip >> 1) & 1

    def physical(mask, core_at):
        return mask if core_at == 0 else (mask & ~3) | ((mask & 1) << 1) | ((mask >> 1) & 1)

    def across(mask):
        return [(r, r ^ (physical(mask, r % 2) << 1)) for r in range(rows)]

    def swap(x):
        return lax.ppermute(x, "rows", [(r, r ^ 1) for r in range(rows)])

    def turn(x, k):
        return lax.ppermute(x, "blk", [(b, (b + k) % planes) for b in range(planes)])

    mine = jnp.where(core == 0, b0, 2 + b1)
    theirs = jnp.where(core == 0, 2 + b1, b0)
    place = jnp.stack([mine, blk, mine, mine ^ 1, theirs, theirs ^ 1]).astype(I32)

    v = vectors.reshape(count, fine, vecs)
    v, right = in_hbm(v), in_hbm(right)

    def project(n):
        return call(
            project_kernel, 1, [HBM, HBM],
            jax.ShapeDtypeStruct((n, coarse, vecs), F32),
            [pltpu.VMEM((n, fine, vecs), F32)] * 2 + [pltpu.SemaphoreType.DMA((2,))],
            (place, v, right), cost(2 * n * 128**3 * 3, 2 * n * 65536), 8 * MIB,
        )

    sent = project(quarter)
    arrived = {k: turn(sent, k) for k in range(1, planes)}
    other_tiles = swap(tiles)

    span = pl.cdiv(cap, 128) * 128
    lists = call(
        functools.partial(list_kernel, chips, held, planes * count), 0, [HBM] * 4,
        jax.ShapeDtypeStruct((chips, 4, span), I32),
        [
            pltpu.VMEM((3, blocks, listed), I32),
            pltpu.SMEM((blocks,), I32),
            pltpu.SemaphoreType.DMA((4,)),
        ],
        (in_hbm(pair_cols), in_hbm(pair_owner), in_hbm(pair_slot), in_hbm(pair_counts)),
        cost(10**8, 16384), 8 * MIB,
    )
    tables = {}
    for m in range(chips):
        to_chip = chip ^ jnp.where(core == 0, physical(m, 0), physical(m, 1))
        chosen = lax.dynamic_index_in_dim(lists, to_chip, 0, keepdims=False)
        tables[m] = chosen if m == 0 else lax.ppermute(chosen, "rows", across(m))

    own = project(count)
    packed = call(
        tile_kernel, 1, [HBM, HBM],
        jax.ShapeDtypeStruct((2 * held, coarse, 2 * coarse), BF16),
        [pltpu.VMEM((held // 4, 8, coarse, coarse), F32), pltpu.SemaphoreType.DMA((held // 4,))],
        (core.reshape(1).astype(I32), in_hbm(tiles), in_hbm(other_tiles)),
        cost(held * 65536 * 4, held * 65536 * 4), 2 * held * 65536 + 4 * MIB,
    )

    pieces = []
    for k in range(1, planes):
        z = arrived[k]
        x = lax.ppermute(z, "rows", across(1))
        pieces += [z, x, swap(z), swap(x)]
    proj = call(
        functools.partial(gather_kernel, planes), 1, [VMEM] * (1 + len(pieces)),
        jax.ShapeDtypeStruct((planes * count + 1, coarse, 2 * vecs), BF16),
        [], (place, own, *pieces), cost(10**6, 3 * planes * count * 32768), 16 * MIB,
    )

    total = {
        m: [
            call(
                entry_kernel, 1, [VMEM, VMEM],
                jax.ShapeDtypeStruct((blocks, coarse, vecs), F32),
                [], (tables[m], packed, proj),
                cost(cap * 128**3 * 8, 4 * MIB), 12 * MIB,
            )
        ]
        for m in range(chips)
    }
    for m in masks_of(chips):
        bit = m & -m
        value = functools.reduce(jnp.add, total[m])
        total[m ^ bit].append(lax.ppermute(value, "rows", across(bit)))
    result = call(
        final_kernel, 0, [VMEM] * (1 + len(total[0])),
        jax.ShapeDtypeStruct((blocks, fine, vecs), F32),
        [], (left, *total[0]), cost(2 * blocks * 128**3 * 3, 2 * MIB), 8 * MIB,
    )
    return result.reshape(blocks * fine, vecs)


def masks_of(chips):
    return sorted(range(1, chips), key=lambda m: (m & -m, -m))


def solution(mesh):
    return jax.shard_map(
        work,
        mesh=mesh,
        in_specs=(
            P("blk", None),
            P(("rows", "blk"), None, None),
            P("blk", None, None),
            P("rows", None, None),
            P(("rows", "blk"), None),
            P(("rows", "blk"), None),
            P(("rows", "blk"), None),
            P(("rows", "blk")),
        ),
        out_specs=P(("rows", "blk"), None),
        check_vma=False,
    )
```

time: 68.2 us -> 71.3 us (1.045)
  the two profiles are of different devices: /device:TPU:16 before, /device:TPU:25 now
where the time goes in v2:
time: 71.3 us; the launch traced here: 71.1 us
  waiting for transfers between devices  35.5 us (50%)
  Pallas kernels  19.3 us (27%)
  starting transfers between devices  16 us (22%)
    pallas_call x10, Pallas kernels, call(): pl.pallas_call(kernel, out_shape=out, grid_spec=pltpu.PrefetchScalarGridS...  19.3 us
    ppermute x3, waiting for transfers between devices, turn(): lax.ppermute(x, 'blk', [(b, (b + k) % planes) for b in range(planes)])  15 us
    ppermute x3, waiting for transfers between devices, work(): total[m ^ bit].append(lax.ppermute(value, 'rows', across(bit)))  11.8 us
    ppermute x3, waiting for transfers between devices, work(): tables[m] = chosen if m == 0 else lax.ppermute(chosen, 'rows', across(m))  6.91 us
    ppermute x7, starting transfers between devices, swap(): return lax.ppermute(x, 'rows', [(r, r ^ 1) for r in range(rows)])  6.24 us
    ppermute x3, starting transfers between devices, work(): x = lax.ppermute(z, 'rows', across(1))  3.72 us
    ppermute x3, starting transfers between devices, work(): tables[m] = chosen if m == 0 else lax.ppermute(chosen, 'rows', across(m))  3.16 us
    ppermute x3, waiting for transfers between devices, work(): x = lax.ppermute(z, 'rows', across(1))  1.85 us
  transfers between devices with their start and end apart: 19, of which 7 were waited for; matrix products, arithmetic and copies ran while one was open for 0% of the time, Pallas kernels for 23%

profile of v2, /device:TPU:25, one launch (start us, length us, event | category | flops | bytes accessed | tf_op | source)
XLA Modules:
  0.0 71.1 jit_solution(16333012537035006620)
XLA Ops:
  0.0 0.7 collective-permute-start
  0.7 0.1 stack.24.place
  0.8 1.9 %shard_map.85 = f32[3,128,128]{2,1,0:T(8,128)S(1)} custom-call(s32[6]{0:T(128)S(1)} %stack.24.place, f32[12,128,128]{2,1,0:T(8,128)} %bitcast.16, f32[12,128,128]{2,1,0:T(8,128)} %r_ref.3), custom_call_target="tpu_custom_call" | custom-call | flops 37748736 | bytes 393216 | tf_op jit(solution)/shard_map/pallas_call | solution.py:199
  2.6 0.1 collective-permute-start.1
  2.7 1.3 %collective-permute-start.5 = (f32[3,128,128]{2,1,0:T(8,128)S(1)}, f32[3,128,128]{2,1,0:T(8,128)S(1)}, u32[]{:S(2)}, u32[]{:S(2)}) collective-permute-start(f32[3,128,128]{2,1,0:T(8,128)S(1)} %shard_map.85), channel_id=1, source_target_pairs={{0,2},{1,3},{2,0},{3,1},{4,6},{5,7},{6,4},{7,5},{8,10},{9,11},{10,... | collective-permute-start | bytes 589832 | tf_op jit(solution)/shard_map/ppermute | solution.py:240
  4.0 0.2 collective-permute-start.9
  4.2 4.9 %collective-permute-done.1.refs_0_ = f32[3,128,128]{2,1,0:T(8,128)S(1)} collective-permute-done((f32[3,128,128]{2,1,0:T(8,128)S(1)}, f32[3,128,128]{2,1,0:T(8,128)S(1)}, u32[]{:S(2)}, u32[]{:S(2)}) %collective-permute-start.1) | collective-permute-done | bytes 196640 | tf_op jit(solution)/shard_map/ppermute | solution.py:240
  9.1 1.2 %collective-permute-start.2 = (f32[3,128,128]{2,1,0:T(8,128)S(1)}, f32[3,128,128]{2,1,0:T(8,128)S(1)}, u32[]{:S(2)}, u32[]{:S(2)}) collective-permute-start(f32[3,128,128]{2,1,0:T(8,128)S(1)} %collective-permute-done.1.refs_0_), channel_id=1, source_target_pairs={{0,8},{4,20},{8,0},{12,28},{16,24},{20,4},{24,16},{28,12},{1,9},{5... | collective-permute-start | bytes 589832 | tf_op jit(solution)/shard_map/ppermute | solution.py:291
  10.4 1.3 %collective-permute-start.3 = (f32[3,128,128]{2,1,0:T(8,128)S(1)}, f32[3,128,128]{2,1,0:T(8,128)S(1)}, u32[]{:S(2)}, u32[]{:S(2)}) collective-permute-start(f32[3,128,128]{2,1,0:T(8,128)S(1)} %collective-permute-done.1.refs_0_), channel_id=1, source_target_pairs={{0,4},{4,0},{8,12},{12,8},{16,20},{20,16},{24,28},{28,24},{1,5},{5... | collective-permute-start | bytes 589832 | tf_op jit(solution)/shard_map/ppermute | solution.py:237
  11.6 10.0 %collective-permute-done.5.refs_4_ = f32[3,128,128]{2,1,0:T(8,128)S(1)} collective-permute-done((f32[3,128,128]{2,1,0:T(8,128)S(1)}, f32[3,128,128]{2,1,0:T(8,128)S(1)}, u32[]{:S(2)}, u32[]{:S(2)}) %collective-permute-start.5) | collective-permute-done | bytes 196640 | tf_op jit(solution)/shard_map/ppermute | solution.py:240
  21.7 1.2 %collective-permute-start.6 = (f32[3,128,128]{2,1,0:T(8,128)S(1)}, f32[3,128,128]{2,1,0:T(8,128)S(1)}, u32[]{:S(2)}, u32[]{:S(2)}) collective-permute-start(f32[3,128,128]{2,1,0:T(8,128)S(1)} %collective-permute-done.5.refs_4_), channel_id=1, source_target_pairs={{0,8},{4,20},{8,0},{12,28},{16,24},{20,4},{24,16},{28,12},{1,9},{5... | collective-permute-start | bytes 589832 | tf_op jit(solution)/shard_map/ppermute | solution.py:291
  22.9 0.0 collective-permute-done.9.refs_8_
  22.9 1.1 %collective-permute-start.7 = (f32[3,128,128]{2,1,0:T(8,128)S(1)}, f32[3,128,128]{2,1,0:T(8,128)S(1)}, u32[]{:S(2)}, u32[]{:S(2)}) collective-permute-start(f32[3,128,128]{2,1,0:T(8,128)S(1)} %collective-permute-done.5.refs_4_), channel_id=1, source_target_pairs={{0,4},{4,0},{8,12},{12,8},{16,20},{20,16},{24,28},{28,24},{1,5},{5... | collective-permute-start | bytes 589832 | tf_op jit(solution)/shard_map/ppermute | solution.py:237
  24.0 0.0 collective-permute-done.2.refs_1_
  24.0 1.2 %collective-permute-start.10 = (f32[3,128,128]{2,1,0:T(8,128)S(1)}, f32[3,128,128]{2,1,0:T(8,128)S(1)}, u32[]{:S(2)}, u32[]{:S(2)}) collective-permute-start(f32[3,128,128]{2,1,0:T(8,128)S(1)} %collective-permute-done.9.refs_8_), channel_id=1, source_target_pairs={{0,8},{4,20},{8,0},{12,28},{16,24},{20,4},{24,16},{28,12},{1,9},{5... | collective-permute-start | bytes 589832 | tf_op jit(solution)/shard_map/ppermute | solution.py:291
  25.3 0.0 collective-permute-done.3.refs_2_
  25.3 0.0 collective-permute-start.11
  25.3 1.2 %collective-permute-done.6.refs_5_ = f32[3,128,128]{2,1,0:T(8,128)S(1)} collective-permute-done((f32[3,128,128]{2,1,0:T(8,128)S(1)}, f32[3,128,128]{2,1,0:T(8,128)S(1)}, u32[]{:S(2)}, u32[]{:S(2)}) %collective-permute-start.6) | collective-permute-done | bytes 196640 | tf_op jit(solution)/shard_map/ppermute | solution.py:291
  26.5 1.7 %collective-permute-start.4 = (f32[3,128,128]{2,1,0:T(8,128)S(1)}, f32[3,128,128]{2,1,0:T(8,128)S(1)}, u32[]{:S(2)}, u32[]{:S(2)}) collective-permute-start(f32[3,128,128]{2,1,0:T(8,128)S(1)} %collective-permute-done.2.refs_1_), channel_id=1, source_target_pairs={{0,4},{4,0},{8,12},{12,8},{16,20},{20,16},{24,28},{28,24},{1,5},{5... | collective-permute-start | bytes 589832 | tf_op jit(solution)/shard_map/ppermute | solution.py:237
  28.2 0.0 collective-permute-done.7.refs_6_
  28.2 0.0 collective-permute-start.8
  28.2 0.6 collective-permute-done.10.refs_9_
  28.8 1.5 %collective-permute-start.12 = (f32[3,128,128]{2,1,0:T(8,128)S(1)}, f32[3,128,128]{2,1,0:T(8,128)S(1)}, u32[]{:S(2)}, u32[]{:S(2)}) collective-permute-start(f32[3,128,128]{2,1,0:T(8,128)S(1)} %collective-permute-done.10.refs_9_), channel_id=1, source_target_pairs={{0,4},{4,0},{8,12},{12,8},{16,20},{20,16},{24,28},{28,24},{1,5},{5... | collective-permute-start | bytes 589832 | tf_op jit(solution)/shard_map/ppermute | solution.py:237
  30.3 2.2 %shard_map.82 = s32[4,4,128]{2,1,0:T(4,128)S(1)} custom-call(s32[8,32]{1,0:T(8,128)} %cols.1, s32[8,32]{1,0:T(8,128)} %owner.1, s32[8,32]{1,0:T(8,128)} %slot.1, s32[8]{0:T(128)} %number.1), custom_call_target="tpu_custom_call" | custom-call | flops 100000000 | bytes 16384 | tf_op jit(solution)/shard_map/pallas_call | solution.py:199
  32.5 2.2 %collective-permute-start.16 = (s32[4,128]{1,0:T(4,128)S(1)}, s32[4,128]{1,0:T(4,128)S(1)}, u32[]{:S(2)}, u32[]{:S(2)}) collective-permute-start(s32[4,128]{1,0:T(4,128)S(1)} %get-tuple-element.5), channel_id=1, source_target_pairs={{0,24},{4,28},{8,16},{12,20},{16,8},{20,12},{24,0},{28,4},{1,25},{... | collective-permute-start | bytes 6152 | tf_op jit(solution)/shard_map/ppermute | solution.py:277
  34.7 2.4 %shard_map.84.own_ref = f32[12,128,128]{2,1,0:T(8,128)S(1)} custom-call(s32[6]{0:T(128)S(1)} %stack.24.place, f32[12,128,128]{2,1,0:T(8,128)} %bitcast.17, f32[12,128,128]{2,1,0:T(8,128)} %r_ref.3), custom_call_target="tpu_custom_call" | custom-call | flops 150994944 | bytes 1572864 | tf_op jit(solution)/shard_map/pallas_call | solution.py:199
  37.2 0.0 collective-permute-done.12.refs_11_
  37.2 1.1 %shard_map.86.proj_ref = bf16[49,128,256]{2,1,0:T(8,128)(2,1)S(1)} custom-call(s32[6]{0:T(128)S(1)} %stack.24.place, f32[12,128,128]{2,1,0:T(8,128)S(1)} %shard_map.84.own_ref, f32[3,128,128]{2,1,0:T(8,128)S(1)} %collective-permute-done.1.refs_0_, f32[3,128,128]{2,1,0:T(8,128)S(1)} %collective-permute-done.2.refs_1_, ...), custom_call_target="tpu_custom_call" | custom-call | flops 1000000 | bytes 4718592 | tf_op jit(solution)/shard_map/pallas_call | solution.py:199
  38.3 0.0 collective-permute-done.other_ref
  38.3 3.6 %shard_map.83.tiles_ref = bf16[128,128,256]{2,1,0:T(8,128)(2,1)S(1)} custom-call(s32[1]{0:T(128)} %bitcast.1.core, f32[64,128,128]{2,1,0:T(8,128)} %own_ref.1, f32[64,128,128]{2,1,0:T(8,128)} %collective-permute-done.other_ref), custom_call_target="tpu_custom_call" | custom-call | flops 16777216 | bytes 16777216 | tf_op jit(solution)/shard_map/pallas_call | solution.py:199
  41.9 0.0 collective-permute-done.16.lists
  41.9 2.0 %shard_map.90 = f32[8,128,128]{2,1,0:T(8,128)S(1)} custom-call(s32[4,128]{1,0:T(4,128)S(1)} %collective-permute-done.16.lists, bf16[128,128,256]{2,1,0:T(8,128)(2,1)S(1)} %shard_map.83.tiles_ref, bf16[49,128,256]{2,1,0:T(8,128)(2,1)S(1)} %shard_map.86.proj_ref), custom_call_target="tpu_custom_call" | custom-call | flops 1073741824 | bytes 4194304 | tf_op jit(solution)/shard_map/pallas_call | solution.py:199
  43.9 0.6 collective-permute-start.17
  44.5 0.9 %collective-permute-start.13 = (s32[4,128]{1,0:T(4,128)S(1)}, s32[4,128]{1,0:T(4,128)S(1)}, u32[]{:S(2)}, u32[]{:S(2)}) collective-permute-start(s32[4,128]{1,0:T(4,128)S(1)} %get-tuple-element.7), channel_id=1, source_target_pairs={{0,8},{4,20},{8,0},{12,28},{16,24},{20,4},{24,16},{28,12},{1,9},{5... | collective-permute-start | bytes 6152 | tf_op jit(solution)/shard_map/ppermute | solution.py:277
  45.4 0.0 collective-permute-start.15
  45.4 6.9 %collective-permute-done.13.lists = s32[4,128]{1,0:T(4,128)S(1)} collective-permute-done((s32[4,128]{1,0:T(4,128)S(1)}, s32[4,128]{1,0:T(4,128)S(1)}, u32[]{:S(2)}, u32[]{:S(2)}) %collective-permute-start.13) | collective-permute-done | bytes 2080 | tf_op jit(solution)/shard_map/ppermute | solution.py:277
  52.3 1.4 %shard_map.88 = f32[8,128,128]{2,1,0:T(8,128)S(1)} custom-call(s32[4,128]{1,0:T(4,128)S(1)} %collective-permute-done.13.lists, bf16[128,128,256]{2,1,0:T(8,128)(2,1)S(1)} %shard_map.83.tiles_ref, bf16[49,128,256]{2,1,0:T(8,128)(2,1)S(1)} %shard_map.86.proj_ref), custom_call_target="tpu_custom_call" | custom-call | flops 1073741824 | bytes 4194304 | tf_op jit(solution)/shard_map/pallas_call | solution.py:199
  53.7 0.6 collective-permute-start.14
  54.3 0.0 collective-permute-done.15.lists
  54.3 2.3 %shard_map.89 = f32[8,128,128]{2,1,0:T(8,128)S(1)} custom-call(s32[4,128]{1,0:T(4,128)S(1)} %collective-permute-done.15.lists, bf16[128,128,256]{2,1,0:T(8,128)(2,1)S(1)} %shard_map.83.tiles_ref, bf16[49,128,256]{2,1,0:T(8,128)(2,1)S(1)} %shard_map.86.proj_ref), custom_call_target="tpu_custom_call" | custom-call | flops 1073741824 | bytes 4194304 | tf_op jit(solution)/shard_map/pallas_call | solution.py:199
  56.6 0.0 collective-permute-done.17
  56.6 0.1 add.25
  56.7 0.1 collective-permute-start.18
  56.8 0.0 copy-start
  56.8 1.4 %shard_map.87.refs_0_ = f32[8,128,128]{2,1,0:T(8,128)S(1)} custom-call(s32[4,128]{1,0:T(4,128)S(1)} %get-tuple-element.8.lists, bf16[128,128,256]{2,1,0:T(8,128)(2,1)S(1)} %shard_map.83.tiles_ref, bf16[49,128,256]{2,1,0:T(8,128)(2,1)S(1)} %shard_map.86.proj_ref), custom_call_target="tpu_custom_call" | custom-call | flops 1073741824 | bytes 4194304 | tf_op jit(solution)/shard_map/pallas_call | solution.py:199
  58.2 3.9 %collective-permute-done.14.refs_1_ = f32[8,128,128]{2,1,0:T(8,128)S(1)} collective-permute-done((f32[8,128,128]{2,1,0:T(8,128)S(1)}, f32[8,128,128]{2,1,0:T(8,128)S(1)}, u32[]{:S(2)}, u32[]{:S(2)}) %collective-permute-start.14) | collective-permute-done | bytes 524320 | tf_op jit(solution)/shard_map/ppermute | solution.py:313
  62.1 7.8 %collective-permute-done.18.refs_2_ = f32[8,128,128]{2,1,0:T(8,128)S(1)} collective-permute-done((f32[8,128,128]{2,1,0:T(8,128)S(1)}, f32[8,128,128]{2,1,0:T(8,128)S(1)}, u32[]{:S(2)}, u32[]{:S(2)}) %collective-permute-start.18) | collective-permute-done | bytes 524320 | tf_op jit(solution)/shard_map/ppermute | solution.py:313
  70.0 1.2 %shard_map.91 = f32[8,128,128]{2,1,0:T(8,128)} custom-call(f32[8,128,128]{2,1,0:T(8,128)S(1)} %copy-done, f32[8,128,128]{2,1,0:T(8,128)S(1)} %shard_map.87.refs_0_, f32[8,128,128]{2,1,0:T(8,128)S(1)} %collective-permute-done.14.refs_1_, f32[8,128,128]{2,1,0:T(8,128)S(1)} %collective-permute-done.18.refs_2_), custom_call_target="tpu_custom_call" | custom-call | flops 100663296 | bytes 2097152 | tf_op jit(solution)/shard_map/pallas_call | solution.py:199
  (5 shorter events, 0.0 us)
Async XLA Ops:
  0.0 38.3 %collective-permute-start = (f32[64,128,128]{2,1,0:T(8,128)}, f32[64,128,128]{2,1,0:T(8,128)}, u32[]{:S(2)}, u32[]{:S(2)}) collective-permute-start(f32[64,128,128]{2,1,0:T(8,128)} %own_ref.1), channel_id=1, source_target_pairs={{0,4},{4,0},{8,12},{12,8},{16,20},{20,16},{24,28},{28,24},{1,5},{5... | collective-permute-start | bytes 12582920 | tf_op jit(solution)/shard_map/ppermute | solution.py:237
  2.6 6.5 %collective-permute-start.1 = (f32[3,128,128]{2,1,0:T(8,128)S(1)}, f32[3,128,128]{2,1,0:T(8,128)S(1)}, u32[]{:S(2)}, u32[]{:S(2)}) collective-permute-start(f32[3,128,128]{2,1,0:T(8,128)S(1)} %shard_map.85), channel_id=1, source_target_pairs={{0,1},{1,2},{2,3},{3,0},{4,5},{5,6},{6,7},{7,4},{8,9},{9,10},{10,1... | collective-permute-start | bytes 589832 | tf_op jit(solution)/shard_map/ppermute | solution.py:240
  2.7 19.0 %collective-permute-start.5 = (f32[3,128,128]{2,1,0:T(8,128)S(1)}, f32[3,128,128]{2,1,0:T(8,128)S(1)}, u32[]{:S(2)}, u32[]{:S(2)}) collective-permute-start(f32[3,128,128]{2,1,0:T(8,128)S(1)} %shard_map.85), channel_id=1, source_target_pairs={{0,2},{1,3},{2,0},{3,1},{4,6},{5,7},{6,4},{7,5},{8,10},{9,11},{10,... | collective-permute-start | bytes 589832 | tf_op jit(solution)/shard_map/ppermute | solution.py:240
  4.0 18.9 %collective-permute-start.9 = (f32[3,128,128]{2,1,0:T(8,128)S(1)}, f32[3,128,128]{2,1,0:T(8,128)S(1)}, u32[]{:S(2)}, u32[]{:S(2)}) collective-permute-start(f32[3,128,128]{2,1,0:T(8,128)S(1)} %shard_map.85), channel_id=1, source_target_pairs={{0,3},{1,0},{2,1},{3,2},{4,7},{5,4},{6,5},{7,6},{8,11},{9,8},{10,9... | collective-permute-start | bytes 589832 | tf_op jit(solution)/shard_map/ppermute | solution.py:240
  9.1 14.9 %collective-permute-start.2 = (f32[3,128,128]{2,1,0:T(8,128)S(1)}, f32[3,128,128]{2,1,0:T(8,128)S(1)}, u32[]{:S(2)}, u32[]{:S(2)}) collective-permute-start(f32[3,128,128]{2,1,0:T(8,128)S(1)} %collective-permute-done.1.refs_0_), channel_id=1, source_target_pairs={{0,8},{4,20},{8,0},{12,28},{16,24},{20,4},{24,16},{28,12},{1,9},{5... | collective-permute-start | bytes 589832 | tf_op jit(solution)/shard_map/ppermute | solution.py:291
  10.4 14.9 %collective-permute-start.3 = (f32[3,128,128]{2,1,0:T(8,128)S(1)}, f32[3,128,128]{2,1,0:T(8,128)S(1)}, u32[]{:S(2)}, u32[]{:S(2)}) collective-permute-start(f32[3,128,128]{2,1,0:T(8,128)S(1)} %collective-permute-done.1.refs_0_), channel_id=1, source_target_pairs={{0,4},{4,0},{8,12},{12,8},{16,20},{20,16},{24,28},{28,24},{1,5},{5... | collective-permute-start | bytes 589832 | tf_op jit(solution)/shard_map/ppermute | solution.py:237
  21.7 4.8 %collective-permute-start.6 = (f32[3,128,128]{2,1,0:T(8,128)S(1)}, f32[3,128,128]{2,1,0:T(8,128)S(1)}, u32[]{:S(2)}, u32[]{:S(2)}) collective-permute-start(f32[3,128,128]{2,1,0:T(8,128)S(1)} %collective-permute-done.5.refs_4_), channel_id=1, source_target_pairs={{0,8},{4,20},{8,0},{12,28},{16,24},{20,4},{24,16},{28,12},{1,9},{5... | collective-permute-start | bytes 589832 | tf_op jit(solution)/shard_map/ppermute | solution.py:291
  22.9 5.3 %collective-permute-start.7 = (f32[3,128,128]{2,1,0:T(8,128)S(1)}, f32[3,128,128]{2,1,0:T(8,128)S(1)}, u32[]{:S(2)}, u32[]{:S(2)}) collective-permute-start(f32[3,128,128]{2,1,0:T(8,128)S(1)} %collective-permute-done.5.refs_4_), channel_id=1, source_target_pairs={{0,4},{4,0},{8,12},{12,8},{16,20},{20,16},{24,28},{28,24},{1,5},{5... | collective-permute-start | bytes 589832 | tf_op jit(solution)/shard_map/ppermute | solution.py:237
  24.0 4.8 %collective-permute-start.10 = (f32[3,128,128]{2,1,0:T(8,128)S(1)}, f32[3,128,128]{2,1,0:T(8,128)S(1)}, u32[]{:S(2)}, u32[]{:S(2)}) collective-permute-start(f32[3,128,128]{2,1,0:T(8,128)S(1)} %collective-permute-done.9.refs_8_), channel_id=1, source_target_pairs={{0,8},{4,20},{8,0},{12,28},{16,24},{20,4},{24,16},{28,12},{1,9},{5... | collective-permute-start | bytes 589832 | tf_op jit(solution)/shard_map/ppermute | solution.py:291
  25.3 7.2 %collective-permute-start.11 = (f32[3,128,128]{2,1,0:T(8,128)S(1)}, f32[3,128,128]{2,1,0:T(8,128)S(1)}, u32[]{:S(2)}, u32[]{:S(2)}) collective-permute-start(f32[3,128,128]{2,1,0:T(8,128)S(1)} %collective-permute-done.9.refs_8_), channel_id=1, source_target_pairs={{0,4},{4,0},{8,12},{12,8},{16,20},{20,16},{24,28},{28,24},{1,5},{5... | collective-permute-start | bytes 589832 | tf_op jit(solution)/shard_map/ppermute | solution.py:237
  26.5 10.7 %collective-permute-start.4 = (f32[3,128,128]{2,1,0:T(8,128)S(1)}, f32[3,128,128]{2,1,0:T(8,128)S(1)}, u32[]{:S(2)}, u32[]{:S(2)}) collective-permute-start(f32[3,128,128]{2,1,0:T(8,128)S(1)} %collective-permute-done.2.refs_1_), channel_id=1, source_target_pairs={{0,4},{4,0},{8,12},{12,8},{16,20},{20,16},{24,28},{28,24},{1,5},{5... | collective-permute-start | bytes 589832 | tf_op jit(solution)/shard_map/ppermute | solution.py:237
  28.2 9.0 %collective-permute-start.8 = (f32[3,128,128]{2,1,0:T(8,128)S(1)}, f32[3,128,128]{2,1,0:T(8,128)S(1)}, u32[]{:S(2)}, u32[]{:S(2)}) collective-permute-start(f32[3,128,128]{2,1,0:T(8,128)S(1)} %collective-permute-done.6.refs_5_), channel_id=1, source_target_pairs={{0,4},{4,0},{8,12},{12,8},{16,20},{20,16},{24,28},{28,24},{1,5},{5... | collective-permute-start | bytes 589832 | tf_op jit(solution)/shard_map/ppermute | solution.py:237
  28.8 8.4 %collective-permute-start.12 = (f32[3,128,128]{2,1,0:T(8,128)S(1)}, f32[3,128,128]{2,1,0:T(8,128)S(1)}, u32[]{:S(2)}, u32[]{:S(2)}) collective-permute-start(f32[3,128,128]{2,1,0:T(8,128)S(1)} %collective-permute-done.10.refs_9_), channel_id=1, source_target_pairs={{0,4},{4,0},{8,12},{12,8},{16,20},{20,16},{24,28},{28,24},{1,5},{5... | collective-permute-start | bytes 589832 | tf_op jit(solution)/shard_map/ppermute | solution.py:237
  32.5 9.4 %collective-permute-start.16 = (s32[4,128]{1,0:T(4,128)S(1)}, s32[4,128]{1,0:T(4,128)S(1)}, u32[]{:S(2)}, u32[]{:S(2)}) collective-permute-start(s32[4,128]{1,0:T(4,128)S(1)} %get-tuple-element.5), channel_id=1, source_target_pairs={{0,24},{4,28},{8,16},{12,20},{16,8},{20,12},{24,0},{28,4},{1,25},{... | collective-permute-start | bytes 6152 | tf_op jit(solution)/shard_map/ppermute | solution.py:277
  43.9 12.7 %collective-permute-start.17 = (f32[8,128,128]{2,1,0:T(8,128)S(1)}, f32[8,128,128]{2,1,0:T(8,128)S(1)}, u32[]{:S(2)}, u32[]{:S(2)}) collective-permute-start(f32[8,128,128]{2,1,0:T(8,128)S(1)} %shard_map.90), channel_id=1, source_target_pairs={{0,8},{4,20},{8,0},{12,28},{16,24},{20,4},{24,16},{28,12},{1,9},{5... | collective-permute-start | bytes 1572872 | tf_op jit(solution)/shard_map/ppermute | solution.py:313
  44.5 7.8 %collective-permute-start.13 = (s32[4,128]{1,0:T(4,128)S(1)}, s32[4,128]{1,0:T(4,128)S(1)}, u32[]{:S(2)}, u32[]{:S(2)}) collective-permute-start(s32[4,128]{1,0:T(4,128)S(1)} %get-tuple-element.7), channel_id=1, source_target_pairs={{0,8},{4,20},{8,0},{12,28},{16,24},{20,4},{24,16},{28,12},{1,9},{5... | collective-permute-start | bytes 6152 | tf_op jit(solution)/shard_map/ppermute | solution.py:277
  45.4 8.9 %collective-permute-start.15 = (s32[4,128]{1,0:T(4,128)S(1)}, s32[4,128]{1,0:T(4,128)S(1)}, u32[]{:S(2)}, u32[]{:S(2)}) collective-permute-start(s32[4,128]{1,0:T(4,128)S(1)} %get-tuple-element.6), channel_id=1, source_target_pairs={{0,16},{4,12},{8,24},{12,4},{16,0},{20,28},{24,8},{28,20},{1,17},{... | collective-permute-start | bytes 6152 | tf_op jit(solution)/shard_map/ppermute | solution.py:277
  53.7 8.4 %collective-permute-start.14 = (f32[8,128,128]{2,1,0:T(8,128)S(1)}, f32[8,128,128]{2,1,0:T(8,128)S(1)}, u32[]{:S(2)}, u32[]{:S(2)}) collective-permute-start(f32[8,128,128]{2,1,0:T(8,128)S(1)} %shard_map.88), channel_id=1, source_target_pairs={{0,8},{4,20},{8,0},{12,28},{16,24},{20,4},{24,16},{28,12},{1,9},{5... | collective-permute-start | bytes 1572872 | tf_op jit(solution)/shard_map/ppermute | solution.py:313
  56.7 13.3 %collective-permute-start.18 = (f32[8,128,128]{2,1,0:T(8,128)S(1)}, f32[8,128,128]{2,1,0:T(8,128)S(1)}, u32[]{:S(2)}, u32[]{:S(2)}) collective-permute-start(f32[8,128,128]{2,1,0:T(8,128)S(1)} %add.25), channel_id=1, source_target_pairs={{0,16},{4,12},{8,24},{12,4},{16,0},{20,28},{24,8},{28,20},{1,17},{... | collective-permute-start | bytes 1572872 | tf_op jit(solution)/shard_map/ppermute | solution.py:313
  56.8 13.2 %copy-start = (f32[8,128,128]{2,1,0:T(8,128)S(1)}, f32[8,128,128]{2,1,0:T(8,128)}, u32[]{:S(2)}) copy-start(f32[8,128,128]{2,1,0:T(8,128)} %left_ref.1) | copy-start | bytes 1572868

commit v3 on v2

--- a/solution.py
+++ b/solution.py
@@ -46,7 +46,8 @@
     return dot(a_hi, b_hi) + dot(a_hi, b_lo) + dot(a_lo, b_hi)
 
 
-def project_kernel(place, v_ref, r_ref, out_ref, v_buf, r_buf, sems):
+def project_kernel(place, v_ref, r_ref, out_ref, *rest):
+    v_buf, r_buf, sems = rest[-3:]
     count = v_buf.shape[0]
     first = place[0] * count if count < v_ref.shape[0] else 0
     copies = [
@@ -59,6 +60,9 @@
         copy.wait()
     for i in range(count):
         out_ref[i] = triple(r_buf[i], v_buf[i], ((0,), (0,)))
+        for half_ref in rest[:-3]:
+            rows = half_ref.shape[1]
+            half_ref[i] = out_ref[i, pl.ds(pl.multiple_of(place[6] * rows, rows), rows)]
 
 
 def list_kernel(chips, held, columns, cols, owner, slot, number, out_ref, words, counts, sems):
@@ -145,17 +149,29 @@
     blk = place[1]
     out_ref[planes * count] = jnp.zeros_like(out_ref[planes * count])
 
-    def put(src, start, n):
-        for i in range(n):
+    def put(src, start, first_row):
+        rows = pl.ds(first_row, src.shape[1])
+        for i in range(src.shape[0]):
             hi, lo = split(src[i])
-            out_ref[start + i, :, :width] = hi
-            out_ref[start + i, :, width:] = lo
-
-    put(own_ref, blk * count, count)
+            out_ref[start + i, rows, :width] = hi
+            out_ref[start + i, rows, width:] = lo
+
+    put(own_ref, blk * count, 0)
+    at = 0
     for k in range(1, planes):
-        plane = lax.rem(blk - k + planes, planes)
+        start = lax.rem(blk - k + planes, planes) * count
+        if k != planes // 2:
+            for p in range(4):
+                put(pieces[at + p], start + place[2 + p] * quarter, 0)
+            at += 4
+            continue
         for p in range(4):
-            put(pieces[(k - 1) * 4 + p], plane * count + place[2 + p] * quarter, quarter)
+            half = place[6 + p // 2]
+            rows = pieces[at].shape[1]
+            for side in range(2):
+                row = pl.multiple_of((half if side == 0 else 1 - half) * rows, rows)
+                put(pieces[at + 2 * p + side], start + place[2 + p] * quarter, row)
+        at += 8
 
 
 def entry_kernel(lists, tiles_ref, proj_ref, out_ref):
@@ -241,21 +257,30 @@
 
     mine = jnp.where(core == 0, b0, 2 + b1)
     theirs = jnp.where(core == 0, 2 + b1, b0)
-    place = jnp.stack([mine, blk, mine, mine ^ 1, theirs, theirs ^ 1]).astype(I32)
+    row_half = jnp.where(core == 0, b1, b0)
+    their_half = jnp.where(core == 0, b0, b1)
+    place = jnp.stack([mine, blk, mine, mine ^ 1, theirs, theirs ^ 1, row_half, their_half]).astype(I32)
 
     v = vectors.reshape(count, fine, vecs)
     v, right = in_hbm(v), in_hbm(right)
 
-    def project(n):
+    def project(n, out):
         return call(
-            project_kernel, 1, [HBM, HBM],
-            jax.ShapeDtypeStruct((n, coarse, vecs), F32),
+            project_kernel, 1, [HBM, HBM], out,
             [pltpu.VMEM((n, fine, vecs), F32)] * 2 + [pltpu.SemaphoreType.DMA((2,))],
             (place, v, right), cost(2 * n * 128**3 * 3, 2 * n * 65536), 8 * MIB,
+            out_spec=[VMEM] * len(out) if isinstance(out, list) else VMEM,
         )
 
-    sent = project(quarter)
-    arrived = {k: turn(sent, k) for k in range(1, planes)}
+    middle = planes // 2
+    sent, sent_half = project(
+        quarter,
+        [
+            jax.ShapeDtypeStruct((quarter, coarse, vecs), F32),
+            jax.ShapeDtypeStruct((quarter, coarse // 2, vecs), F32),
+        ],
+    )
+    arrived = {k: turn(sent_half if k == middle else sent, k) for k in range(1, planes)}
     other_tiles = swap(tiles)
 
     span = pl.cdiv(cap, 128) * 128
@@ -276,7 +301,7 @@
         chosen = lax.dynamic_index_in_dim(lists, to_chip, 0, keepdims=False)
         tables[m] = chosen if m == 0 else lax.ppermute(chosen, "rows", across(m))
 
-    own = project(count)
+    own = project(count, jax.ShapeDtypeStruct((count, coarse, vecs), F32))
     packed = call(
         tile_kernel, 1, [HBM, HBM],
         jax.ShapeDtypeStruct((2 * held, coarse, 2 * coarse), BF16),
@@ -285,11 +310,20 @@
         cost(held * 65536 * 4, held * 65536 * 4), 2 * held * 65536 + 4 * MIB,
     )
 
+    def spread(x, mask=1):
+        return lax.ppermute(x, "rows", across(mask))
+
     pieces = []
     for k in range(1, planes):
         z = arrived[k]
-        x = lax.ppermute(z, "rows", across(1))
-        pieces += [z, x, swap(z), swap(x)]
+        if k == middle:
+            rest = spread(z, 2)
+            x, x_rest = spread(z), spread(rest)
+            pieces += [z, rest, x, x_rest, swap(z), swap(rest)]
+            pieces += [swap(x), swap(x_rest)]
+        else:
+            x = spread(z)
+            pieces += [z, x, swap(z), swap(x)]
     proj = call(
         functools.partial(gather_kernel, planes), 1, [VMEM] * (1 + len(pieces)),
         jax.ShapeDtypeStruct((planes * count + 1, coarse, 2 * vecs), BF16),

time: 71.3 us -> 74.7 us (1.048)
  starting transfers between devices: 16 us -> 18.4 us
  waiting for transfers between devices: 35.5 us -> 36.4 us
    ppermute x7 -> x9, waiting for transfers between devices: 0.02 us -> 2.58 us  [swap(): return lax.ppermute(x, 'rows', [(r, r ^ 1) for r in range(rows)])]
    ppermute x7 -> x9, starting transfers between devices: 6.24 us -> 7.94 us  [swap(): return lax.ppermute(x, 'rows', [(r, r ^ 1) for r in range(rows)])]
    ppermute x3, waiting for transfers between devices: 15 us -> 13.3 us  [turn(): lax.ppermute(x, 'blk', [(b, (b + k) % planes) for b in range(planes)])]
    ppermute x3 -> x5, starting transfers between devices: 3.72 us -> 4.74 us  [spread(): return lax.ppermute(x, 'rows', across(mask))]
    ppermute x3 -> x5, waiting for transfers between devices: 1.85 us -> 2 us  [spread(): return lax.ppermute(x, 'rows', across(mask))]
  transfers between devices with their start and end apart: 19 -> 23, of which waited for: 7 -> 8; matrix products, arithmetic and copies ran while one was open for 0% -> 0% of each run, Pallas kernels for 23% -> 22%
where the time goes in v3:
time: 74.7 us; the launch traced here: 74.5 us
  waiting for transfers between devices  36.4 us (49%)
  Pallas kernels  19.3 us (26%)
  starting transfers between devices  18.4 us (25%)
    pallas_call x10, Pallas kernels, call(): pl.pallas_call(kernel, out_shape=out, grid_spec=pltpu.PrefetchScalarGridS...  19.3 us
    ppermute x3, waiting for transfers between devices, turn(): lax.ppermute(x, 'blk', [(b, (b + k) % planes) for b in range(planes)])  13.3 us
    ppermute x3, waiting for transfers between devices, work(): total[m ^ bit].append(lax.ppermute(value, 'rows', across(bit)))  11.9 us
    ppermute x9, starting transfers between devices, swap(): return lax.ppermute(x, 'rows', [(r, r ^ 1) for r in range(rows)])  7.94 us
    ppermute x3, waiting for transfers between devices, work(): tables[m] = chosen if m == 0 else lax.ppermute(chosen, 'rows', across(m))  6.67 us
    ppermute x5, starting transfers between devices, spread(): return lax.ppermute(x, 'rows', across(mask))  4.74 us
    ppermute x3, starting transfers between devices, work(): tables[m] = chosen if m == 0 else lax.ppermute(chosen, 'rows', across(m))  2.87 us
    ppermute x9, waiting for transfers between devices, swap(): return lax.ppermute(x, 'rows', [(r, r ^ 1) for r in range(rows)])  2.58 us
  transfers between devices with their start and end apart: 23, of which 8 were waited for; matrix products, arithmetic and copies ran while one was open for 0% of the time, Pallas kernels for 22%

profile of v3, /device:TPU:25, one launch (start us, length us, event | category | flops | bytes accessed | tf_op | source)
XLA Modules:
  0.0 74.5 jit_solution(16353575510416081298)
XLA Ops:
  0.0 0.7 collective-permute-start
  0.7 0.1 stack.32.place
  0.8 1.9 %shard_map.85 = (f32[3,128,128]{2,1,0:T(8,128)S(1)}, f32[3,64,128]{2,1,0:T(8,128)S(1)}) custom-call(s32[8]{0:T(128)S(1)} %stack.32.place, f32[12,128,128]{2,1,0:T(8,128)} %bitcast.18, f32[12,128,128]{2,1,0:T(8,128)} %r_ref.3), custom_call_target="tpu_custom_call" | custom-call | flops 37748736 | bytes 393216 | tf_op jit(solution)/shard_map/pallas_call | solution.py:215
  2.6 0.1 collective-permute-start.1
  2.7 1.3 %collective-permute-start.5 = (f32[3,64,128]{2,1,0:T(8,128)S(1)}, f32[3,64,128]{2,1,0:T(8,128)S(1)}, u32[]{:S(2)}, u32[]{:S(2)}) collective-permute-start(f32[3,64,128]{2,1,0:T(8,128)S(1)} %get-tuple-element.8), channel_id=1, source_target_pairs={{0,2},{1,3},{2,0},{3,1},{4,6},{5,7},{6,4},{7,5},{8,10},{9,11},{10,... | collective-permute-start | bytes 294920 | tf_op jit(solution)/shard_map/ppermute | solution.py:256
  4.0 0.2 collective-permute-start.13
  4.2 13.2 %collective-permute-done.5.refs_4_ = f32[3,64,128]{2,1,0:T(8,128)S(1)} collective-permute-done((f32[3,64,128]{2,1,0:T(8,128)S(1)}, f32[3,64,128]{2,1,0:T(8,128)S(1)}, u32[]{:S(2)}, u32[]{:S(2)}) %collective-permute-start.5) | collective-permute-done | bytes 98336 | tf_op jit(solution)/shard_map/ppermute | solution.py:256
  17.5 1.2 %collective-permute-start.6 = (f32[3,64,128]{2,1,0:T(8,128)S(1)}, f32[3,64,128]{2,1,0:T(8,128)S(1)}, u32[]{:S(2)}, u32[]{:S(2)}) collective-permute-start(f32[3,64,128]{2,1,0:T(8,128)S(1)} %collective-permute-done.5.refs_4_), channel_id=1, source_target_pairs={{0,16},{4,12},{8,24},{12,4},{16,0},{20,28},{24,8},{28,20},{1,17},{... | collective-permute-start | bytes 294920 | tf_op jit(solution)/shard_map/ppermute | solution.py:314
  18.7 1.2 %collective-permute-start.7 = (f32[3,64,128]{2,1,0:T(8,128)S(1)}, f32[3,64,128]{2,1,0:T(8,128)S(1)}, u32[]{:S(2)}, u32[]{:S(2)}) collective-permute-start(f32[3,64,128]{2,1,0:T(8,128)S(1)} %collective-permute-done.5.refs_4_), channel_id=1, source_target_pairs={{0,8},{4,20},{8,0},{12,28},{16,24},{20,4},{24,16},{28,12},{1,9},{5... | collective-permute-start | bytes 294920 | tf_op jit(solution)/shard_map/ppermute | solution.py:314
  19.9 0.0 collective-permute-done.1.refs_0_
  19.9 1.4 %collective-permute-start.9 = (f32[3,64,128]{2,1,0:T(8,128)S(1)}, f32[3,64,128]{2,1,0:T(8,128)S(1)}, u32[]{:S(2)}, u32[]{:S(2)}) collective-permute-start(f32[3,64,128]{2,1,0:T(8,128)S(1)} %collective-permute-done.5.refs_4_), channel_id=1, source_target_pairs={{0,4},{4,0},{8,12},{12,8},{16,20},{20,16},{24,28},{28,24},{1,5},{5... | collective-permute-start | bytes 294920 | tf_op jit(solution)/shard_map/ppermute | solution.py:253
  21.3 0.8 %collective-permute-start.8 = (f32[3,64,128]{2,1,0:T(8,128)S(1)}, f32[3,64,128]{2,1,0:T(8,128)S(1)}, u32[]{:S(2)}, u32[]{:S(2)}) collective-permute-start(f32[3,64,128]{2,1,0:T(8,128)S(1)} %collective-permute-done.6.refs_5_), channel_id=1, source_target_pairs={{0,8},{4,20},{8,0},{12,28},{16,24},{20,4},{24,16},{28,12},{1,9},{5... | collective-permute-start | bytes 294920 | tf_op jit(solution)/shard_map/ppermute | solution.py:314
  22.2 1.2 %collective-permute-done.7.refs_6_ = f32[3,64,128]{2,1,0:T(8,128)S(1)} collective-permute-done((f32[3,64,128]{2,1,0:T(8,128)S(1)}, f32[3,64,128]{2,1,0:T(8,128)S(1)}, u32[]{:S(2)}, u32[]{:S(2)}) %collective-permute-start.7) | collective-permute-done | bytes 98336 | tf_op jit(solution)/shard_map/ppermute | solution.py:314
  23.4 1.1 %collective-permute-start.10 = (f32[3,64,128]{2,1,0:T(8,128)S(1)}, f32[3,64,128]{2,1,0:T(8,128)S(1)}, u32[]{:S(2)}, u32[]{:S(2)}) collective-permute-start(f32[3,64,128]{2,1,0:T(8,128)S(1)} %collective-permute-done.6.refs_5_), channel_id=1, source_target_pairs={{0,4},{4,0},{8,12},{12,8},{16,20},{20,16},{24,28},{28,24},{1,5},{5... | collective-permute-start | bytes 294920 | tf_op jit(solution)/shard_map/ppermute | solution.py:253
  24.5 0.0 collective-permute-done.9.refs_8_
  24.5 1.2 %collective-permute-start.2 = (f32[3,128,128]{2,1,0:T(8,128)S(1)}, f32[3,128,128]{2,1,0:T(8,128)S(1)}, u32[]{:S(2)}, u32[]{:S(2)}) collective-permute-start(f32[3,128,128]{2,1,0:T(8,128)S(1)} %collective-permute-done.1.refs_0_), channel_id=1, source_target_pairs={{0,8},{4,20},{8,0},{12,28},{16,24},{20,4},{24,16},{28,12},{1,9},{5... | collective-permute-start | bytes 589832 | tf_op jit(solution)/shard_map/ppermute | solution.py:314
  25.7 0.0 collective-permute-done.13.refs_12_
  25.7 0.3 collective-permute-start.14
  25.9 2.6 %collective-permute-start.3 = (f32[3,128,128]{2,1,0:T(8,128)S(1)}, f32[3,128,128]{2,1,0:T(8,128)S(1)}, u32[]{:S(2)}, u32[]{:S(2)}) collective-permute-start(f32[3,128,128]{2,1,0:T(8,128)S(1)} %collective-permute-done.1.refs_0_), channel_id=1, source_target_pairs={{0,4},{4,0},{8,12},{12,8},{16,20},{20,16},{24,28},{28,24},{1,5},{5... | collective-permute-start | bytes 589832 | tf_op jit(solution)/shard_map/ppermute | solution.py:253
  28.5 0.0 collective-permute-start.11
  28.5 1.3 %collective-permute-done.11.refs_10_ = f32[3,64,128]{2,1,0:T(8,128)S(1)} collective-permute-done((f32[3,64,128]{2,1,0:T(8,128)S(1)}, f32[3,64,128]{2,1,0:T(8,128)S(1)}, u32[]{:S(2)}, u32[]{:S(2)}) %collective-permute-start.11) | collective-permute-done | bytes 98336 | tf_op jit(solution)/shard_map/ppermute | solution.py:253
  29.8 0.3 collective-permute-start.15
  30.1 0.5 collective-permute-start.4
  30.6 0.8 %collective-permute-done.14.refs_13_ = f32[3,128,128]{2,1,0:T(8,128)S(1)} collective-permute-done((f32[3,128,128]{2,1,0:T(8,128)S(1)}, f32[3,128,128]{2,1,0:T(8,128)S(1)}, u32[]{:S(2)}, u32[]{:S(2)}) %collective-permute-start.14) | collective-permute-done | bytes 196640 | tf_op jit(solution)/shard_map/ppermute | solution.py:314
  31.4 1.3 %collective-permute-start.16 = (f32[3,128,128]{2,1,0:T(8,128)S(1)}, f32[3,128,128]{2,1,0:T(8,128)S(1)}, u32[]{:S(2)}, u32[]{:S(2)}) collective-permute-start(f32[3,128,128]{2,1,0:T(8,128)S(1)} %collective-permute-done.14.refs_13_), channel_id=1, source_target_pairs={{0,4},{4,0},{8,12},{12,8},{16,20},{20,16},{24,28},{28,24},{1,5},{5... | collective-permute-start | bytes 589832 | tf_op jit(solution)/shard_map/ppermute | solution.py:253
  32.7 2.2 %shard_map.82 = s32[4,4,128]{2,1,0:T(4,128)S(1)} custom-call(s32[8,32]{1,0:T(8,128)} %cols.1, s32[8,32]{1,0:T(8,128)} %owner.1, s32[8,32]{1,0:T(8,128)} %slot.1, s32[8]{0:T(128)} %number.1), custom_call_target="tpu_custom_call" | custom-call | flops 100000000 | bytes 16384 | tf_op jit(solution)/shard_map/pallas_call | solution.py:215
  34.9 0.0 collective-permute-done.3.refs_2_
  34.9 0.1 collective-permute-start.12
  35.0 1.3 %collective-permute-done.12.refs_11_ = f32[3,64,128]{2,1,0:T(8,128)S(1)} collective-permute-done((f32[3,64,128]{2,1,0:T(8,128)S(1)}, f32[3,64,128]{2,1,0:T(8,128)S(1)}, u32[]{:S(2)}, u32[]{:S(2)}) %collective-permute-start.12) | collective-permute-done | bytes 98336 | tf_op jit(solution)/shard_map/ppermute | solution.py:253
  36.3 1.7 %collective-permute-start.20 = (s32[4,128]{1,0:T(4,128)S(1)}, s32[4,128]{1,0:T(4,128)S(1)}, u32[]{:S(2)}, u32[]{:S(2)}) collective-permute-start(s32[4,128]{1,0:T(4,128)S(1)} %get-tuple-element.9), channel_id=1, source_target_pairs={{0,24},{4,28},{8,16},{12,20},{16,8},{20,12},{24,0},{28,4},{1,25},{... | collective-permute-start | bytes 6152 | tf_op jit(solution)/shard_map/ppermute | solution.py:302
  38.0 2.4 %shard_map.84.own_ref = f32[12,128,128]{2,1,0:T(8,128)S(1)} custom-call(s32[8]{0:T(128)S(1)} %stack.32.place, f32[12,128,128]{2,1,0:T(8,128)} %bitcast.19, f32[12,128,128]{2,1,0:T(8,128)} %r_ref.3), custom_call_target="tpu_custom_call" | custom-call | flops 150994944 | bytes 1572864 | tf_op jit(solution)/shard_map/pallas_call | solution.py:215
  40.5 1.1 %shard_map.86.proj_ref = bf16[49,128,256]{2,1,0:T(8,128)(2,1)S(1)} custom-call(s32[8]{0:T(128)S(1)} %stack.32.place, f32[12,128,128]{2,1,0:T(8,128)S(1)} %shard_map.84.own_ref, f32[3,128,128]{2,1,0:T(8,128)S(1)} %collective-permute-done.1.refs_0_, f32[3,128,128]{2,1,0:T(8,128)S(1)} %collective-permute-done.2.refs_1_, ...), custom_call_target="tpu_custom_call" | custom-call | flops 1000000 | bytes 4718592 | tf_op jit(solution)/shard_map/pallas_call | solution.py:215
  41.5 3.6 %shard_map.83.tiles_ref = bf16[128,128,256]{2,1,0:T(8,128)(2,1)S(1)} custom-call(s32[1]{0:T(128)} %bitcast.1.core, f32[64,128,128]{2,1,0:T(8,128)} %own_ref.1, f32[64,128,128]{2,1,0:T(8,128)} %collective-permute-done.other_ref), custom_call_target="tpu_custom_call" | custom-call | flops 16777216 | bytes 16777216 | tf_op jit(solution)/shard_map/pallas_call | solution.py:215
  45.2 2.0 %shard_map.90 = f32[8,128,128]{2,1,0:T(8,128)S(1)} custom-call(s32[4,128]{1,0:T(4,128)S(1)} %collective-permute-done.20.lists, bf16[128,128,256]{2,1,0:T(8,128)(2,1)S(1)} %shard_map.83.tiles_ref, bf16[49,128,256]{2,1,0:T(8,128)(2,1)S(1)} %shard_map.86.proj_ref), custom_call_target="tpu_custom_call" | custom-call | flops 1073741824 | bytes 4194304 | tf_op jit(solution)/shard_map/pallas_call | solution.py:215
  47.2 0.6 collective-permute-start.21
  47.8 0.9 %collective-permute-start.17 = (s32[4,128]{1,0:T(4,128)S(1)}, s32[4,128]{1,0:T(4,128)S(1)}, u32[]{:S(2)}, u32[]{:S(2)}) collective-permute-start(s32[4,128]{1,0:T(4,128)S(1)} %get-tuple-element.11), channel_id=1, source_target_pairs={{0,8},{4,20},{8,0},{12,28},{16,24},{20,4},{24,16},{28,12},{1,9},{5... | collective-permute-start | bytes 6152 | tf_op jit(solution)/shard_map/ppermute | solution.py:302
  48.7 0.2 collective-permute-start.19
  48.9 6.7 %collective-permute-done.17.lists = s32[4,128]{1,0:T(4,128)S(1)} collective-permute-done((s32[4,128]{1,0:T(4,128)S(1)}, s32[4,128]{1,0:T(4,128)S(1)}, u32[]{:S(2)}, u32[]{:S(2)}) %collective-permute-start.17) | collective-permute-done | bytes 2080 | tf_op jit(solution)/shard_map/ppermute | solution.py:302
  55.6 1.4 %shard_map.88 = f32[8,128,128]{2,1,0:T(8,128)S(1)} custom-call(s32[4,128]{1,0:T(4,128)S(1)} %collective-permute-done.17.lists, bf16[128,128,256]{2,1,0:T(8,128)(2,1)S(1)} %shard_map.83.tiles_ref, bf16[49,128,256]{2,1,0:T(8,128)(2,1)S(1)} %shard_map.86.proj_ref), custom_call_target="tpu_custom_call" | custom-call | flops 1073741824 | bytes 4194304 | tf_op jit(solution)/shard_map/pallas_call | solution.py:215
  57.0 0.6 collective-permute-start.18
  57.6 2.3 %shard_map.89 = f32[8,128,128]{2,1,0:T(8,128)S(1)} custom-call(s32[4,128]{1,0:T(4,128)S(1)} %collective-permute-done.19.lists, bf16[128,128,256]{2,1,0:T(8,128)(2,1)S(1)} %shard_map.83.tiles_ref, bf16[49,128,256]{2,1,0:T(8,128)(2,1)S(1)} %shard_map.86.proj_ref), custom_call_target="tpu_custom_call" | custom-call | flops 1073741824 | bytes 4194304 | tf_op jit(solution)/shard_map/pallas_call | solution.py:215
  59.9 0.1 add.25
  60.0 0.1 collective-permute-start.22
  60.1 0.0 copy-start
  60.1 1.4 %shard_map.87.refs_0_ = f32[8,128,128]{2,1,0:T(8,128)S(1)} custom-call(s32[4,128]{1,0:T(4,128)S(1)} %get-tuple-element.12.lists, bf16[128,128,256]{2,1,0:T(8,128)(2,1)S(1)} %shard_map.83.tiles_ref, bf16[49,128,256]{2,1,0:T(8,128)(2,1)S(1)} %shard_map.86.proj_ref), custom_call_target="tpu_custom_call" | custom-call | flops 1073741824 | bytes 4194304 | tf_op jit(solution)/shard_map/pallas_call | solution.py:215
  61.4 3.9 %collective-permute-done.18.refs_1_ = f32[8,128,128]{2,1,0:T(8,128)S(1)} collective-permute-done((f32[8,128,128]{2,1,0:T(8,128)S(1)}, f32[8,128,128]{2,1,0:T(8,128)S(1)}, u32[]{:S(2)}, u32[]{:S(2)}) %collective-permute-start.18) | collective-permute-done | bytes 524320 | tf_op jit(solution)/shard_map/ppermute | solution.py:347
  65.4 8.0 %collective-permute-done.22.refs_2_ = f32[8,128,128]{2,1,0:T(8,128)S(1)} collective-permute-done((f32[8,128,128]{2,1,0:T(8,128)S(1)}, f32[8,128,128]{2,1,0:T(8,128)S(1)}, u32[]{:S(2)}, u32[]{:S(2)}) %collective-permute-start.22) | collective-permute-done | bytes 524320 | tf_op jit(solution)/shard_map/ppermute | solution.py:347
  73.4 1.2 %shard_map.91 = f32[8,128,128]{2,1,0:T(8,128)} custom-call(f32[8,128,128]{2,1,0:T(8,128)S(1)} %copy-done, f32[8,128,128]{2,1,0:T(8,128)S(1)} %shard_map.87.refs_0_, f32[8,128,128]{2,1,0:T(8,128)S(1)} %collective-permute-done.18.refs_1_, f32[8,128,128]{2,1,0:T(8,128)S(1)} %collective-permute-done.22.refs_2_), custom_call_target="tpu_custom_call" | custom-call | flops 100663296 | bytes 2097152 | tf_op jit(solution)/shard_map/pallas_call | solution.py:215
  (13 shorter events, 0.0 us)
Async XLA Ops:
  0.0 41.5 %collective-permute-start = (f32[64,128,128]{2,1,0:T(8,128)}, f32[64,128,128]{2,1,0:T(8,128)}, u32[]{:S(2)}, u32[]{:S(2)}) collective-permute-start(f32[64,128,128]{2,1,0:T(8,128)} %own_ref.1), channel_id=1, source_target_pairs={{0,4},{4,0},{8,12},{12,8},{16,20},{20,16},{24,28},{28,24},{1,5},{5... | collective-permute-start | bytes 12582920 | tf_op jit(solution)/shard_map/ppermute | solution.py:253
  2.6 17.3 %collective-permute-start.1 = (f32[3,128,128]{2,1,0:T(8,128)S(1)}, f32[3,128,128]{2,1,0:T(8,128)S(1)}, u32[]{:S(2)}, u32[]{:S(2)}) collective-permute-start(f32[3,128,128]{2,1,0:T(8,128)S(1)} %get-tuple-element.7), channel_id=1, source_target_pairs={{0,1},{1,2},{2,3},{3,0},{4,5},{5,6},{6,7},{7,4},{8,9},{9,10},{10,1... | collective-permute-start | bytes 589832 | tf_op jit(solution)/shard_map/ppermute | solution.py:256
  2.7 14.8 %collective-permute-start.5 = (f32[3,64,128]{2,1,0:T(8,128)S(1)}, f32[3,64,128]{2,1,0:T(8,128)S(1)}, u32[]{:S(2)}, u32[]{:S(2)}) collective-permute-start(f32[3,64,128]{2,1,0:T(8,128)S(1)} %get-tuple-element.8), channel_id=1, source_target_pairs={{0,2},{1,3},{2,0},{3,1},{4,6},{5,7},{6,4},{7,5},{8,10},{9,11},{10,... | collective-permute-start | bytes 294920 | tf_op jit(solution)/shard_map/ppermute | solution.py:256
  4.0 21.6 %collective-permute-start.13 = (f32[3,128,128]{2,1,0:T(8,128)S(1)}, f32[3,128,128]{2,1,0:T(8,128)S(1)}, u32[]{:S(2)}, u32[]{:S(2)}) collective-permute-start(f32[3,128,128]{2,1,0:T(8,128)S(1)} %get-tuple-element.7), channel_id=1, source_target_pairs={{0,3},{1,0},{2,1},{3,2},{4,7},{5,4},{6,5},{7,6},{8,11},{9,8},{10,9... | collective-permute-start | bytes 589832 | tf_op jit(solution)/shard_map/ppermute | solution.py:256
  17.5 3.9 %collective-permute-start.6 = (f32[3,64,128]{2,1,0:T(8,128)S(1)}, f32[3,64,128]{2,1,0:T(8,128)S(1)}, u32[]{:S(2)}, u32[]{:S(2)}) collective-permute-start(f32[3,64,128]{2,1,0:T(8,128)S(1)} %collective-permute-done.5.refs_4_), channel_id=1, source_target_pairs={{0,16},{4,12},{8,24},{12,4},{16,0},{20,28},{24,8},{28,20},{1,17},{... | collective-permute-start | bytes 294920 | tf_op jit(solution)/shard_map/ppermute | solution.py:314
  18.7 4.7 %collective-permute-start.7 = (f32[3,64,128]{2,1,0:T(8,128)S(1)}, f32[3,64,128]{2,1,0:T(8,128)S(1)}, u32[]{:S(2)}, u32[]{:S(2)}) collective-permute-start(f32[3,64,128]{2,1,0:T(8,128)S(1)} %collective-permute-done.5.refs_4_), channel_id=1, source_target_pairs={{0,8},{4,20},{8,0},{12,28},{16,24},{20,4},{24,16},{28,12},{1,9},{5... | collective-permute-start | bytes 294920 | tf_op jit(solution)/shard_map/ppermute | solution.py:314
  19.9 4.5 %collective-permute-start.9 = (f32[3,64,128]{2,1,0:T(8,128)S(1)}, f32[3,64,128]{2,1,0:T(8,128)S(1)}, u32[]{:S(2)}, u32[]{:S(2)}) collective-permute-start(f32[3,64,128]{2,1,0:T(8,128)S(1)} %collective-permute-done.5.refs_4_), channel_id=1, source_target_pairs={{0,4},{4,0},{8,12},{12,8},{16,20},{20,16},{24,28},{28,24},{1,5},{5... | collective-permute-start | bytes 294920 | tf_op jit(solution)/shard_map/ppermute | solution.py:253
  21.3 4.6 %collective-permute-start.8 = (f32[3,64,128]{2,1,0:T(8,128)S(1)}, f32[3,64,128]{2,1,0:T(8,128)S(1)}, u32[]{:S(2)}, u32[]{:S(2)}) collective-permute-start(f32[3,64,128]{2,1,0:T(8,128)S(1)} %collective-permute-done.6.refs_5_), channel_id=1, source_target_pairs={{0,8},{4,20},{8,0},{12,28},{16,24},{20,4},{24,16},{28,12},{1,9},{5... | collective-permute-start | bytes 294920 | tf_op jit(solution)/shard_map/ppermute | solution.py:314
  23.4 5.1 %collective-permute-start.10 = (f32[3,64,128]{2,1,0:T(8,128)S(1)}, f32[3,64,128]{2,1,0:T(8,128)S(1)}, u32[]{:S(2)}, u32[]{:S(2)}) collective-permute-start(f32[3,64,128]{2,1,0:T(8,128)S(1)} %collective-permute-done.6.refs_5_), channel_id=1, source_target_pairs={{0,4},{4,0},{8,12},{12,8},{16,20},{20,16},{24,28},{28,24},{1,5},{5... | collective-permute-start | bytes 294920 | tf_op jit(solution)/shard_map/ppermute | solution.py:253
  24.5 5.6 %collective-permute-start.2 = (f32[3,128,128]{2,1,0:T(8,128)S(1)}, f32[3,128,128]{2,1,0:T(8,128)S(1)}, u32[]{:S(2)}, u32[]{:S(2)}) collective-permute-start(f32[3,128,128]{2,1,0:T(8,128)S(1)} %collective-permute-done.1.refs_0_), channel_id=1, source_target_pairs={{0,8},{4,20},{8,0},{12,28},{16,24},{20,4},{24,16},{28,12},{1,9},{5... | collective-permute-start | bytes 589832 | tf_op jit(solution)/shard_map/ppermute | solution.py:314
  25.7 5.7 %collective-permute-start.14 = (f32[3,128,128]{2,1,0:T(8,128)S(1)}, f32[3,128,128]{2,1,0:T(8,128)S(1)}, u32[]{:S(2)}, u32[]{:S(2)}) collective-permute-start(f32[3,128,128]{2,1,0:T(8,128)S(1)} %collective-permute-done.13.refs_12_), channel_id=1, source_target_pairs={{0,8},{4,20},{8,0},{12,28},{16,24},{20,4},{24,16},{28,12},{1,9},{5... | collective-permute-start | bytes 589832 | tf_op jit(solution)/shard_map/ppermute | solution.py:314
  25.9 9.0 %collective-permute-start.3 = (f32[3,128,128]{2,1,0:T(8,128)S(1)}, f32[3,128,128]{2,1,0:T(8,128)S(1)}, u32[]{:S(2)}, u32[]{:S(2)}) collective-permute-start(f32[3,128,128]{2,1,0:T(8,128)S(1)} %collective-permute-done.1.refs_0_), channel_id=1, source_target_pairs={{0,4},{4,0},{8,12},{12,8},{16,20},{20,16},{24,28},{28,24},{1,5},{5... | collective-permute-start | bytes 589832 | tf_op jit(solution)/shard_map/ppermute | solution.py:253
  28.5 1.3 %collective-permute-start.11 = (f32[3,64,128]{2,1,0:T(8,128)S(1)}, f32[3,64,128]{2,1,0:T(8,128)S(1)}, u32[]{:S(2)}, u32[]{:S(2)}) collective-permute-start(f32[3,64,128]{2,1,0:T(8,128)S(1)} %collective-permute-done.7.refs_6_), channel_id=1, source_target_pairs={{0,4},{4,0},{8,12},{12,8},{16,20},{20,16},{24,28},{28,24},{1,5},{5... | collective-permute-start | bytes 294920 | tf_op jit(solution)/shard_map/ppermute | solution.py:253
  29.8 10.6 %collective-permute-start.15 = (f32[3,128,128]{2,1,0:T(8,128)S(1)}, f32[3,128,128]{2,1,0:T(8,128)S(1)}, u32[]{:S(2)}, u32[]{:S(2)}) collective-permute-start(f32[3,128,128]{2,1,0:T(8,128)S(1)} %collective-permute-done.13.refs_12_), channel_id=1, source_target_pairs={{0,4},{4,0},{8,12},{12,8},{16,20},{20,16},{24,28},{28,24},{1,5},{5... | collective-permute-start | bytes 589832 | tf_op jit(solution)/shard_map/ppermute | solution.py:253
  30.1 10.4 %collective-permute-start.4 = (f32[3,128,128]{2,1,0:T(8,128)S(1)}, f32[3,128,128]{2,1,0:T(8,128)S(1)}, u32[]{:S(2)}, u32[]{:S(2)}) collective-permute-start(f32[3,128,128]{2,1,0:T(8,128)S(1)} %collective-permute-done.2.refs_1_), channel_id=1, source_target_pairs={{0,4},{4,0},{8,12},{12,8},{16,20},{20,16},{24,28},{28,24},{1,5},{5... | collective-permute-start | bytes 589832 | tf_op jit(solution)/shard_map/ppermute | solution.py:253
  31.4 9.1 %collective-permute-start.16 = (f32[3,128,128]{2,1,0:T(8,128)S(1)}, f32[3,128,128]{2,1,0:T(8,128)S(1)}, u32[]{:S(2)}, u32[]{:S(2)}) collective-permute-start(f32[3,128,128]{2,1,0:T(8,128)S(1)} %collective-permute-done.14.refs_13_), channel_id=1, source_target_pairs={{0,4},{4,0},{8,12},{12,8},{16,20},{20,16},{24,28},{28,24},{1,5},{5... | collective-permute-start | bytes 589832 | tf_op jit(solution)/shard_map/ppermute | solution.py:253
  34.9 1.4 %collective-permute-start.12 = (f32[3,64,128]{2,1,0:T(8,128)S(1)}, f32[3,64,128]{2,1,0:T(8,128)S(1)}, u32[]{:S(2)}, u32[]{:S(2)}) collective-permute-start(f32[3,64,128]{2,1,0:T(8,128)S(1)} %collective-permute-done.8.refs_7_), channel_id=1, source_target_pairs={{0,4},{4,0},{8,12},{12,8},{16,20},{20,16},{24,28},{28,24},{1,5},{5... | collective-permute-start | bytes 294920 | tf_op jit(solution)/shard_map/ppermute | solution.py:253
  36.3 8.9 %collective-permute-start.20 = (s32[4,128]{1,0:T(4,128)S(1)}, s32[4,128]{1,0:T(4,128)S(1)}, u32[]{:S(2)}, u32[]{:S(2)}) collective-permute-start(s32[4,128]{1,0:T(4,128)S(1)} %get-tuple-element.9), channel_id=1, source_target_pairs={{0,24},{4,28},{8,16},{12,20},{16,8},{20,12},{24,0},{28,4},{1,25},{... | collective-permute-start | bytes 6152 | tf_op jit(solution)/shard_map/ppermute | solution.py:302
  47.2 12.7 %collective-permute-start.21 = (f32[8,128,128]{2,1,0:T(8,128)S(1)}, f32[8,128,128]{2,1,0:T(8,128)S(1)}, u32[]{:S(2)}, u32[]{:S(2)}) collective-permute-start(f32[8,128,128]{2,1,0:T(8,128)S(1)} %shard_map.90), channel_id=1, source_target_pairs={{0,8},{4,20},{8,0},{12,28},{16,24},{20,4},{24,16},{28,12},{1,9},{5... | collective-permute-start | bytes 1572872 | tf_op jit(solution)/shard_map/ppermute | solution.py:347
  47.8 7.8 %collective-permute-start.17 = (s32[4,128]{1,0:T(4,128)S(1)}, s32[4,128]{1,0:T(4,128)S(1)}, u32[]{:S(2)}, u32[]{:S(2)}) collective-permute-start(s32[4,128]{1,0:T(4,128)S(1)} %get-tuple-element.11), channel_id=1, source_target_pairs={{0,8},{4,20},{8,0},{12,28},{16,24},{20,4},{24,16},{28,12},{1,9},{5... | collective-permute-start | bytes 6152 | tf_op jit(solution)/shard_map/ppermute | solution.py:302
  48.7 8.9 %collective-permute-start.19 = (s32[4,128]{1,0:T(4,128)S(1)}, s32[4,128]{1,0:T(4,128)S(1)}, u32[]{:S(2)}, u32[]{:S(2)}) collective-permute-start(s32[4,128]{1,0:T(4,128)S(1)} %get-tuple-element.10), channel_id=1, source_target_pairs={{0,16},{4,12},{8,24},{12,4},{16,0},{20,28},{24,8},{28,20},{1,17},{... | collective-permute-start | bytes 6152 | tf_op jit(solution)/shard_map/ppermute | solution.py:302
  57.0 8.4 %collective-permute-start.18 = (f32[8,128,128]{2,1,0:T(8,128)S(1)}, f32[8,128,128]{2,1,0:T(8,128)S(1)}, u32[]{:S(2)}, u32[]{:S(2)}) collective-permute-start(f32[8,128,128]{2,1,0:T(8,128)S(1)} %shard_map.88), channel_id=1, source_target_pairs={{0,8},{4,20},{8,0},{12,28},{16,24},{20,4},{24,16},{28,12},{1,9},{5... | collective-permute-start | bytes 1572872 | tf_op jit(solution)/shard_map/ppermute | solution.py:347
  60.0 13.4 %collective-permute-start.22 = (f32[8,128,128]{2,1,0:T(8,128)S(1)}, f32[8,128,128]{2,1,0:T(8,128)S(1)}, u32[]{:S(2)}, u32[]{:S(2)}) collective-permute-start(f32[8,128,128]{2,1,0:T(8,128)S(1)} %add.25), channel_id=1, source_target_pairs={{0,16},{4,12},{8,24},{12,4},{16,0},{20,28},{24,8},{28,20},{1,17},{... | collective-permute-start | bytes 1572872 | tf_op jit(solution)/shard_map/ppermute | solution.py:347
  60.1 13.3 %copy-start = (f32[8,128,128]{2,1,0:T(8,128)S(1)}, f32[8,128,128]{2,1,0:T(8,128)}, u32[]{:S(2)}) copy-start(f32[8,128,128]{2,1,0:T(8,128)} %left_ref.1) | copy-start | bytes 1572868

commit v4 on v3

--- a/solution.py
+++ b/solution.py
@@ -67,7 +67,7 @@
 
 def list_kernel(chips, held, columns, cols, owner, slot, number, out_ref, words, counts, sems):
     blocks, listed = cols.shape
-    span = out_ref.shape[2]
+    span = out_ref.shape[1]
     copies = [
         pltpu.make_async_copy(ref, words.at[i], sems.at[i])
         for i, ref in enumerate((cols, owner, slot))
@@ -111,7 +111,7 @@
         part = total[:, c * span : (c + 1) * span]
         number = jnp.broadcast_to(offset[c : c + 1], (8, span))
         part = jnp.where(row == 0, number, jnp.where(row == 2, part + columns, part))
-        out_ref[c] = part[:4].astype(I32)
+        out_ref[8 * c : 8 * c + 8] = part
 
 
 def tile_kernel(core, own_ref, other_ref, out_ref, buf, sems):
@@ -142,35 +142,45 @@
         lax.fori_loop(0, step, one, 0, unroll=4)
 
 
-def gather_kernel(planes, place, own_ref, *refs):
-    pieces, out_ref = refs[:-1], refs[-1]
+def gather_kernel(planes, holders, place, own_ref, *refs):
+    chips = len(holders)
+    pieces, (out_ref, *table_refs) = refs[: -1 - chips], refs[-1 - chips :]
+    for holder, table in zip(holders, table_refs):
+        base = pieces[holder].shape[0] - 8 * chips
+        table[...] = pieces[holder][pl.ds(pl.multiple_of(base + 8 * place[8], 8), 8)].astype(I32)
     count, _, width = own_ref.shape
     quarter = count // 4
     blk = place[1]
     out_ref[planes * count] = jnp.zeros_like(out_ref[planes * count])
 
-    def put(src, start, first_row):
-        rows = pl.ds(first_row, src.shape[1])
+    def put(src, start):
         for i in range(src.shape[0]):
             hi, lo = split(src[i])
+            out_ref[start + i, :, :width] = hi
+            out_ref[start + i, :, width:] = lo
+
+    def put_rows(src, start, half):
+        n = out_ref.shape[1] // 2
+        rows = pl.ds(pl.multiple_of(half * n, n), n)
+        for i in range(quarter):
+            hi, lo = split(src[i * n : (i + 1) * n])
             out_ref[start + i, rows, :width] = hi
             out_ref[start + i, rows, width:] = lo
 
-    put(own_ref, blk * count, 0)
+    put(own_ref, blk * count)
     at = 0
     for k in range(1, planes):
         start = lax.rem(blk - k + planes, planes) * count
         if k != planes // 2:
             for p in range(4):
-                put(pieces[at + p], start + place[2 + p] * quarter, 0)
+                put(pieces[at + p], start + place[2 + p] * quarter)
             at += 4
             continue
         for p in range(4):
             half = place[6 + p // 2]
-            rows = pieces[at].shape[1]
-            for side in range(2):
-                row = pl.multiple_of((half if side == 0 else 1 - half) * rows, rows)
-                put(pieces[at + 2 * p + side], start + place[2 + p] * quarter, row)
+            to = start + place[2 + p] * quarter
+            put_rows(pieces[at + 2 * p], to, half)
+            put_rows(pieces[at + 2 * p + 1], to, 1 - half)
         at += 8
 
 
@@ -259,7 +269,7 @@
     theirs = jnp.where(core == 0, 2 + b1, b0)
     row_half = jnp.where(core == 0, b1, b0)
     their_half = jnp.where(core == 0, b0, b1)
-    place = jnp.stack([mine, blk, mine, mine ^ 1, theirs, theirs ^ 1, row_half, their_half]).astype(I32)
+    place = jnp.stack([mine, blk, mine, mine ^ 1, theirs, theirs ^ 1, row_half, their_half, chip]).astype(I32)
 
     v = vectors.reshape(count, fine, vecs)
     v, right = in_hbm(v), in_hbm(right)
@@ -286,7 +296,7 @@
     span = pl.cdiv(cap, 128) * 128
     lists = call(
         functools.partial(list_kernel, chips, held, planes * count), 0, [HBM] * 4,
-        jax.ShapeDtypeStruct((chips, 4, span), I32),
+        jax.ShapeDtypeStruct((chips * 8, span), F32),
         [
             pltpu.VMEM((3, blocks, listed), I32),
             pltpu.SMEM((blocks,), I32),
@@ -295,18 +305,12 @@
         (in_hbm(pair_cols), in_hbm(pair_owner), in_hbm(pair_slot), in_hbm(pair_counts)),
         cost(10**8, 16384), 8 * MIB,
     )
-    tables = {}
-    for m in range(chips):
-        to_chip = chip ^ jnp.where(core == 0, physical(m, 0), physical(m, 1))
-        chosen = lax.dynamic_index_in_dim(lists, to_chip, 0, keepdims=False)
-        tables[m] = chosen if m == 0 else lax.ppermute(chosen, "rows", across(m))
-
     own = project(count, jax.ShapeDtypeStruct((count, coarse, vecs), F32))
     packed = call(
-        tile_kernel, 1, [HBM, HBM],
+        tile_kernel, 1, [HBM, pl.BlockSpec(memory_space=pl.ANY)],
         jax.ShapeDtypeStruct((2 * held, coarse, 2 * coarse), BF16),
         [pltpu.VMEM((held // 4, 8, coarse, coarse), F32), pltpu.SemaphoreType.DMA((held // 4,))],
-        (core.reshape(1).astype(I32), in_hbm(tiles), in_hbm(other_tiles)),
+        (core.reshape(1).astype(I32), in_hbm(tiles), other_tiles),
         cost(held * 65536 * 4, held * 65536 * 4), 2 * held * 65536 + 4 * MIB,
     )
 
@@ -317,17 +321,30 @@
     for k in range(1, planes):
         z = arrived[k]
         if k == middle:
+            z = jnp.concatenate([z.reshape(-1, vecs), lists], axis=0)
             rest = spread(z, 2)
             x, x_rest = spread(z), spread(rest)
+            ridden = {1: x, 2: rest, 3: x_rest}
             pieces += [z, rest, x, x_rest, swap(z), swap(rest)]
             pieces += [swap(x), swap(x_rest)]
         else:
             x = spread(z)
             pieces += [z, x, swap(z), swap(x)]
-    proj = call(
-        functools.partial(gather_kernel, planes), 1, [VMEM] * (1 + len(pieces)),
-        jax.ShapeDtypeStruct((planes * count + 1, coarse, 2 * vecs), BF16),
+
+    holders = [len(pieces)] + [next(i for i, p in enumerate(pieces) if p is ridden[m]) for m in (1, 2, 3)]
+    pieces += [lists]
+    from_chip = [lists] + [ridden[m][-8 * chips :] for m in (1, 2, 3)]
+    for bit in (1 << j for j in range(2, chips.bit_length() - 1)):
+        for m in range(bit):
+            from_chip.append(lax.ppermute(from_chip[m], "rows", across(bit)))
+            holders.append(len(pieces))
+            pieces.append(from_chip[-1])
+    proj, *tables = call(
+        functools.partial(gather_kernel, planes, holders), 1, [VMEM] * (1 + len(pieces)),
+        [jax.ShapeDtypeStruct((planes * count + 1, coarse, 2 * vecs), BF16)]
+        + [jax.ShapeDtypeStruct((8, span), I32)] * chips,
         [], (place, own, *pieces), cost(10**6, 3 * planes * count * 32768), 16 * MIB,
+        out_spec=[VMEM] * (1 + chips),
     )
 
     total = {

time: 74.7 us -> 62.2 us (0.83)
  the two profiles are of different devices: /device:TPU:25 before, /device:TPU:29 now
where the time goes in v4:
time: 62.2 us; the launch traced here: 62 us
  waiting for transfers between devices  26.6 us (43%)
  Pallas kernels  19.5 us (31%)
  starting transfers between devices  15.6 us (25%)
    pallas_call x10, Pallas kernels, call(): pl.pallas_call(kernel, out_shape=out, grid_spec=pltpu.PrefetchScalarGridS...  19.5 us
    ppermute x3, waiting for transfers between devices, work(): total[m ^ bit].append(lax.ppermute(value, 'rows', across(bit)))  13.6 us
    ppermute x9, starting transfers between devices, swap(): return lax.ppermute(x, 'rows', [(r, r ^ 1) for r in range(rows)])  7.36 us
    ppermute x5, waiting for transfers between devices, spread(): return lax.ppermute(x, 'rows', across(mask))  6.55 us
    ppermute x3, waiting for transfers between devices, turn(): lax.ppermute(x, 'blk', [(b, (b + k) % planes) for b in range(planes)])  6.42 us
    ppermute x3, starting transfers between devices, turn(): lax.ppermute(x, 'blk', [(b, (b + k) % planes) for b in range(planes)])  3.39 us
    ppermute x5, starting transfers between devices, spread(): return lax.ppermute(x, 'rows', across(mask))  3.19 us
    ppermute x3, starting transfers between devices, work(): total[m ^ bit].append(lax.ppermute(value, 'rows', across(bit)))  1.66 us
  transfers between devices with their start and end apart: 20, of which 6 were waited for; matrix products, arithmetic and copies ran while one was open for 0% of the time, Pallas kernels for 20%

profile of v4, /device:TPU:29, one launch (start us, length us, event | category | flops | bytes accessed | tf_op | source)
XLA Modules:
  0.0 62.0 jit_solution(9719624391655130159)
XLA Ops:
  0.0 0.7 %collective-permute-start.16 = (f32[64,128,128]{2,1,0:T(8,128)}, f32[64,128,128]{2,1,0:T(8,128)}, u32[]{:S(2)}, u32[]{:S(2)}) collective-permute-start(f32[64,128,128]{2,1,0:T(8,128)} %own_ref.1), channel_id=1, source_target_pairs={{0,4},{4,0},{8,12},{12,8},{16,20},{20,16},{24,28},{28,24},{1,5},{5... | collective-permute-start | bytes 12582920 | tf_op jit(solution)/shard_map/ppermute | solution.py:263
  0.7 0.1 stack.36.place
  0.8 1.9 %shard_map.83 = (f32[3,128,128]{2,1,0:T(8,128)S(1)}, f32[3,64,128]{2,1,0:T(8,128)S(1)}) custom-call(s32[9]{0:T(128)S(1)} %stack.36.place, f32[12,128,128]{2,1,0:T(8,128)} %bitcast.12, f32[12,128,128]{2,1,0:T(8,128)} %r_ref.3), custom_call_target="tpu_custom_call" | custom-call | flops 37748736 | bytes 393216 | tf_op jit(solution)/shard_map/pallas_call | solution.py:225
  2.6 0.1 collective-permute-start.4
  2.8 0.2 collective-permute-start.12
  2.9 3.1 %collective-permute-start = (f32[3,128,128]{2,1,0:T(8,128)S(1)}, f32[3,128,128]{2,1,0:T(8,128)S(1)}, u32[]{:S(2)}, u32[]{:S(2)}) collective-permute-start(f32[3,128,128]{2,1,0:T(8,128)S(1)} %get-tuple-element.12), channel_id=1, source_target_pairs={{0,1},{1,2},{2,3},{3,0},{4,5},{5,6},{6,7},{7,4},{8,9},{9,10},{10,1... | collective-permute-start | bytes 589832 | tf_op jit(solution)/shard_map/ppermute | solution.py:266
  6.0 2.2 %shard_map.84.refs_16_ = f32[32,128]{1,0:T(8,128)S(1)} custom-call(s32[8,32]{1,0:T(8,128)} %cols.1, s32[8,32]{1,0:T(8,128)} %owner.1, s32[8,32]{1,0:T(8,128)} %slot.1, s32[8]{0:T(128)} %number.1), custom_call_target="tpu_custom_call" | custom-call | flops 100000000 | bytes 16384 | tf_op jit(solution)/shard_map/pallas_call | solution.py:225
  8.2 6.4 %collective-permute-done.4 = f32[3,64,128]{2,1,0:T(8,128)S(1)} collective-permute-done((f32[3,64,128]{2,1,0:T(8,128)S(1)}, f32[3,64,128]{2,1,0:T(8,128)S(1)}, u32[]{:S(2)}, u32[]{:S(2)}) %collective-permute-start.4) | collective-permute-done | bytes 98336 | tf_op jit(solution)/shard_map/ppermute | solution.py:266
  14.6 0.3 collective-permute-start.6
  14.9 1.2 %collective-permute-start.5 = (f32[224,128]{1,0:T(8,128)S(1)}, f32[224,128]{1,0:T(8,128)S(1)}, u32[]{:S(2)}, u32[]{:S(2)}) collective-permute-start(f32[224,128]{1,0:T(8,128)S(1)} %pad_maximum_fusion.refs_4_), channel_id=1, source_target_pairs={{0,16},{4,12},{8,24},{12,4},{16,0},{20,28},{24,8},{28,20},{1,17},{... | collective-permute-start | bytes 344072 | tf_op jit(solution)/shard_map/ppermute | solution.py:318
  16.1 0.0 collective-permute-done.12.refs_12_
  16.1 1.1 %collective-permute-start.8 = (f32[224,128]{1,0:T(8,128)S(1)}, f32[224,128]{1,0:T(8,128)S(1)}, u32[]{:S(2)}, u32[]{:S(2)}) collective-permute-start(f32[224,128]{1,0:T(8,128)S(1)} %pad_maximum_fusion.refs_4_), channel_id=1, source_target_pairs={{0,4},{4,0},{8,12},{12,8},{16,20},{20,16},{24,28},{28,24},{1,5},{5... | collective-permute-start | bytes 344072 | tf_op jit(solution)/shard_map/ppermute | solution.py:263
  17.2 1.4 %collective-permute-done.6.refs_6_ = f32[224,128]{1,0:T(8,128)S(1)} collective-permute-done((f32[224,128]{1,0:T(8,128)S(1)}, f32[224,128]{1,0:T(8,128)S(1)}, u32[]{:S(2)}, u32[]{:S(2)}) %collective-permute-start.6) | collective-permute-done | bytes 114720 | tf_op jit(solution)/shard_map/ppermute | solution.py:318
  18.6 1.9 %collective-permute-start.10 = (f32[224,128]{1,0:T(8,128)S(1)}, f32[224,128]{1,0:T(8,128)S(1)}, u32[]{:S(2)}, u32[]{:S(2)}) collective-permute-start(f32[224,128]{1,0:T(8,128)S(1)} %collective-permute-done.6.refs_6_), channel_id=1, source_target_pairs={{0,4},{4,0},{8,12},{12,8},{16,20},{20,16},{24,28},{28,24},{1,5},{5... | collective-permute-start | bytes 344072 | tf_op jit(solution)/shard_map/ppermute | solution.py:263
  20.5 0.0 collective-permute-done.5.refs_5_
  20.5 1.0 %collective-permute-start.9 = (f32[224,128]{1,0:T(8,128)S(1)}, f32[224,128]{1,0:T(8,128)S(1)}, u32[]{:S(2)}, u32[]{:S(2)}) collective-permute-start(f32[224,128]{1,0:T(8,128)S(1)} %collective-permute-done.5.refs_5_), channel_id=1, source_target_pairs={{0,4},{4,0},{8,12},{12,8},{16,20},{20,16},{24,28},{28,24},{1,5},{5... | collective-permute-start | bytes 344072 | tf_op jit(solution)/shard_map/ppermute | solution.py:263
  21.5 0.0 collective-permute-done.refs_0_
  21.5 0.2 collective-permute-start.13
  21.7 0.0 collective-permute-done.8.refs_8_
  21.7 1.2 %collective-permute-start.1 = (f32[3,128,128]{2,1,0:T(8,128)S(1)}, f32[3,128,128]{2,1,0:T(8,128)S(1)}, u32[]{:S(2)}, u32[]{:S(2)}) collective-permute-start(f32[3,128,128]{2,1,0:T(8,128)S(1)} %collective-permute-done.refs_0_), channel_id=1, source_target_pairs={{0,8},{4,20},{8,0},{12,28},{16,24},{20,4},{24,16},{28,12},{1,9},{5... | collective-permute-start | bytes 589832 | tf_op jit(solution)/shard_map/ppermute | solution.py:318
  23.0 0.0 collective-permute-done.10.refs_10_
  23.0 0.2 collective-permute-start.7
  23.2 0.0 collective-permute-done.9.refs_9_
  23.2 1.3 %collective-permute-start.14 = (f32[3,128,128]{2,1,0:T(8,128)S(1)}, f32[3,128,128]{2,1,0:T(8,128)S(1)}, u32[]{:S(2)}, u32[]{:S(2)}) collective-permute-start(f32[3,128,128]{2,1,0:T(8,128)S(1)} %collective-permute-done.12.refs_12_), channel_id=1, source_target_pairs={{0,4},{4,0},{8,12},{12,8},{16,20},{20,16},{24,28},{28,24},{1,5},{5... | collective-permute-start | bytes 589832 | tf_op jit(solution)/shard_map/ppermute | solution.py:263
  24.5 5.1 %collective-permute-done.7.refs_7_ = f32[224,128]{1,0:T(8,128)S(1)} collective-permute-done((f32[224,128]{1,0:T(8,128)S(1)}, f32[224,128]{1,0:T(8,128)S(1)}, u32[]{:S(2)}, u32[]{:S(2)}) %collective-permute-start.7) | collective-permute-done | bytes 114720 | tf_op jit(solution)/shard_map/ppermute | solution.py:318
  29.6 0.9 %collective-permute-start.2 = (f32[3,128,128]{2,1,0:T(8,128)S(1)}, f32[3,128,128]{2,1,0:T(8,128)S(1)}, u32[]{:S(2)}, u32[]{:S(2)}) collective-permute-start(f32[3,128,128]{2,1,0:T(8,128)S(1)} %collective-permute-done.refs_0_), channel_id=1, source_target_pairs={{0,4},{4,0},{8,12},{12,8},{16,20},{20,16},{24,28},{28,24},{1,5},{5... | collective-permute-start | bytes 589832 | tf_op jit(solution)/shard_map/ppermute | solution.py:263
  30.5 0.0 collective-permute-start.15
  30.5 0.0 collective-permute-done.1.refs_1_
  30.5 0.5 collective-permute-start.3
  31.0 0.1 collective-permute-start.11
  31.1 2.4 %shard_map.82.own_ref = f32[12,128,128]{2,1,0:T(8,128)S(1)} custom-call(s32[9]{0:T(128)S(1)} %stack.36.place, f32[12,128,128]{2,1,0:T(8,128)} %bitcast.13, f32[12,128,128]{2,1,0:T(8,128)} %r_ref.3), custom_call_target="tpu_custom_call" | custom-call | flops 150994944 | bytes 1572864 | tf_op jit(solution)/shard_map/pallas_call | solution.py:225
  33.5 0.0 collective-permute-done.11.refs_11_
  33.5 0.0 collective-permute-done.15.refs_15_
  33.6 1.1 %shard_map.85 = (bf16[49,128,256]{2,1,0:T(8,128)(2,1)S(1)}, s32[8,128]{1,0:T(8,128)S(1)}, s32[8,128]{1,0:T(8,128)S(1)}, s32[8,128]{1,0:T(8,128)S(1)}, s32[8,128]{1,0:T(8,128)S(1)}) custom-call(s32[9]{0:T(128)S(1)} %stack.36.place, f32[12,128,128]{2,1,0:T(8,128)S(1)} %shard_map.82.own_ref, f32[3,128,128]{2,1,0:T(8,128)S(1)} %collective-permute-done.refs_0_, ...), custom_call_target="tpu_custom_call" | custom-call | flops 1000000 | bytes 4718592 | tf_op jit(solution)/shard_map/pallas_call | solution.py:225
  34.7 3.6 %shard_map.86.tiles_ref = bf16[128,128,256]{2,1,0:T(8,128)(2,1)S(1)} custom-call(s32[1]{0:T(128)} %bitcast.10.core, f32[64,128,128]{2,1,0:T(8,128)} %own_ref.1, f32[64,128,128]{2,1,0:T(8,128)} %collective-permute-done.16.other_ref), custom_call_target="tpu_custom_call" | custom-call | flops 16777216 | bytes 16777216 | tf_op jit(solution)/shard_map/pallas_call | solution.py:225
  38.3 2.3 %shard_map.90 = f32[8,128,128]{2,1,0:T(8,128)S(1)} custom-call(s32[8,128]{1,0:T(8,128)S(1)} %get-tuple-element.18.lists, bf16[128,128,256]{2,1,0:T(8,128)(2,1)S(1)} %shard_map.86.tiles_ref, bf16[49,128,256]{2,1,0:T(8,128)(2,1)S(1)} %get-tuple-element.15.proj_ref), custom_call_target="tpu_custom_call" | custom-call | flops 1073741824 | bytes 4194304 | tf_op jit(solution)/shard_map/pallas_call | solution.py:225
  40.6 0.1 collective-permute-start.18
  40.7 1.4 %shard_map.88 = f32[8,128,128]{2,1,0:T(8,128)S(1)} custom-call(s32[8,128]{1,0:T(8,128)S(1)} %get-tuple-element.16.lists, bf16[128,128,256]{2,1,0:T(8,128)(2,1)S(1)} %shard_map.86.tiles_ref, bf16[49,128,256]{2,1,0:T(8,128)(2,1)S(1)} %get-tuple-element.15.proj_ref), custom_call_target="tpu_custom_call" | custom-call | flops 1073741824 | bytes 4194304 | tf_op jit(solution)/shard_map/pallas_call | solution.py:225
  42.1 1.5 %collective-permute-start.17 = (f32[8,128,128]{2,1,0:T(8,128)S(1)}, f32[8,128,128]{2,1,0:T(8,128)S(1)}, u32[]{:S(2)}, u32[]{:S(2)}) collective-permute-start(f32[8,128,128]{2,1,0:T(8,128)S(1)} %shard_map.88), channel_id=1, source_target_pairs={{0,8},{4,20},{8,0},{12,28},{16,24},{20,4},{24,16},{28,12},{1,9},{5... | collective-permute-start | bytes 1572872 | tf_op jit(solution)/shard_map/ppermute | solution.py:364
  43.6 2.0 %shard_map.89 = f32[8,128,128]{2,1,0:T(8,128)S(1)} custom-call(s32[8,128]{1,0:T(8,128)S(1)} %get-tuple-element.17.lists, bf16[128,128,256]{2,1,0:T(8,128)(2,1)S(1)} %shard_map.86.tiles_ref, bf16[49,128,256]{2,1,0:T(8,128)(2,1)S(1)} %get-tuple-element.15.proj_ref), custom_call_target="tpu_custom_call" | custom-call | flops 1073741824 | bytes 4194304 | tf_op jit(solution)/shard_map/pallas_call | solution.py:225
  45.6 3.4 %collective-permute-done.18 = f32[8,128,128]{2,1,0:T(8,128)S(1)} collective-permute-done((f32[8,128,128]{2,1,0:T(8,128)S(1)}, f32[8,128,128]{2,1,0:T(8,128)S(1)}, u32[]{:S(2)}, u32[]{:S(2)}) %collective-permute-start.18) | collective-permute-done | bytes 524320 | tf_op jit(solution)/shard_map/ppermute | solution.py:364
  49.0 0.1 add.8
  49.1 0.1 collective-permute-start.19
  49.1 0.0 copy-start
  49.2 1.4 %shard_map.87.refs_0_ = f32[8,128,128]{2,1,0:T(8,128)S(1)} custom-call(s32[8,128]{1,0:T(8,128)S(1)} %get-tuple-element.14.lists, bf16[128,128,256]{2,1,0:T(8,128)(2,1)S(1)} %shard_map.86.tiles_ref, bf16[49,128,256]{2,1,0:T(8,128)(2,1)S(1)} %get-tuple-element.15.proj_ref), custom_call_target="tpu_custom_call" | custom-call | flops 1073741824 | bytes 4194304 | tf_op jit(solution)/shard_map/pallas_call | solution.py:225
  50.6 5.0 %collective-permute-done.17.refs_1_ = f32[8,128,128]{2,1,0:T(8,128)S(1)} collective-permute-done((f32[8,128,128]{2,1,0:T(8,128)S(1)}, f32[8,128,128]{2,1,0:T(8,128)S(1)}, u32[]{:S(2)}, u32[]{:S(2)}) %collective-permute-start.17) | collective-permute-done | bytes 524320 | tf_op jit(solution)/shard_map/ppermute | solution.py:364
  55.6 5.2 %collective-permute-done.19.refs_2_ = f32[8,128,128]{2,1,0:T(8,128)S(1)} collective-permute-done((f32[8,128,128]{2,1,0:T(8,128)S(1)}, f32[8,128,128]{2,1,0:T(8,128)S(1)}, u32[]{:S(2)}, u32[]{:S(2)}) %collective-permute-start.19) | collective-permute-done | bytes 524320 | tf_op jit(solution)/shard_map/ppermute | solution.py:364
  60.8 1.2 %shard_map.91 = f32[8,128,128]{2,1,0:T(8,128)} custom-call(f32[8,128,128]{2,1,0:T(8,128)S(1)} %copy-done, f32[8,128,128]{2,1,0:T(8,128)S(1)} %shard_map.87.refs_0_, f32[8,128,128]{2,1,0:T(8,128)S(1)} %collective-permute-done.17.refs_1_, f32[8,128,128]{2,1,0:T(8,128)S(1)} %collective-permute-done.19.refs_2_), custom_call_target="tpu_custom_call" | custom-call | flops 100663296 | bytes 2097152 | tf_op jit(solution)/shard_map/pallas_call | solution.py:225
  (7 shorter events, 0.0 us)
Async XLA Ops:
  0.0 34.6 %collective-permute-start.16 = (f32[64,128,128]{2,1,0:T(8,128)}, f32[64,128,128]{2,1,0:T(8,128)}, u32[]{:S(2)}, u32[]{:S(2)}) collective-permute-start(f32[64,128,128]{2,1,0:T(8,128)} %own_ref.1), channel_id=1, source_target_pairs={{0,4},{4,0},{8,12},{12,8},{16,20},{20,16},{24,28},{28,24},{1,5},{5... | collective-permute-start | bytes 12582920 | tf_op jit(solution)/shard_map/ppermute | solution.py:263
  2.6 12.0 %collective-permute-start.4 = (f32[3,64,128]{2,1,0:T(8,128)S(1)}, f32[3,64,128]{2,1,0:T(8,128)S(1)}, u32[]{:S(2)}, u32[]{:S(2)}) collective-permute-start(f32[3,64,128]{2,1,0:T(8,128)S(1)} %get-tuple-element.13), channel_id=1, source_target_pairs={{0,2},{1,3},{2,0},{3,1},{4,6},{5,7},{6,4},{7,5},{8,10},{9,11},{10,... | collective-permute-start | bytes 294920 | tf_op jit(solution)/shard_map/ppermute | solution.py:266
  2.8 13.4 %collective-permute-start.12 = (f32[3,128,128]{2,1,0:T(8,128)S(1)}, f32[3,128,128]{2,1,0:T(8,128)S(1)}, u32[]{:S(2)}, u32[]{:S(2)}) collective-permute-start(f32[3,128,128]{2,1,0:T(8,128)S(1)} %get-tuple-element.12), channel_id=1, source_target_pairs={{0,3},{1,0},{2,1},{3,2},{4,7},{5,4},{6,5},{7,6},{8,11},{9,8},{10,9... | collective-permute-start | bytes 589832 | tf_op jit(solution)/shard_map/ppermute | solution.py:266
  2.9 18.5 %collective-permute-start = (f32[3,128,128]{2,1,0:T(8,128)S(1)}, f32[3,128,128]{2,1,0:T(8,128)S(1)}, u32[]{:S(2)}, u32[]{:S(2)}) collective-permute-start(f32[3,128,128]{2,1,0:T(8,128)S(1)} %get-tuple-element.12), channel_id=1, source_target_pairs={{0,1},{1,2},{2,3},{3,0},{4,5},{5,6},{6,7},{7,4},{8,9},{9,10},{10,1... | collective-permute-start | bytes 589832 | tf_op jit(solution)/shard_map/ppermute | solution.py:266
  14.6 4.0 %collective-permute-start.6 = (f32[224,128]{1,0:T(8,128)S(1)}, f32[224,128]{1,0:T(8,128)S(1)}, u32[]{:S(2)}, u32[]{:S(2)}) collective-permute-start(f32[224,128]{1,0:T(8,128)S(1)} %pad_maximum_fusion.refs_4_), channel_id=1, source_target_pairs={{0,8},{4,20},{8,0},{12,28},{16,24},{20,4},{24,16},{28,12},{1,9},{5... | collective-permute-start | bytes 344072 | tf_op jit(solution)/shard_map/ppermute | solution.py:318
  14.9 5.6 %collective-permute-start.5 = (f32[224,128]{1,0:T(8,128)S(1)}, f32[224,128]{1,0:T(8,128)S(1)}, u32[]{:S(2)}, u32[]{:S(2)}) collective-permute-start(f32[224,128]{1,0:T(8,128)S(1)} %pad_maximum_fusion.refs_4_), channel_id=1, source_target_pairs={{0,16},{4,12},{8,24},{12,4},{16,0},{20,28},{24,8},{28,20},{1,17},{... | collective-permute-start | bytes 344072 | tf_op jit(solution)/shard_map/ppermute | solution.py:318
  16.1 5.6 %collective-permute-start.8 = (f32[224,128]{1,0:T(8,128)S(1)}, f32[224,128]{1,0:T(8,128)S(1)}, u32[]{:S(2)}, u32[]{:S(2)}) collective-permute-start(f32[224,128]{1,0:T(8,128)S(1)} %pad_maximum_fusion.refs_4_), channel_id=1, source_target_pairs={{0,4},{4,0},{8,12},{12,8},{16,20},{20,16},{24,28},{28,24},{1,5},{5... | collective-permute-start | bytes 344072 | tf_op jit(solution)/shard_map/ppermute | solution.py:263
  18.6 4.3 %collective-permute-start.10 = (f32[224,128]{1,0:T(8,128)S(1)}, f32[224,128]{1,0:T(8,128)S(1)}, u32[]{:S(2)}, u32[]{:S(2)}) collective-permute-start(f32[224,128]{1,0:T(8,128)S(1)} %collective-permute-done.6.refs_6_), channel_id=1, source_target_pairs={{0,4},{4,0},{8,12},{12,8},{16,20},{20,16},{24,28},{28,24},{1,5},{5... | collective-permute-start | bytes 344072 | tf_op jit(solution)/shard_map/ppermute | solution.py:263
  20.5 2.7 %collective-permute-start.9 = (f32[224,128]{1,0:T(8,128)S(1)}, f32[224,128]{1,0:T(8,128)S(1)}, u32[]{:S(2)}, u32[]{:S(2)}) collective-permute-start(f32[224,128]{1,0:T(8,128)S(1)} %collective-permute-done.5.refs_5_), channel_id=1, source_target_pairs={{0,4},{4,0},{8,12},{12,8},{16,20},{20,16},{24,28},{28,24},{1,5},{5... | collective-permute-start | bytes 344072 | tf_op jit(solution)/shard_map/ppermute | solution.py:263
  21.5 9.0 %collective-permute-start.13 = (f32[3,128,128]{2,1,0:T(8,128)S(1)}, f32[3,128,128]{2,1,0:T(8,128)S(1)}, u32[]{:S(2)}, u32[]{:S(2)}) collective-permute-start(f32[3,128,128]{2,1,0:T(8,128)S(1)} %collective-permute-done.12.refs_12_), channel_id=1, source_target_pairs={{0,8},{4,20},{8,0},{12,28},{16,24},{20,4},{24,16},{28,12},{1,9},{5... | collective-permute-start | bytes 589832 | tf_op jit(solution)/shard_map/ppermute | solution.py:318
  21.7 8.8 %collective-permute-start.1 = (f32[3,128,128]{2,1,0:T(8,128)S(1)}, f32[3,128,128]{2,1,0:T(8,128)S(1)}, u32[]{:S(2)}, u32[]{:S(2)}) collective-permute-start(f32[3,128,128]{2,1,0:T(8,128)S(1)} %collective-permute-done.refs_0_), channel_id=1, source_target_pairs={{0,8},{4,20},{8,0},{12,28},{16,24},{20,4},{24,16},{28,12},{1,9},{5... | collective-permute-start | bytes 589832 | tf_op jit(solution)/shard_map/ppermute | solution.py:318
  23.0 6.7 %collective-permute-start.7 = (f32[224,128]{1,0:T(8,128)S(1)}, f32[224,128]{1,0:T(8,128)S(1)}, u32[]{:S(2)}, u32[]{:S(2)}) collective-permute-start(f32[224,128]{1,0:T(8,128)S(1)} %collective-permute-done.5.refs_5_), channel_id=1, source_target_pairs={{0,8},{4,20},{8,0},{12,28},{16,24},{20,4},{24,16},{28,12},{1,9},{5... | collective-permute-start | bytes 344072 | tf_op jit(solution)/shard_map/ppermute | solution.py:318
  23.2 7.8 %collective-permute-start.14 = (f32[3,128,128]{2,1,0:T(8,128)S(1)}, f32[3,128,128]{2,1,0:T(8,128)S(1)}, u32[]{:S(2)}, u32[]{:S(2)}) collective-permute-start(f32[3,128,128]{2,1,0:T(8,128)S(1)} %collective-permute-done.12.refs_12_), channel_id=1, source_target_pairs={{0,4},{4,0},{8,12},{12,8},{16,20},{20,16},{24,28},{28,24},{1,5},{5... | collective-permute-start | bytes 589832 | tf_op jit(solution)/shard_map/ppermute | solution.py:263
  29.6 3.9 %collective-permute-start.2 = (f32[3,128,128]{2,1,0:T(8,128)S(1)}, f32[3,128,128]{2,1,0:T(8,128)S(1)}, u32[]{:S(2)}, u32[]{:S(2)}) collective-permute-start(f32[3,128,128]{2,1,0:T(8,128)S(1)} %collective-permute-done.refs_0_), channel_id=1, source_target_pairs={{0,4},{4,0},{8,12},{12,8},{16,20},{20,16},{24,28},{28,24},{1,5},{5... | collective-permute-start | bytes 589832 | tf_op jit(solution)/shard_map/ppermute | solution.py:263
  30.5 3.0 %collective-permute-start.15 = (f32[3,128,128]{2,1,0:T(8,128)S(1)}, f32[3,128,128]{2,1,0:T(8,128)S(1)}, u32[]{:S(2)}, u32[]{:S(2)}) collective-permute-start(f32[3,128,128]{2,1,0:T(8,128)S(1)} %collective-permute-done.13.refs_13_), channel_id=1, source_target_pairs={{0,4},{4,0},{8,12},{12,8},{16,20},{20,16},{24,28},{28,24},{1,5},{5... | collective-permute-start | bytes 589832 | tf_op jit(solution)/shard_map/ppermute | solution.py:263
  30.5 3.1 %collective-permute-start.3 = (f32[3,128,128]{2,1,0:T(8,128)S(1)}, f32[3,128,128]{2,1,0:T(8,128)S(1)}, u32[]{:S(2)}, u32[]{:S(2)}) collective-permute-start(f32[3,128,128]{2,1,0:T(8,128)S(1)} %collective-permute-done.1.refs_1_), channel_id=1, source_target_pairs={{0,4},{4,0},{8,12},{12,8},{16,20},{20,16},{24,28},{28,24},{1,5},{5... | collective-permute-start | bytes 589832 | tf_op jit(solution)/shard_map/ppermute | solution.py:263
  31.0 2.5 %collective-permute-start.11 = (f32[224,128]{1,0:T(8,128)S(1)}, f32[224,128]{1,0:T(8,128)S(1)}, u32[]{:S(2)}, u32[]{:S(2)}) collective-permute-start(f32[224,128]{1,0:T(8,128)S(1)} %collective-permute-done.7.refs_7_), channel_id=1, source_target_pairs={{0,4},{4,0},{8,12},{12,8},{16,20},{20,16},{24,28},{28,24},{1,5},{5... | collective-permute-start | bytes 344072 | tf_op jit(solution)/shard_map/ppermute | solution.py:263
  40.6 8.4 %collective-permute-start.18 = (f32[8,128,128]{2,1,0:T(8,128)S(1)}, f32[8,128,128]{2,1,0:T(8,128)S(1)}, u32[]{:S(2)}, u32[]{:S(2)}) collective-permute-start(f32[8,128,128]{2,1,0:T(8,128)S(1)} %shard_map.90), channel_id=1, source_target_pairs={{0,8},{4,20},{8,0},{12,28},{16,24},{20,4},{24,16},{28,12},{1,9},{5... | collective-permute-start | bytes 1572872 | tf_op jit(solution)/shard_map/ppermute | solution.py:364
  42.1 13.5 %collective-permute-start.17 = (f32[8,128,128]{2,1,0:T(8,128)S(1)}, f32[8,128,128]{2,1,0:T(8,128)S(1)}, u32[]{:S(2)}, u32[]{:S(2)}) collective-permute-start(f32[8,128,128]{2,1,0:T(8,128)S(1)} %shard_map.88), channel_id=1, source_target_pairs={{0,8},{4,20},{8,0},{12,28},{16,24},{20,4},{24,16},{28,12},{1,9},{5... | collective-permute-start | bytes 1572872 | tf_op jit(solution)/shard_map/ppermute | solution.py:364
  49.1 11.8 %collective-permute-start.19 = (f32[8,128,128]{2,1,0:T(8,128)S(1)}, f32[8,128,128]{2,1,0:T(8,128)S(1)}, u32[]{:S(2)}, u32[]{:S(2)}) collective-permute-start(f32[8,128,128]{2,1,0:T(8,128)S(1)} %add.8), channel_id=1, source_target_pairs={{0,16},{4,12},{8,24},{12,4},{16,0},{20,28},{24,8},{28,20},{1,17},{... | collective-permute-start | bytes 1572872 | tf_op jit(solution)/shard_map/ppermute | solution.py:364
  49.1 11.7 %copy-start = (f32[8,128,128]{2,1,0:T(8,128)S(1)}, f32[8,128,128]{2,1,0:T(8,128)}, u32[]{:S(2)}) copy-start(f32[8,128,128]{2,1,0:T(8,128)} %left_ref.1) | copy-start | bytes 1572868

commit v5 on v4

--- a/solution.py
+++ b/solution.py
@@ -84,6 +84,8 @@
     offset = jnp.zeros((16, 1), F32)
     total = jnp.zeros((8, chips * span), F32)
     for i in range(blocks):
+        if i == blocks // 2:
+            first_half = offset
         col, own, place = words[0, i : i + 1], words[1, i : i + 1], words[2, i : i + 1]
         chip = jnp.where(lanes((1, listed)) < counts[i], own >> 1, chips)
         match = (kinds == chip).astype(F32)
@@ -110,6 +112,8 @@
     for c in range(chips):
         part = total[:, c * span : (c + 1) * span]
         number = jnp.broadcast_to(offset[c : c + 1], (8, span))
+        number_half = jnp.broadcast_to(first_half[c : c + 1], (8, span))
+        part = jnp.where(row == 4, number_half, part)
         part = jnp.where(row == 0, number, jnp.where(row == 2, part + columns, part))
         out_ref[8 * c : 8 * c + 8] = part
 
@@ -184,44 +188,54 @@
         at += 8
 
 
-def entry_kernel(lists, tiles_ref, proj_ref, out_ref):
-    _, _, width = out_ref.shape
+def entry_kernel(second, lists, tiles_ref, proj_ref, out_ref):
+    blocks, _, width = out_ref.shape
+    zeros = proj_ref.shape[0] - 1
+    first, last = (lists[4, 0], lists[0, 0]) if second else (0, lists[4, 0])
     out_ref[...] = jnp.zeros_like(out_ref)
 
     def multiply(base, n):
         terms = []
         for u in range(n):
-            proj = proj_ref[lists[2, base + u]]
+            at = base + u
+            proj = proj_ref[jnp.where(at < last, lists[2, at], zeros)]
             d = jnp.dot(
-                tiles_ref[lists[1, base + u]],
+                tiles_ref[lists[1, at]],
                 jnp.concatenate([proj, proj], axis=0),
                 preferred_element_type=F32,
             )
             terms.append(d[:, :width] + d[:, width:])
         for u in range(n):
-            out_ref[lists[3, base + u]] += terms[u]
+            block = lists[3, base + u] - (blocks if second else 0)
+            out_ref[jnp.clip(block, 0, blocks - 1)] += terms[u]
 
     def step(s, _):
-        multiply(s * UNROLL, UNROLL)
+        multiply(first + s * UNROLL, UNROLL)
         return 0
 
-    number = lists[0, 0]
+    number = last - first
     steps = (number + UNROLL // 2 - 1) // UNROLL
     lax.fori_loop(0, steps, step, 0)
 
     @pl.when(number > steps * UNROLL)
     def _():
-        multiply(steps * UNROLL, UNROLL // 2)
-
-
-def final_kernel(left_ref, *refs):
-    sums, out_ref = refs[:-1], refs[-1]
-    for i in range(out_ref.shape[0]):
+        multiply(first + steps * UNROLL, UNROLL // 2)
+
+
+def final_kernel(second, left_ref, *refs):
+    out_ref, buf, sem = refs[-3:]
+    sums = refs[1:-3] if second else refs[:-3]
+    blocks = buf.shape[0]
+    start = blocks if second else 0
+    for i in range(blocks):
         total = functools.reduce(jnp.add, [r[i] for r in sums])
-        out_ref[i] = triple(left_ref[i], total, ((1,), (0,)))
-
-
-def call(kernel, prefetch, ins, out, scratch, args, estimate, limit, grid=(), out_spec=VMEM):
+        buf[i] = triple(left_ref[start + i], total, ((1,), (0,)))
+    copy = pltpu.make_async_copy(buf, out_ref.at[pl.ds(start, blocks)], sem)
+    copy.start()
+    copy.wait()
+
+
+def call(kernel, prefetch, ins, out, scratch, args, estimate, limit, grid=(), out_spec=VMEM, aliases={}):
     return pl.pallas_call(
         kernel,
         out_shape=out,
@@ -234,6 +248,7 @@
         ),
         compiler_params=pltpu.CompilerParams(vmem_limit_bytes=limit),
         cost_estimate=estimate,
+        input_output_aliases=aliases,
     )(*args)
 
 
@@ -348,26 +363,35 @@
     )
 
     total = {
-        m: [
+        (m, h): [
             call(
-                entry_kernel, 1, [VMEM, VMEM],
-                jax.ShapeDtypeStruct((blocks, coarse, vecs), F32),
+                functools.partial(entry_kernel, h), 1, [VMEM, VMEM],
+                jax.ShapeDtypeStruct((blocks // 2, coarse, vecs), F32),
                 [], (tables[m], packed, proj),
-                cost(cap * 128**3 * 8, 4 * MIB), 12 * MIB,
+                cost(cap * 128**3 * 4, 4 * MIB), 12 * MIB,
             )
         ]
         for m in range(chips)
+        for h in range(2)
     }
     for m in masks_of(chips):
         bit = m & -m
-        value = functools.reduce(jnp.add, total[m])
-        total[m ^ bit].append(lax.ppermute(value, "rows", across(bit)))
-    result = call(
-        final_kernel, 0, [VMEM] * (1 + len(total[0])),
-        jax.ShapeDtypeStruct((blocks, fine, vecs), F32),
-        [], (left, *total[0]), cost(2 * blocks * 128**3 * 3, 2 * MIB), 8 * MIB,
-    )
-    return result.reshape(blocks * fine, vecs)
+        for h in range(2):
+            value = functools.reduce(jnp.add, total[m, h])
+            total[m ^ bit, h].append(lax.ppermute(value, "rows", across(bit)))
+    result = []
+    for h in range(2):
+        result = [
+            call(
+                functools.partial(final_kernel, h), 0,
+                [VMEM] + [HBM] * len(result) + [VMEM] * len(total[0, h]),
+                jax.ShapeDtypeStruct((blocks, fine, vecs), F32),
+                [pltpu.VMEM((blocks // 2, fine, vecs), F32), pltpu.SemaphoreType.DMA(())],
+                (left, *result, *total[0, h]), cost(blocks * 128**3 * 3, MIB), 8 * MIB,
+                out_spec=HBM, aliases={1: 0} if result else {},
+            )
+        ]
+    return result[0].reshape(blocks * fine, vecs)
 
 
 def masks_of(chips):

time: 62.2 us -> 61.8 us (level)
  the two profiles are of different devices: /device:TPU:29 before, /device:TPU:24 now
where the time goes in v5:
time: 61.8 us; the launch traced here: 61.6 us
  Pallas kernels  25 us (40%)
  starting transfers between devices  18.4 us (30%)
  waiting for transfers between devices  17.8 us (29%)
    pallas_call x15, Pallas kernels, call(): pl.pallas_call(kernel, out_shape=out, grid_spec=pltpu.PrefetchScalarGridS...  25 us
    ppermute x5, waiting for transfers between devices, spread(): return lax.ppermute(x, 'rows', across(mask))  8.78 us
    ppermute x6, starting transfers between devices, work(): total[m ^ bit, h].append(lax.ppermute(value, 'rows', across(bit)))  6.61 us
    ppermute x5, starting transfers between devices, spread(): return lax.ppermute(x, 'rows', across(mask))  6.56 us
    ppermute x3, waiting for transfers between devices, turn(): lax.ppermute(x, 'blk', [(b, (b + k) % planes) for b in range(planes)])  6.08 us
    ppermute x3, starting transfers between devices, turn(): lax.ppermute(x, 'blk', [(b, (b + k) % planes) for b in range(planes)])  4.22 us
    ppermute x6, waiting for transfers between devices, work(): total[m ^ bit, h].append(lax.ppermute(value, 'rows', across(bit)))  2.91 us
  transfers between devices with their start and end apart: 23, of which 7 were waited for; matrix products, arithmetic and copies ran while one was open for 0% of the time, Pallas kernels for 31%

profile of v5, /device:TPU:24, one launch (start us, length us, event | category | flops | bytes accessed | tf_op | source)
XLA Modules:
  0.0 61.6 jit_solution(6487321905044804604)
XLA Ops:
  0.0 0.1 stack.36.place
  0.1 1.9 %shard_map.83 = (f32[3,128,128]{2,1,0:T(8,128)S(1)}, f32[3,64,128]{2,1,0:T(8,128)S(1)}) custom-call(s32[9]{0:T(128)S(1)} %stack.36.place, f32[12,128,128]{2,1,0:T(8,128)} %bitcast.12, f32[12,128,128]{2,1,0:T(8,128)} %r_ref.3), custom_call_target="tpu_custom_call" | custom-call | flops 37748736 | bytes 393216 | tf_op jit(solution)/shard_map/pallas_call | solution.py:239
  2.0 0.4 collective-permute-start.4
  2.4 0.2 collective-permute-start.12
  2.5 3.6 %collective-permute-start = (f32[3,128,128]{2,1,0:T(8,128)S(1)}, f32[3,128,128]{2,1,0:T(8,128)S(1)}, u32[]{:S(2)}, u32[]{:S(2)}) collective-permute-start(f32[3,128,128]{2,1,0:T(8,128)S(1)} %get-tuple-element.12), channel_id=1, source_target_pairs={{0,1},{1,2},{2,3},{3,0},{4,5},{5,6},{6,7},{7,4},{8,9},{9,10},{10,1... | collective-permute-start | bytes 589832 | tf_op jit(solution)/shard_map/ppermute | solution.py:281
  6.2 2.2 %shard_map.84.refs_16_ = f32[32,128]{1,0:T(8,128)S(1)} custom-call(s32[8,32]{1,0:T(8,128)} %cols.1, s32[8,32]{1,0:T(8,128)} %owner.1, s32[8,32]{1,0:T(8,128)} %slot.1, s32[8]{0:T(128)} %number.1), custom_call_target="tpu_custom_call" | custom-call | flops 100000000 | bytes 16384 | tf_op jit(solution)/shard_map/pallas_call | solution.py:239
  8.4 6.1 %collective-permute-done.4 = f32[3,64,128]{2,1,0:T(8,128)S(1)} collective-permute-done((f32[3,64,128]{2,1,0:T(8,128)S(1)}, f32[3,64,128]{2,1,0:T(8,128)S(1)}, u32[]{:S(2)}, u32[]{:S(2)}) %collective-permute-start.4) | collective-permute-done | bytes 98336 | tf_op jit(solution)/shard_map/ppermute | solution.py:281
  14.4 1.6 %collective-permute-start.6 = (f32[224,128]{1,0:T(8,128)S(1)}, f32[224,128]{1,0:T(8,128)S(1)}, u32[]{:S(2)}, u32[]{:S(2)}) collective-permute-start(f32[224,128]{1,0:T(8,128)S(1)} %pad_maximum_fusion.refs_4_), channel_id=1, source_target_pairs={{0,8},{4,20},{8,0},{12,28},{16,24},{20,4},{24,16},{28,12},{1,9},{5... | collective-permute-start | bytes 344072 | tf_op jit(solution)/shard_map/ppermute | solution.py:333
  16.0 1.5 %collective-permute-start.5 = (f32[224,128]{1,0:T(8,128)S(1)}, f32[224,128]{1,0:T(8,128)S(1)}, u32[]{:S(2)}, u32[]{:S(2)}) collective-permute-start(f32[224,128]{1,0:T(8,128)S(1)} %pad_maximum_fusion.refs_4_), channel_id=1, source_target_pairs={{0,16},{4,12},{8,24},{12,4},{16,0},{20,28},{24,8},{28,20},{1,17},{... | collective-permute-start | bytes 344072 | tf_op jit(solution)/shard_map/ppermute | solution.py:333
  17.5 0.0 collective-permute-start.8
  17.5 2.7 %collective-permute-done.6.refs_6_ = f32[224,128]{1,0:T(8,128)S(1)} collective-permute-done((f32[224,128]{1,0:T(8,128)S(1)}, f32[224,128]{1,0:T(8,128)S(1)}, u32[]{:S(2)}, u32[]{:S(2)}) %collective-permute-start.6) | collective-permute-done | bytes 114720 | tf_op jit(solution)/shard_map/ppermute | solution.py:333
  20.2 0.0 collective-permute-start.10
  20.2 0.6 collective-permute-done.5.refs_5_
  20.8 0.0 collective-permute-start.9
  20.8 0.0 collective-permute-done.refs_0_
  20.8 1.4 %collective-permute-start.13 = (f32[3,128,128]{2,1,0:T(8,128)S(1)}, f32[3,128,128]{2,1,0:T(8,128)S(1)}, u32[]{:S(2)}, u32[]{:S(2)}) collective-permute-start(f32[3,128,128]{2,1,0:T(8,128)S(1)} %collective-permute-done.12.refs_12_), channel_id=1, source_target_pairs={{0,8},{4,20},{8,0},{12,28},{16,24},{20,4},{24,16},{28,12},{1,9},{5... | collective-permute-start | bytes 589832 | tf_op jit(solution)/shard_map/ppermute | solution.py:333
  22.3 0.0 collective-permute-done.8.refs_8_
  22.3 0.6 collective-permute-start.1
  22.8 0.0 collective-permute-done.10.refs_10_
  22.8 1.4 %collective-permute-start.7 = (f32[224,128]{1,0:T(8,128)S(1)}, f32[224,128]{1,0:T(8,128)S(1)}, u32[]{:S(2)}, u32[]{:S(2)}) collective-permute-start(f32[224,128]{1,0:T(8,128)S(1)} %collective-permute-done.5.refs_5_), channel_id=1, source_target_pairs={{0,8},{4,20},{8,0},{12,28},{16,24},{20,4},{24,16},{28,12},{1,9},{5... | collective-permute-start | bytes 344072 | tf_op jit(solution)/shard_map/ppermute | solution.py:333
  24.3 0.0 collective-permute-done.9.refs_9_
  24.3 5.5 %collective-permute-done.7.refs_7_ = f32[224,128]{1,0:T(8,128)S(1)} collective-permute-done((f32[224,128]{1,0:T(8,128)S(1)}, f32[224,128]{1,0:T(8,128)S(1)}, u32[]{:S(2)}, u32[]{:S(2)}) %collective-permute-start.7) | collective-permute-done | bytes 114720 | tf_op jit(solution)/shard_map/ppermute | solution.py:333
  29.8 0.5 collective-permute-start.15
  30.3 0.1 collective-permute-start.3
  30.4 0.4 collective-permute-start.11
  30.8 2.4 %shard_map.82.own_ref = f32[12,128,128]{2,1,0:T(8,128)S(1)} custom-call(s32[9]{0:T(128)S(1)} %stack.36.place, f32[12,128,128]{2,1,0:T(8,128)} %bitcast.13, f32[12,128,128]{2,1,0:T(8,128)} %r_ref.3), custom_call_target="tpu_custom_call" | custom-call | flops 150994944 | bytes 1572864 | tf_op jit(solution)/shard_map/pallas_call | solution.py:239
  33.3 1.1 %shard_map.85 = (bf16[49,128,256]{2,1,0:T(8,128)(2,1)S(1)}, s32[8,128]{1,0:T(8,128)S(1)}, s32[8,128]{1,0:T(8,128)S(1)}, s32[8,128]{1,0:T(8,128)S(1)}, s32[8,128]{1,0:T(8,128)S(1)}) custom-call(s32[9]{0:T(128)S(1)} %stack.36.place, f32[12,128,128]{2,1,0:T(8,128)S(1)} %shard_map.82.own_ref, f32[3,128,128]{2,1,0:T(8,128)S(1)} %collective-permute-done.refs_0_, ...), custom_call_target="tpu_custom_call" | custom-call | flops 1000000 | bytes 4718592 | tf_op jit(solution)/shard_map/pallas_call | solution.py:239
  34.4 3.6 %shard_map.86.tiles_ref = bf16[128,128,256]{2,1,0:T(8,128)(2,1)S(1)} custom-call(s32[1]{0:T(128)} %bitcast.10.core, f32[64,128,128]{2,1,0:T(8,128)} %own_ref.1, f32[64,128,128]{2,1,0:T(8,128)} %collective-permute-done.16.other_ref), custom_call_target="tpu_custom_call" | custom-call | flops 16777216 | bytes 16777216 | tf_op jit(solution)/shard_map/pallas_call | solution.py:239
  38.0 1.5 %shard_map.90 = f32[4,128,128]{2,1,0:T(8,128)S(1)} custom-call(s32[8,128]{1,0:T(8,128)S(1)} %get-tuple-element.18.lists, bf16[128,128,256]{2,1,0:T(8,128)(2,1)S(1)} %shard_map.86.tiles_ref, bf16[49,128,256]{2,1,0:T(8,128)(2,1)S(1)} %get-tuple-element.15.proj_ref), custom_call_target="tpu_custom_call" | custom-call | flops 536870912 | bytes 4194304 | tf_op jit(solution)/shard_map/pallas_call | solution.py:239
  39.6 1.5 %collective-permute-start.18 = (f32[4,128,128]{2,1,0:T(8,128)S(1)}, f32[4,128,128]{2,1,0:T(8,128)S(1)}, u32[]{:S(2)}, u32[]{:S(2)}) collective-permute-start(f32[4,128,128]{2,1,0:T(8,128)S(1)} %shard_map.90), channel_id=1, source_target_pairs={{0,8},{4,20},{8,0},{12,28},{16,24},{20,4},{24,16},{28,12},{1,9},{5... | collective-permute-start | bytes 786440 | tf_op jit(solution)/shard_map/ppermute | solution.py:381
  41.1 1.5 %shard_map.95 = f32[4,128,128]{2,1,0:T(8,128)S(1)} custom-call(s32[8,128]{1,0:T(8,128)S(1)} %get-tuple-element.18.lists, bf16[128,128,256]{2,1,0:T(8,128)(2,1)S(1)} %shard_map.86.tiles_ref, bf16[49,128,256]{2,1,0:T(8,128)(2,1)S(1)} %get-tuple-element.15.proj_ref), custom_call_target="tpu_custom_call" | custom-call | flops 536870912 | bytes 4194304 | tf_op jit(solution)/shard_map/pallas_call | solution.py:239
  42.6 0.6 %collective-permute-start.21 = (f32[4,128,128]{2,1,0:T(8,128)S(1)}, f32[4,128,128]{2,1,0:T(8,128)S(1)}, u32[]{:S(2)}, u32[]{:S(2)}) collective-permute-start(f32[4,128,128]{2,1,0:T(8,128)S(1)} %shard_map.95), channel_id=1, source_target_pairs={{0,8},{4,20},{8,0},{12,28},{16,24},{20,4},{24,16},{28,12},{1,9},{5... | collective-permute-start | bytes 786440 | tf_op jit(solution)/shard_map/ppermute | solution.py:381
  43.3 1.6 %shard_map.88 = f32[4,128,128]{2,1,0:T(8,128)S(1)} custom-call(s32[8,128]{1,0:T(8,128)S(1)} %get-tuple-element.16.lists, bf16[128,128,256]{2,1,0:T(8,128)(2,1)S(1)} %shard_map.86.tiles_ref, bf16[49,128,256]{2,1,0:T(8,128)(2,1)S(1)} %get-tuple-element.15.proj_ref), custom_call_target="tpu_custom_call" | custom-call | flops 536870912 | bytes 4194304 | tf_op jit(solution)/shard_map/pallas_call | solution.py:239
  44.8 1.4 %collective-permute-start.17 = (f32[4,128,128]{2,1,0:T(8,128)S(1)}, f32[4,128,128]{2,1,0:T(8,128)S(1)}, u32[]{:S(2)}, u32[]{:S(2)}) collective-permute-start(f32[4,128,128]{2,1,0:T(8,128)S(1)} %shard_map.88), channel_id=1, source_target_pairs={{0,8},{4,20},{8,0},{12,28},{16,24},{20,4},{24,16},{28,12},{1,9},{5... | collective-permute-start | bytes 786440 | tf_op jit(solution)/shard_map/ppermute | solution.py:381
  46.2 1.5 %shard_map.94 = f32[4,128,128]{2,1,0:T(8,128)S(1)} custom-call(s32[8,128]{1,0:T(8,128)S(1)} %get-tuple-element.17.lists, bf16[128,128,256]{2,1,0:T(8,128)(2,1)S(1)} %shard_map.86.tiles_ref, bf16[49,128,256]{2,1,0:T(8,128)(2,1)S(1)} %get-tuple-element.15.proj_ref), custom_call_target="tpu_custom_call" | custom-call | flops 536870912 | bytes 4194304 | tf_op jit(solution)/shard_map/pallas_call | solution.py:239
  47.8 1.4 %shard_map.89 = f32[4,128,128]{2,1,0:T(8,128)S(1)} custom-call(s32[8,128]{1,0:T(8,128)S(1)} %get-tuple-element.17.lists, bf16[128,128,256]{2,1,0:T(8,128)(2,1)S(1)} %shard_map.86.tiles_ref, bf16[49,128,256]{2,1,0:T(8,128)(2,1)S(1)} %get-tuple-element.15.proj_ref), custom_call_target="tpu_custom_call" | custom-call | flops 536870912 | bytes 4194304 | tf_op jit(solution)/shard_map/pallas_call | solution.py:239
  49.2 1.2 %collective-permute-start.19 = (f32[4,128,128]{2,1,0:T(8,128)S(1)}, f32[4,128,128]{2,1,0:T(8,128)S(1)}, u32[]{:S(2)}, u32[]{:S(2)}) collective-permute-start(f32[4,128,128]{2,1,0:T(8,128)S(1)} %add.11), channel_id=1, source_target_pairs={{0,16},{4,12},{8,24},{12,4},{16,0},{20,28},{24,8},{28,20},{1,17},{... | collective-permute-start | bytes 786440 | tf_op jit(solution)/shard_map/ppermute | solution.py:381
  50.4 1.4 %shard_map.93 = f32[4,128,128]{2,1,0:T(8,128)S(1)} custom-call(s32[8,128]{1,0:T(8,128)S(1)} %get-tuple-element.16.lists, bf16[128,128,256]{2,1,0:T(8,128)(2,1)S(1)} %shard_map.86.tiles_ref, bf16[49,128,256]{2,1,0:T(8,128)(2,1)S(1)} %get-tuple-element.15.proj_ref), custom_call_target="tpu_custom_call" | custom-call | flops 536870912 | bytes 4194304 | tf_op jit(solution)/shard_map/pallas_call | solution.py:239
  51.8 1.4 %collective-permute-start.20 = (f32[4,128,128]{2,1,0:T(8,128)S(1)}, f32[4,128,128]{2,1,0:T(8,128)S(1)}, u32[]{:S(2)}, u32[]{:S(2)}) collective-permute-start(f32[4,128,128]{2,1,0:T(8,128)S(1)} %shard_map.93), channel_id=1, source_target_pairs={{0,8},{4,20},{8,0},{12,28},{16,24},{20,4},{24,16},{28,12},{1,9},{5... | collective-permute-start | bytes 786440 | tf_op jit(solution)/shard_map/ppermute | solution.py:381
  53.2 0.6 collective-permute-start.22
  53.8 1.5 %shard_map.92.refs_1_ = f32[4,128,128]{2,1,0:T(8,128)S(1)} custom-call(s32[8,128]{1,0:T(8,128)S(1)} %get-tuple-element.14.lists, bf16[128,128,256]{2,1,0:T(8,128)(2,1)S(1)} %shard_map.86.tiles_ref, bf16[49,128,256]{2,1,0:T(8,128)(2,1)S(1)} %get-tuple-element.15.proj_ref), custom_call_target="tpu_custom_call" | custom-call | flops 536870912 | bytes 4194304 | tf_op jit(solution)/shard_map/pallas_call | solution.py:239
  55.3 0.0 copy-start
  55.3 1.4 %shard_map.87.refs_0_ = f32[4,128,128]{2,1,0:T(8,128)S(1)} custom-call(s32[8,128]{1,0:T(8,128)S(1)} %get-tuple-element.14.lists, bf16[128,128,256]{2,1,0:T(8,128)(2,1)S(1)} %shard_map.86.tiles_ref, bf16[49,128,256]{2,1,0:T(8,128)(2,1)S(1)} %get-tuple-element.15.proj_ref), custom_call_target="tpu_custom_call" | custom-call | flops 536870912 | bytes 4194304 | tf_op jit(solution)/shard_map/pallas_call | solution.py:239
  56.7 1.1 %collective-permute-done.19.refs_2_ = f32[4,128,128]{2,1,0:T(8,128)S(1)} collective-permute-done((f32[4,128,128]{2,1,0:T(8,128)S(1)}, f32[4,128,128]{2,1,0:T(8,128)S(1)}, u32[]{:S(2)}, u32[]{:S(2)}) %collective-permute-start.19) | collective-permute-done | bytes 262176 | tf_op jit(solution)/shard_map/ppermute | solution.py:381
  57.8 1.0 %shard_map.91.refs_0_ = f32[8,128,128]{2,1,0:T(8,128)} custom-call(f32[8,128,128]{2,1,0:T(8,128)S(1)} %copy-done, f32[4,128,128]{2,1,0:T(8,128)S(1)} %shard_map.87.refs_0_, f32[4,128,128]{2,1,0:T(8,128)S(1)} %collective-permute-done.17.refs_1_, f32[4,128,128]{2,1,0:T(8,128)S(1)} %collective-permute-done.19.refs_2_), custom_call_target="tpu_custom_call" | custom-call | flops 50331648 | bytes 1048576 | tf_op jit(solution)/shard_map/pallas_call | solution.py:239
  58.8 1.5 %collective-permute-done.20.refs_2_ = f32[4,128,128]{2,1,0:T(8,128)S(1)} collective-permute-done((f32[4,128,128]{2,1,0:T(8,128)S(1)}, f32[4,128,128]{2,1,0:T(8,128)S(1)}, u32[]{:S(2)}, u32[]{:S(2)}) %collective-permute-start.20) | collective-permute-done | bytes 262176 | tf_op jit(solution)/shard_map/ppermute | solution.py:381
  60.3 0.3 collective-permute-done.22.refs_3_
  60.6 1.0 %shard_map.96 = f32[8,128,128]{2,1,0:T(8,128)} custom-call(f32[8,128,128]{2,1,0:T(8,128)S(1)} %copy-done, f32[8,128,128]{2,1,0:T(8,128)} %shard_map.91.refs_0_, f32[4,128,128]{2,1,0:T(8,128)S(1)} %shard_map.92.refs_1_, f32[4,128,128]{2,1,0:T(8,128)S(1)} %collective-permute-done.20.refs_2_, ...), custom_call_target="tpu_custom_call", output_to_operand_aliasing={{}: (1, {})} | custom-call | flops 50331648 | bytes 1048576 | tf_op jit(solution)/shard_map/pallas_call | solution.py:239
  (19 shorter events, 0.1 us)
Async XLA Ops:
  0.0 34.4 %collective-permute-start.16 = (f32[64,128,128]{2,1,0:T(8,128)}, f32[64,128,128]{2,1,0:T(8,128)}, u32[]{:S(2)}, u32[]{:S(2)}) collective-permute-start(f32[64,128,128]{2,1,0:T(8,128)} %own_ref.1), channel_id=1, source_target_pairs={{0,4},{4,0},{8,12},{12,8},{16,20},{20,16},{24,28},{28,24},{1,5},{5... | collective-permute-start | bytes 12582920 | tf_op jit(solution)/shard_map/ppermute | solution.py:278
  2.0 12.5 %collective-permute-start.4 = (f32[3,64,128]{2,1,0:T(8,128)S(1)}, f32[3,64,128]{2,1,0:T(8,128)S(1)}, u32[]{:S(2)}, u32[]{:S(2)}) collective-permute-start(f32[3,64,128]{2,1,0:T(8,128)S(1)} %get-tuple-element.13), channel_id=1, source_target_pairs={{0,2},{1,3},{2,0},{3,1},{4,6},{5,7},{6,4},{7,5},{8,10},{9,11},{10,... | collective-permute-start | bytes 294920 | tf_op jit(solution)/shard_map/ppermute | solution.py:281
  2.4 15.2 %collective-permute-start.12 = (f32[3,128,128]{2,1,0:T(8,128)S(1)}, f32[3,128,128]{2,1,0:T(8,128)S(1)}, u32[]{:S(2)}, u32[]{:S(2)}) collective-permute-start(f32[3,128,128]{2,1,0:T(8,128)S(1)} %get-tuple-element.12), channel_id=1, source_target_pairs={{0,3},{1,0},{2,1},{3,2},{4,7},{5,4},{6,5},{7,6},{8,11},{9,8},{10,9... | collective-permute-start | bytes 589832 | tf_op jit(solution)/shard_map/ppermute | solution.py:281
  2.5 18.3 %collective-permute-start = (f32[3,128,128]{2,1,0:T(8,128)S(1)}, f32[3,128,128]{2,1,0:T(8,128)S(1)}, u32[]{:S(2)}, u32[]{:S(2)}) collective-permute-start(f32[3,128,128]{2,1,0:T(8,128)S(1)} %get-tuple-element.12), channel_id=1, source_target_pairs={{0,1},{1,2},{2,3},{3,0},{4,5},{5,6},{6,7},{7,4},{8,9},{9,10},{10,1... | collective-permute-start | bytes 589832 | tf_op jit(solution)/shard_map/ppermute | solution.py:281
  14.4 5.8 %collective-permute-start.6 = (f32[224,128]{1,0:T(8,128)S(1)}, f32[224,128]{1,0:T(8,128)S(1)}, u32[]{:S(2)}, u32[]{:S(2)}) collective-permute-start(f32[224,128]{1,0:T(8,128)S(1)} %pad_maximum_fusion.refs_4_), channel_id=1, source_target_pairs={{0,8},{4,20},{8,0},{12,28},{16,24},{20,4},{24,16},{28,12},{1,9},{5... | collective-permute-start | bytes 344072 | tf_op jit(solution)/shard_map/ppermute | solution.py:333
  16.0 4.8 %collective-permute-start.5 = (f32[224,128]{1,0:T(8,128)S(1)}, f32[224,128]{1,0:T(8,128)S(1)}, u32[]{:S(2)}, u32[]{:S(2)}) collective-permute-start(f32[224,128]{1,0:T(8,128)S(1)} %pad_maximum_fusion.refs_4_), channel_id=1, source_target_pairs={{0,16},{4,12},{8,24},{12,4},{16,0},{20,28},{24,8},{28,20},{1,17},{... | collective-permute-start | bytes 344072 | tf_op jit(solution)/shard_map/ppermute | solution.py:333
  17.5 4.7 %collective-permute-start.8 = (f32[224,128]{1,0:T(8,128)S(1)}, f32[224,128]{1,0:T(8,128)S(1)}, u32[]{:S(2)}, u32[]{:S(2)}) collective-permute-start(f32[224,128]{1,0:T(8,128)S(1)} %pad_maximum_fusion.refs_4_), channel_id=1, source_target_pairs={{0,4},{4,0},{8,12},{12,8},{16,20},{20,16},{24,28},{28,24},{1,5},{5... | collective-permute-start | bytes 344072 | tf_op jit(solution)/shard_map/ppermute | solution.py:278
  20.2 2.6 %collective-permute-start.10 = (f32[224,128]{1,0:T(8,128)S(1)}, f32[224,128]{1,0:T(8,128)S(1)}, u32[]{:S(2)}, u32[]{:S(2)}) collective-permute-start(f32[224,128]{1,0:T(8,128)S(1)} %collective-permute-done.6.refs_6_), channel_id=1, source_target_pairs={{0,4},{4,0},{8,12},{12,8},{16,20},{20,16},{24,28},{28,24},{1,5},{5... | collective-permute-start | bytes 344072 | tf_op jit(solution)/shard_map/ppermute | solution.py:278
  20.8 3.5 %collective-permute-start.9 = (f32[224,128]{1,0:T(8,128)S(1)}, f32[224,128]{1,0:T(8,128)S(1)}, u32[]{:S(2)}, u32[]{:S(2)}) collective-permute-start(f32[224,128]{1,0:T(8,128)S(1)} %collective-permute-done.5.refs_5_), channel_id=1, source_target_pairs={{0,4},{4,0},{8,12},{12,8},{16,20},{20,16},{24,28},{28,24},{1,5},{5... | collective-permute-start | bytes 344072 | tf_op jit(solution)/shard_map/ppermute | solution.py:278
  20.8 9.0 %collective-permute-start.13 = (f32[3,128,128]{2,1,0:T(8,128)S(1)}, f32[3,128,128]{2,1,0:T(8,128)S(1)}, u32[]{:S(2)}, u32[]{:S(2)}) collective-permute-start(f32[3,128,128]{2,1,0:T(8,128)S(1)} %collective-permute-done.12.refs_12_), channel_id=1, source_target_pairs={{0,8},{4,20},{8,0},{12,28},{16,24},{20,4},{24,16},{28,12},{1,9},{5... | collective-permute-start | bytes 589832 | tf_op jit(solution)/shard_map/ppermute | solution.py:333
  22.3 8.1 %collective-permute-start.1 = (f32[3,128,128]{2,1,0:T(8,128)S(1)}, f32[3,128,128]{2,1,0:T(8,128)S(1)}, u32[]{:S(2)}, u32[]{:S(2)}) collective-permute-start(f32[3,128,128]{2,1,0:T(8,128)S(1)} %collective-permute-done.refs_0_), channel_id=1, source_target_pairs={{0,8},{4,20},{8,0},{12,28},{16,24},{20,4},{24,16},{28,12},{1,9},{5... | collective-permute-start | bytes 589832 | tf_op jit(solution)/shard_map/ppermute | solution.py:333
  22.8 7.0 %collective-permute-start.7 = (f32[224,128]{1,0:T(8,128)S(1)}, f32[224,128]{1,0:T(8,128)S(1)}, u32[]{:S(2)}, u32[]{:S(2)}) collective-permute-start(f32[224,128]{1,0:T(8,128)S(1)} %collective-permute-done.5.refs_5_), channel_id=1, source_target_pairs={{0,8},{4,20},{8,0},{12,28},{16,24},{20,4},{24,16},{28,12},{1,9},{5... | collective-permute-start | bytes 344072 | tf_op jit(solution)/shard_map/ppermute | solution.py:333
  24.3 6.1 %collective-permute-start.14 = (f32[3,128,128]{2,1,0:T(8,128)S(1)}, f32[3,128,128]{2,1,0:T(8,128)S(1)}, u32[]{:S(2)}, u32[]{:S(2)}) collective-permute-start(f32[3,128,128]{2,1,0:T(8,128)S(1)} %collective-permute-done.12.refs_12_), channel_id=1, source_target_pairs={{0,4},{4,0},{8,12},{12,8},{16,20},{20,16},{24,28},{28,24},{1,5},{5... | collective-permute-start | bytes 589832 | tf_op jit(solution)/shard_map/ppermute | solution.py:278
  29.8 3.5 %collective-permute-start.2 = (f32[3,128,128]{2,1,0:T(8,128)S(1)}, f32[3,128,128]{2,1,0:T(8,128)S(1)}, u32[]{:S(2)}, u32[]{:S(2)}) collective-permute-start(f32[3,128,128]{2,1,0:T(8,128)S(1)} %collective-permute-done.refs_0_), channel_id=1, source_target_pairs={{0,4},{4,0},{8,12},{12,8},{16,20},{20,16},{24,28},{28,24},{1,5},{5... | collective-permute-start | bytes 589832 | tf_op jit(solution)/shard_map/ppermute | solution.py:278
  29.8 3.5 %collective-permute-start.15 = (f32[3,128,128]{2,1,0:T(8,128)S(1)}, f32[3,128,128]{2,1,0:T(8,128)S(1)}, u32[]{:S(2)}, u32[]{:S(2)}) collective-permute-start(f32[3,128,128]{2,1,0:T(8,128)S(1)} %collective-permute-done.13.refs_13_), channel_id=1, source_target_pairs={{0,4},{4,0},{8,12},{12,8},{16,20},{20,16},{24,28},{28,24},{1,5},{5... | collective-permute-start | bytes 589832 | tf_op jit(solution)/shard_map/ppermute | solution.py:278
  30.3 3.0 %collective-permute-start.3 = (f32[3,128,128]{2,1,0:T(8,128)S(1)}, f32[3,128,128]{2,1,0:T(8,128)S(1)}, u32[]{:S(2)}, u32[]{:S(2)}) collective-permute-start(f32[3,128,128]{2,1,0:T(8,128)S(1)} %collective-permute-done.1.refs_1_), channel_id=1, source_target_pairs={{0,4},{4,0},{8,12},{12,8},{16,20},{20,16},{24,28},{28,24},{1,5},{5... | collective-permute-start | bytes 589832 | tf_op jit(solution)/shard_map/ppermute | solution.py:278
  30.4 2.9 %collective-permute-start.11 = (f32[224,128]{1,0:T(8,128)S(1)}, f32[224,128]{1,0:T(8,128)S(1)}, u32[]{:S(2)}, u32[]{:S(2)}) collective-permute-start(f32[224,128]{1,0:T(8,128)S(1)} %collective-permute-done.7.refs_7_), channel_id=1, source_target_pairs={{0,4},{4,0},{8,12},{12,8},{16,20},{20,16},{24,28},{28,24},{1,5},{5... | collective-permute-start | bytes 344072 | tf_op jit(solution)/shard_map/ppermute | solution.py:278
  39.6 9.6 %collective-permute-start.18 = (f32[4,128,128]{2,1,0:T(8,128)S(1)}, f32[4,128,128]{2,1,0:T(8,128)S(1)}, u32[]{:S(2)}, u32[]{:S(2)}) collective-permute-start(f32[4,128,128]{2,1,0:T(8,128)S(1)} %shard_map.90), channel_id=1, source_target_pairs={{0,8},{4,20},{8,0},{12,28},{16,24},{20,4},{24,16},{28,12},{1,9},{5... | collective-permute-start | bytes 786440 | tf_op jit(solution)/shard_map/ppermute | solution.py:381
  42.6 10.5 %collective-permute-start.21 = (f32[4,128,128]{2,1,0:T(8,128)S(1)}, f32[4,128,128]{2,1,0:T(8,128)S(1)}, u32[]{:S(2)}, u32[]{:S(2)}) collective-permute-start(f32[4,128,128]{2,1,0:T(8,128)S(1)} %shard_map.95), channel_id=1, source_target_pairs={{0,8},{4,20},{8,0},{12,28},{16,24},{20,4},{24,16},{28,12},{1,9},{5... | collective-permute-start | bytes 786440 | tf_op jit(solution)/shard_map/ppermute | solution.py:381
  44.8 11.9 %collective-permute-start.17 = (f32[4,128,128]{2,1,0:T(8,128)S(1)}, f32[4,128,128]{2,1,0:T(8,128)S(1)}, u32[]{:S(2)}, u32[]{:S(2)}) collective-permute-start(f32[4,128,128]{2,1,0:T(8,128)S(1)} %shard_map.88), channel_id=1, source_target_pairs={{0,8},{4,20},{8,0},{12,28},{16,24},{20,4},{24,16},{28,12},{1,9},{5... | collective-permute-start | bytes 786440 | tf_op jit(solution)/shard_map/ppermute | solution.py:381
  49.2 8.6 %collective-permute-start.19 = (f32[4,128,128]{2,1,0:T(8,128)S(1)}, f32[4,128,128]{2,1,0:T(8,128)S(1)}, u32[]{:S(2)}, u32[]{:S(2)}) collective-permute-start(f32[4,128,128]{2,1,0:T(8,128)S(1)} %add.11), channel_id=1, source_target_pairs={{0,16},{4,12},{8,24},{12,4},{16,0},{20,28},{24,8},{28,20},{1,17},{... | collective-permute-start | bytes 786440 | tf_op jit(solution)/shard_map/ppermute | solution.py:381
  51.8 8.5 %collective-permute-start.20 = (f32[4,128,128]{2,1,0:T(8,128)S(1)}, f32[4,128,128]{2,1,0:T(8,128)S(1)}, u32[]{:S(2)}, u32[]{:S(2)}) collective-permute-start(f32[4,128,128]{2,1,0:T(8,128)S(1)} %shard_map.93), channel_id=1, source_target_pairs={{0,8},{4,20},{8,0},{12,28},{16,24},{20,4},{24,16},{28,12},{1,9},{5... | collective-permute-start | bytes 786440 | tf_op jit(solution)/shard_map/ppermute | solution.py:381
  53.2 7.4 %collective-permute-start.22 = (f32[4,128,128]{2,1,0:T(8,128)S(1)}, f32[4,128,128]{2,1,0:T(8,128)S(1)}, u32[]{:S(2)}, u32[]{:S(2)}) collective-permute-start(f32[4,128,128]{2,1,0:T(8,128)S(1)} %add.12), channel_id=1, source_target_pairs={{0,16},{4,12},{8,24},{12,4},{16,0},{20,28},{24,8},{28,20},{1,17},{... | collective-permute-start | bytes 786440 | tf_op jit(solution)/shard_map/ppermute | solution.py:381
  55.3 2.5 %copy-start = (f32[8,128,128]{2,1,0:T(8,128)S(1)}, f32[8,128,128]{2,1,0:T(8,128)}, u32[]{:S(2)}) copy-start(f32[8,128,128]{2,1,0:T(8,128)} %left_ref.3) | copy-start | bytes 1572868

commit v6 on v4

--- a/solution.py
+++ b/solution.py
@@ -84,6 +84,8 @@
     offset = jnp.zeros((16, 1), F32)
     total = jnp.zeros((8, chips * span), F32)
     for i in range(blocks):
+        if i == blocks // 2:
+            first_half = offset
         col, own, place = words[0, i : i + 1], words[1, i : i + 1], words[2, i : i + 1]
         chip = jnp.where(lanes((1, listed)) < counts[i], own >> 1, chips)
         match = (kinds == chip).astype(F32)
@@ -110,6 +112,8 @@
     for c in range(chips):
         part = total[:, c * span : (c + 1) * span]
         number = jnp.broadcast_to(offset[c : c + 1], (8, span))
+        number_half = jnp.broadcast_to(first_half[c : c + 1], (8, span))
+        part = jnp.where(row == 4, number_half, part)
         part = jnp.where(row == 0, number, jnp.where(row == 2, part + columns, part))
         out_ref[8 * c : 8 * c + 8] = part
 
@@ -184,34 +188,39 @@
         at += 8
 
 
-def entry_kernel(lists, tiles_ref, proj_ref, out_ref):
-    _, _, width = out_ref.shape
+def entry_kernel(half, lists, tiles_ref, proj_ref, out_ref):
+    blocks, _, width = out_ref.shape
+    zeros = proj_ref.shape[0] - 1
+    first = lists[4, 0] if half == 1 else 0
+    last = lists[4, 0] if half == 0 else lists[0, 0]
     out_ref[...] = jnp.zeros_like(out_ref)
 
     def multiply(base, n):
         terms = []
         for u in range(n):
-            proj = proj_ref[lists[2, base + u]]
+            at = base + u
+            proj = proj_ref[jnp.where(at < last, lists[2, at], zeros)]
             d = jnp.dot(
-                tiles_ref[lists[1, base + u]],
+                tiles_ref[lists[1, at]],
                 jnp.concatenate([proj, proj], axis=0),
                 preferred_element_type=F32,
             )
             terms.append(d[:, :width] + d[:, width:])
         for u in range(n):
-            out_ref[lists[3, base + u]] += terms[u]
+            block = lists[3, base + u] - (blocks if half == 1 else 0)
+            out_ref[jnp.clip(block, 0, blocks - 1)] += terms[u]
 
     def step(s, _):
-        multiply(s * UNROLL, UNROLL)
+        multiply(first + s * UNROLL, UNROLL)
         return 0
 
-    number = lists[0, 0]
+    number = last - first
     steps = (number + UNROLL // 2 - 1) // UNROLL
     lax.fori_loop(0, steps, step, 0)
 
     @pl.when(number > steps * UNROLL)
     def _():
-        multiply(steps * UNROLL, UNROLL // 2)
+        multiply(first + steps * UNROLL, UNROLL // 2)
 
 
 def final_kernel(left_ref, *refs):
@@ -347,18 +356,21 @@
         out_spec=[VMEM] * (1 + chips),
     )
 
-    total = {
-        m: [
-            call(
-                entry_kernel, 1, [VMEM, VMEM],
-                jax.ShapeDtypeStruct((blocks, coarse, vecs), F32),
-                [], (tables[m], packed, proj),
-                cost(cap * 128**3 * 8, 4 * MIB), 12 * MIB,
-            )
-        ]
-        for m in range(chips)
-    }
-    for m in masks_of(chips):
+    def sum_of(m, half=None):
+        return call(
+            functools.partial(entry_kernel, half), 1, [VMEM, VMEM],
+            jax.ShapeDtypeStruct((blocks if half is None else blocks // 2, coarse, vecs), F32),
+            [], (tables[m], packed, proj), cost(cap * 128**3 * 4, 4 * MIB), 12 * MIB,
+        )
+
+    masks = masks_of(chips)
+    total = {m: [sum_of(m)] for m in range(chips) if m != masks[0]}
+    arriving = []
+    for half in range(2):
+        value = sum_of(masks[0], half)
+        arriving.append(lax.ppermute(value, "rows", across(1)))
+    total[masks[0] ^ 1].append(jnp.concatenate(arriving, axis=0))
+    for m in masks[1:]:
         bit = m & -m
         value = functools.reduce(jnp.add, total[m])
         total[m ^ bit].append(lax.ppermute(value, "rows", across(bit)))

time: 62.2 us -> 63 us (1.013)
  Pallas kernels: 19.5 us -> 20.3 us
    ppermute x3 -> x2, waiting for transfers between devices: 13.6 us -> 10.3 us  [work(): total[m ^ bit].append(lax.ppermute(value, 'rows', across(bit)))]
    ppermute x0 -> x2, waiting for transfers between devices: none -> 3.27 us  [work(): arriving.append(lax.ppermute(value, 'rows', across(1)))]
    ppermute x0 -> x2, starting transfers between devices: none -> 1.52 us  [work(): arriving.append(lax.ppermute(value, 'rows', across(1)))]
    ppermute x3 -> x2, starting transfers between devices: 1.66 us -> 0.21 us  [work(): total[m ^ bit].append(lax.ppermute(value, 'rows', across(bit)))]
    pallas_call x10 -> x11, Pallas kernels: 19.5 us -> 20.3 us  [call(): pl.pallas_call(kernel, out_shape=out, grid_spec=pltpu.PrefetchScalarGridS...]
  transfers between devices with their start and end apart: 20 -> 21, of which waited for: 6 -> 7; matrix products, arithmetic and copies ran while one was open for 0% -> 0% of each run, Pallas kernels for 20% -> 20%
where the time goes in v6:
time: 63 us; the launch traced here: 62.8 us
  waiting for transfers between devices  26.5 us (42%)
  Pallas kernels  20.3 us (32%)
  starting transfers between devices  15.7 us (25%)
    pallas_call x11, Pallas kernels, call(): pl.pallas_call(kernel, out_shape=out, grid_spec=pltpu.PrefetchScalarGridS...  20.3 us
    ppermute x2, waiting for transfers between devices, work(): total[m ^ bit].append(lax.ppermute(value, 'rows', across(bit)))  10.3 us
    ppermute x9, starting transfers between devices, swap(): return lax.ppermute(x, 'rows', [(r, r ^ 1) for r in range(rows)])  7.36 us
    ppermute x5, waiting for transfers between devices, spread(): return lax.ppermute(x, 'rows', across(mask))  6.55 us
    ppermute x3, waiting for transfers between devices, turn(): lax.ppermute(x, 'blk', [(b, (b + k) % planes) for b in range(planes)])  6.42 us
    ppermute x3, starting transfers between devices, turn(): lax.ppermute(x, 'blk', [(b, (b + k) % planes) for b in range(planes)])  3.39 us
    ppermute x2, waiting for transfers between devices, work(): arriving.append(lax.ppermute(value, 'rows', across(1)))  3.27 us
    ppermute x5, starting transfers between devices, spread(): return lax.ppermute(x, 'rows', across(mask))  3.19 us
  transfers between devices with their start and end apart: 21, of which 7 were waited for; matrix products, arithmetic and copies ran while one was open for 0% of the time, Pallas kernels for 20%

profile of v6, /device:TPU:29, one launch (start us, length us, event | category | flops | bytes accessed | tf_op | source)
XLA Modules:
  0.0 62.8 jit_solution(6526786351744922214)
XLA Ops:
  0.0 0.7 %collective-permute-start.16 = (f32[64,128,128]{2,1,0:T(8,128)}, f32[64,128,128]{2,1,0:T(8,128)}, u32[]{:S(2)}, u32[]{:S(2)}) collective-permute-start(f32[64,128,128]{2,1,0:T(8,128)} %own_ref.1), channel_id=1, source_target_pairs={{0,4},{4,0},{8,12},{12,8},{16,20},{20,16},{24,28},{28,24},{1,5},{5... | collective-permute-start | bytes 12582920 | tf_op jit(solution)/shard_map/ppermute | solution.py:272
  0.7 0.1 stack.36.place
  0.8 1.9 %shard_map.83 = (f32[3,128,128]{2,1,0:T(8,128)S(1)}, f32[3,64,128]{2,1,0:T(8,128)S(1)}) custom-call(s32[9]{0:T(128)S(1)} %stack.36.place, f32[12,128,128]{2,1,0:T(8,128)} %bitcast.12, f32[12,128,128]{2,1,0:T(8,128)} %r_ref.3), custom_call_target="tpu_custom_call" | custom-call | flops 37748736 | bytes 393216 | tf_op jit(solution)/shard_map/pallas_call | solution.py:234
  2.6 0.1 collective-permute-start.4
  2.8 0.2 collective-permute-start.12
  2.9 3.1 %collective-permute-start = (f32[3,128,128]{2,1,0:T(8,128)S(1)}, f32[3,128,128]{2,1,0:T(8,128)S(1)}, u32[]{:S(2)}, u32[]{:S(2)}) collective-permute-start(f32[3,128,128]{2,1,0:T(8,128)S(1)} %get-tuple-element.12), channel_id=1, source_target_pairs={{0,1},{1,2},{2,3},{3,0},{4,5},{5,6},{6,7},{7,4},{8,9},{9,10},{10,1... | collective-permute-start | bytes 589832 | tf_op jit(solution)/shard_map/ppermute | solution.py:275
  6.0 2.2 %shard_map.84.refs_16_ = f32[32,128]{1,0:T(8,128)S(1)} custom-call(s32[8,32]{1,0:T(8,128)} %cols.1, s32[8,32]{1,0:T(8,128)} %owner.1, s32[8,32]{1,0:T(8,128)} %slot.1, s32[8]{0:T(128)} %number.1), custom_call_target="tpu_custom_call" | custom-call | flops 100000000 | bytes 16384 | tf_op jit(solution)/shard_map/pallas_call | solution.py:234
  8.2 6.4 %collective-permute-done.4 = f32[3,64,128]{2,1,0:T(8,128)S(1)} collective-permute-done((f32[3,64,128]{2,1,0:T(8,128)S(1)}, f32[3,64,128]{2,1,0:T(8,128)S(1)}, u32[]{:S(2)}, u32[]{:S(2)}) %collective-permute-start.4) | collective-permute-done | bytes 98336 | tf_op jit(solution)/shard_map/ppermute | solution.py:275
  14.6 0.3 collective-permute-start.6
  14.9 1.2 %collective-permute-start.5 = (f32[224,128]{1,0:T(8,128)S(1)}, f32[224,128]{1,0:T(8,128)S(1)}, u32[]{:S(2)}, u32[]{:S(2)}) collective-permute-start(f32[224,128]{1,0:T(8,128)S(1)} %pad_maximum_fusion.refs_4_), channel_id=1, source_target_pairs={{0,16},{4,12},{8,24},{12,4},{16,0},{20,28},{24,8},{28,20},{1,17},{... | collective-permute-start | bytes 344072 | tf_op jit(solution)/shard_map/ppermute | solution.py:327
  16.1 0.0 collective-permute-done.12.refs_12_
  16.1 1.1 %collective-permute-start.8 = (f32[224,128]{1,0:T(8,128)S(1)}, f32[224,128]{1,0:T(8,128)S(1)}, u32[]{:S(2)}, u32[]{:S(2)}) collective-permute-start(f32[224,128]{1,0:T(8,128)S(1)} %pad_maximum_fusion.refs_4_), channel_id=1, source_target_pairs={{0,4},{4,0},{8,12},{12,8},{16,20},{20,16},{24,28},{28,24},{1,5},{5... | collective-permute-start | bytes 344072 | tf_op jit(solution)/shard_map/ppermute | solution.py:272
  17.2 1.4 %collective-permute-done.6.refs_6_ = f32[224,128]{1,0:T(8,128)S(1)} collective-permute-done((f32[224,128]{1,0:T(8,128)S(1)}, f32[224,128]{1,0:T(8,128)S(1)}, u32[]{:S(2)}, u32[]{:S(2)}) %collective-permute-start.6) | collective-permute-done | bytes 114720 | tf_op jit(solution)/shard_map/ppermute | solution.py:327
  18.6 1.9 %collective-permute-start.10 = (f32[224,128]{1,0:T(8,128)S(1)}, f32[224,128]{1,0:T(8,128)S(1)}, u32[]{:S(2)}, u32[]{:S(2)}) collective-permute-start(f32[224,128]{1,0:T(8,128)S(1)} %collective-permute-done.6.refs_6_), channel_id=1, source_target_pairs={{0,4},{4,0},{8,12},{12,8},{16,20},{20,16},{24,28},{28,24},{1,5},{5... | collective-permute-start | bytes 344072 | tf_op jit(solution)/shard_map/ppermute | solution.py:272
  20.5 0.0 collective-permute-done.5.refs_5_
  20.5 1.0 %collective-permute-start.9 = (f32[224,128]{1,0:T(8,128)S(1)}, f32[224,128]{1,0:T(8,128)S(1)}, u32[]{:S(2)}, u32[]{:S(2)}) collective-permute-start(f32[224,128]{1,0:T(8,128)S(1)} %collective-permute-done.5.refs_5_), channel_id=1, source_target_pairs={{0,4},{4,0},{8,12},{12,8},{16,20},{20,16},{24,28},{28,24},{1,5},{5... | collective-permute-start | bytes 344072 | tf_op jit(solution)/shard_map/ppermute | solution.py:272
  21.5 0.0 collective-permute-done.refs_0_
  21.5 0.2 collective-permute-start.13
  21.7 1.2 %collective-permute-start.1 = (f32[3,128,128]{2,1,0:T(8,128)S(1)}, f32[3,128,128]{2,1,0:T(8,128)S(1)}, u32[]{:S(2)}, u32[]{:S(2)}) collective-permute-start(f32[3,128,128]{2,1,0:T(8,128)S(1)} %collective-permute-done.refs_0_), channel_id=1, source_target_pairs={{0,8},{4,20},{8,0},{12,28},{16,24},{20,4},{24,16},{28,12},{1,9},{5... | collective-permute-start | bytes 589832 | tf_op jit(solution)/shard_map/ppermute | solution.py:327
  23.0 0.2 collective-permute-start.7
  23.2 0.0 collective-permute-done.9.refs_9_
  23.2 1.3 %collective-permute-start.14 = (f32[3,128,128]{2,1,0:T(8,128)S(1)}, f32[3,128,128]{2,1,0:T(8,128)S(1)}, u32[]{:S(2)}, u32[]{:S(2)}) collective-permute-start(f32[3,128,128]{2,1,0:T(8,128)S(1)} %collective-permute-done.12.refs_12_), channel_id=1, source_target_pairs={{0,4},{4,0},{8,12},{12,8},{16,20},{20,16},{24,28},{28,24},{1,5},{5... | collective-permute-start | bytes 589832 | tf_op jit(solution)/shard_map/ppermute | solution.py:272
  24.5 5.1 %collective-permute-done.7.refs_7_ = f32[224,128]{1,0:T(8,128)S(1)} collective-permute-done((f32[224,128]{1,0:T(8,128)S(1)}, f32[224,128]{1,0:T(8,128)S(1)}, u32[]{:S(2)}, u32[]{:S(2)}) %collective-permute-start.7) | collective-permute-done | bytes 114720 | tf_op jit(solution)/shard_map/ppermute | solution.py:327
  29.6 0.9 %collective-permute-start.2 = (f32[3,128,128]{2,1,0:T(8,128)S(1)}, f32[3,128,128]{2,1,0:T(8,128)S(1)}, u32[]{:S(2)}, u32[]{:S(2)}) collective-permute-start(f32[3,128,128]{2,1,0:T(8,128)S(1)} %collective-permute-done.refs_0_), channel_id=1, source_target_pairs={{0,4},{4,0},{8,12},{12,8},{16,20},{20,16},{24,28},{28,24},{1,5},{5... | collective-permute-start | bytes 589832 | tf_op jit(solution)/shard_map/ppermute | solution.py:272
  30.5 0.0 collective-permute-start.15
  30.5 0.0 collective-permute-done.1.refs_1_
  30.5 0.5 collective-permute-start.3
  31.0 0.1 collective-permute-start.11
  31.1 2.4 %shard_map.82.own_ref = f32[12,128,128]{2,1,0:T(8,128)S(1)} custom-call(s32[9]{0:T(128)S(1)} %stack.36.place, f32[12,128,128]{2,1,0:T(8,128)} %bitcast.13, f32[12,128,128]{2,1,0:T(8,128)} %r_ref.3), custom_call_target="tpu_custom_call" | custom-call | flops 150994944 | bytes 1572864 | tf_op jit(solution)/shard_map/pallas_call | solution.py:234
  33.5 0.0 collective-permute-done.11.refs_11_
  33.6 1.1 %shard_map.85 = (bf16[49,128,256]{2,1,0:T(8,128)(2,1)S(1)}, s32[8,128]{1,0:T(8,128)S(1)}, s32[8,128]{1,0:T(8,128)S(1)}, s32[8,128]{1,0:T(8,128)S(1)}, s32[8,128]{1,0:T(8,128)S(1)}) custom-call(s32[9]{0:T(128)S(1)} %stack.36.place, f32[12,128,128]{2,1,0:T(8,128)S(1)} %shard_map.82.own_ref, f32[3,128,128]{2,1,0:T(8,128)S(1)} %collective-permute-done.refs_0_, ...), custom_call_target="tpu_custom_call" | custom-call | flops 1000000 | bytes 4718592 | tf_op jit(solution)/shard_map/pallas_call | solution.py:234
  34.7 3.6 %shard_map.86.tiles_ref = bf16[128,128,256]{2,1,0:T(8,128)(2,1)S(1)} custom-call(s32[1]{0:T(128)} %bitcast.10.core, f32[64,128,128]{2,1,0:T(8,128)} %own_ref.1, f32[64,128,128]{2,1,0:T(8,128)} %collective-permute-done.16.other_ref), custom_call_target="tpu_custom_call" | custom-call | flops 16777216 | bytes 16777216 | tf_op jit(solution)/shard_map/pallas_call | solution.py:234
  38.3 1.5 %shard_map.91 = f32[4,128,128]{2,1,0:T(8,128)S(1)} custom-call(s32[8,128]{1,0:T(8,128)S(1)} %get-tuple-element.18.lists, bf16[128,128,256]{2,1,0:T(8,128)(2,1)S(1)} %shard_map.86.tiles_ref, bf16[49,128,256]{2,1,0:T(8,128)(2,1)S(1)} %get-tuple-element.15.proj_ref), custom_call_target="tpu_custom_call" | custom-call | flops 536870912 | bytes 4194304 | tf_op jit(solution)/shard_map/pallas_call | solution.py:234
  39.8 1.6 %shard_map.90 = f32[4,128,128]{2,1,0:T(8,128)S(1)} custom-call(s32[8,128]{1,0:T(8,128)S(1)} %get-tuple-element.18.lists, bf16[128,128,256]{2,1,0:T(8,128)(2,1)S(1)} %shard_map.86.tiles_ref, bf16[49,128,256]{2,1,0:T(8,128)(2,1)S(1)} %get-tuple-element.15.proj_ref), custom_call_target="tpu_custom_call" | custom-call | flops 536870912 | bytes 4194304 | tf_op jit(solution)/shard_map/pallas_call | solution.py:234
  41.4 0.1 collective-permute-start.18
  41.5 1.5 %collective-permute-start.19 = (f32[4,128,128]{2,1,0:T(8,128)S(1)}, f32[4,128,128]{2,1,0:T(8,128)S(1)}, u32[]{:S(2)}, u32[]{:S(2)}) collective-permute-start(f32[4,128,128]{2,1,0:T(8,128)S(1)} %shard_map.91), channel_id=1, source_target_pairs={{0,8},{4,20},{8,0},{12,28},{16,24},{20,4},{24,16},{28,12},{1,9},{5... | collective-permute-start | bytes 786440 | tf_op jit(solution)/shard_map/ppermute | solution.py:371
  42.9 1.4 %shard_map.88 = f32[8,128,128]{2,1,0:T(8,128)S(1)} custom-call(s32[8,128]{1,0:T(8,128)S(1)} %get-tuple-element.16.lists, bf16[128,128,256]{2,1,0:T(8,128)(2,1)S(1)} %shard_map.86.tiles_ref, bf16[49,128,256]{2,1,0:T(8,128)(2,1)S(1)} %get-tuple-element.15.proj_ref), custom_call_target="tpu_custom_call" | custom-call | flops 536870912 | bytes 4194304 | tf_op jit(solution)/shard_map/pallas_call | solution.py:234
  44.3 0.1 collective-permute-start.17
  44.5 2.0 %shard_map.89 = f32[8,128,128]{2,1,0:T(8,128)S(1)} custom-call(s32[8,128]{1,0:T(8,128)S(1)} %get-tuple-element.17.lists, bf16[128,128,256]{2,1,0:T(8,128)(2,1)S(1)} %shard_map.86.tiles_ref, bf16[49,128,256]{2,1,0:T(8,128)(2,1)S(1)} %get-tuple-element.15.proj_ref), custom_call_target="tpu_custom_call" | custom-call | flops 536870912 | bytes 4194304 | tf_op jit(solution)/shard_map/pallas_call | solution.py:234
  46.5 0.5 collective-permute-done.18
  47.0 2.8 %collective-permute-done.19 = f32[4,128,128]{2,1,0:T(8,128)S(1)} collective-permute-done((f32[4,128,128]{2,1,0:T(8,128)S(1)}, f32[4,128,128]{2,1,0:T(8,128)S(1)}, u32[]{:S(2)}, u32[]{:S(2)}) %collective-permute-start.19) | collective-permute-done | bytes 262176 | tf_op jit(solution)/shard_map/ppermute | solution.py:371
  49.8 0.1 maximum_add_fusion
  49.8 0.1 collective-permute-start.20
  49.9 0.0 copy-start
  49.9 1.4 %shard_map.87.refs_0_ = f32[8,128,128]{2,1,0:T(8,128)S(1)} custom-call(s32[8,128]{1,0:T(8,128)S(1)} %get-tuple-element.14.lists, bf16[128,128,256]{2,1,0:T(8,128)(2,1)S(1)} %shard_map.86.tiles_ref, bf16[49,128,256]{2,1,0:T(8,128)(2,1)S(1)} %get-tuple-element.15.proj_ref), custom_call_target="tpu_custom_call" | custom-call | flops 536870912 | bytes 4194304 | tf_op jit(solution)/shard_map/pallas_call | solution.py:234
  51.3 5.1 %collective-permute-done.17.refs_1_ = f32[8,128,128]{2,1,0:T(8,128)S(1)} collective-permute-done((f32[8,128,128]{2,1,0:T(8,128)S(1)}, f32[8,128,128]{2,1,0:T(8,128)S(1)}, u32[]{:S(2)}, u32[]{:S(2)}) %collective-permute-start.17) | collective-permute-done | bytes 524320 | tf_op jit(solution)/shard_map/ppermute | solution.py:376
  56.4 5.2 %collective-permute-done.20.refs_2_ = f32[8,128,128]{2,1,0:T(8,128)S(1)} collective-permute-done((f32[8,128,128]{2,1,0:T(8,128)S(1)}, f32[8,128,128]{2,1,0:T(8,128)S(1)}, u32[]{:S(2)}, u32[]{:S(2)}) %collective-permute-start.20) | collective-permute-done | bytes 524320 | tf_op jit(solution)/shard_map/ppermute | solution.py:376
  61.6 1.2 %shard_map.92 = f32[8,128,128]{2,1,0:T(8,128)} custom-call(f32[8,128,128]{2,1,0:T(8,128)S(1)} %copy-done, f32[8,128,128]{2,1,0:T(8,128)S(1)} %shard_map.87.refs_0_, f32[8,128,128]{2,1,0:T(8,128)S(1)} %collective-permute-done.17.refs_1_, f32[8,128,128]{2,1,0:T(8,128)S(1)} %collective-permute-done.20.refs_2_), custom_call_target="tpu_custom_call" | custom-call | flops 100663296 | bytes 2097152 | tf_op jit(solution)/shard_map/pallas_call | solution.py:234
  (10 shorter events, 0.0 us)
Async XLA Ops:
  0.0 34.6 %collective-permute-start.16 = (f32[64,128,128]{2,1,0:T(8,128)}, f32[64,128,128]{2,1,0:T(8,128)}, u32[]{:S(2)}, u32[]{:S(2)}) collective-permute-start(f32[64,128,128]{2,1,0:T(8,128)} %own_ref.1), channel_id=1, source_target_pairs={{0,4},{4,0},{8,12},{12,8},{16,20},{20,16},{24,28},{28,24},{1,5},{5... | collective-permute-start | bytes 12582920 | tf_op jit(solution)/shard_map/ppermute | solution.py:272
  2.6 12.0 %collective-permute-start.4 = (f32[3,64,128]{2,1,0:T(8,128)S(1)}, f32[3,64,128]{2,1,0:T(8,128)S(1)}, u32[]{:S(2)}, u32[]{:S(2)}) collective-permute-start(f32[3,64,128]{2,1,0:T(8,128)S(1)} %get-tuple-element.13), channel_id=1, source_target_pairs={{0,2},{1,3},{2,0},{3,1},{4,6},{5,7},{6,4},{7,5},{8,10},{9,11},{10,... | collective-permute-start | bytes 294920 | tf_op jit(solution)/shard_map/ppermute | solution.py:275
  2.8 13.4 %collective-permute-start.12 = (f32[3,128,128]{2,1,0:T(8,128)S(1)}, f32[3,128,128]{2,1,0:T(8,128)S(1)}, u32[]{:S(2)}, u32[]{:S(2)}) collective-permute-start(f32[3,128,128]{2,1,0:T(8,128)S(1)} %get-tuple-element.12), channel_id=1, source_target_pairs={{0,3},{1,0},{2,1},{3,2},{4,7},{5,4},{6,5},{7,6},{8,11},{9,8},{10,9... | collective-permute-start | bytes 589832 | tf_op jit(solution)/shard_map/ppermute | solution.py:275
  2.9 18.5 %collective-permute-start = (f32[3,128,128]{2,1,0:T(8,128)S(1)}, f32[3,128,128]{2,1,0:T(8,128)S(1)}, u32[]{:S(2)}, u32[]{:S(2)}) collective-permute-start(f32[3,128,128]{2,1,0:T(8,128)S(1)} %get-tuple-element.12), channel_id=1, source_target_pairs={{0,1},{1,2},{2,3},{3,0},{4,5},{5,6},{6,7},{7,4},{8,9},{9,10},{10,1... | collective-permute-start | bytes 589832 | tf_op jit(solution)/shard_map/ppermute | solution.py:275
  14.6 4.0 %collective-permute-start.6 = (f32[224,128]{1,0:T(8,128)S(1)}, f32[224,128]{1,0:T(8,128)S(1)}, u32[]{:S(2)}, u32[]{:S(2)}) collective-permute-start(f32[224,128]{1,0:T(8,128)S(1)} %pad_maximum_fusion.refs_4_), channel_id=1, source_target_pairs={{0,8},{4,20},{8,0},{12,28},{16,24},{20,4},{24,16},{28,12},{1,9},{5... | collective-permute-start | bytes 344072 | tf_op jit(solution)/shard_map/ppermute | solution.py:327
  14.9 5.6 %collective-permute-start.5 = (f32[224,128]{1,0:T(8,128)S(1)}, f32[224,128]{1,0:T(8,128)S(1)}, u32[]{:S(2)}, u32[]{:S(2)}) collective-permute-start(f32[224,128]{1,0:T(8,128)S(1)} %pad_maximum_fusion.refs_4_), channel_id=1, source_target_pairs={{0,16},{4,12},{8,24},{12,4},{16,0},{20,28},{24,8},{28,20},{1,17},{... | collective-permute-start | bytes 344072 | tf_op jit(solution)/shard_map/ppermute | solution.py:327
  16.1 5.6 %collective-permute-start.8 = (f32[224,128]{1,0:T(8,128)S(1)}, f32[224,128]{1,0:T(8,128)S(1)}, u32[]{:S(2)}, u32[]{:S(2)}) collective-permute-start(f32[224,128]{1,0:T(8,128)S(1)} %pad_maximum_fusion.refs_4_), channel_id=1, source_target_pairs={{0,4},{4,0},{8,12},{12,8},{16,20},{20,16},{24,28},{28,24},{1,5},{5... | collective-permute-start | bytes 344072 | tf_op jit(solution)/shard_map/ppermute | solution.py:272
  18.6 4.3 %collective-permute-start.10 = (f32[224,128]{1,0:T(8,128)S(1)}, f32[224,128]{1,0:T(8,128)S(1)}, u32[]{:S(2)}, u32[]{:S(2)}) collective-permute-start(f32[224,128]{1,0:T(8,128)S(1)} %collective-permute-done.6.refs_6_), channel_id=1, source_target_pairs={{0,4},{4,0},{8,12},{12,8},{16,20},{20,16},{24,28},{28,24},{1,5},{5... | collective-permute-start | bytes 344072 | tf_op jit(solution)/shard_map/ppermute | solution.py:272
  20.5 2.7 %collective-permute-start.9 = (f32[224,128]{1,0:T(8,128)S(1)}, f32[224,128]{1,0:T(8,128)S(1)}, u32[]{:S(2)}, u32[]{:S(2)}) collective-permute-start(f32[224,128]{1,0:T(8,128)S(1)} %collective-permute-done.5.refs_5_), channel_id=1, source_target_pairs={{0,4},{4,0},{8,12},{12,8},{16,20},{20,16},{24,28},{28,24},{1,5},{5... | collective-permute-start | bytes 344072 | tf_op jit(solution)/shard_map/ppermute | solution.py:272
  21.5 9.0 %collective-permute-start.13 = (f32[3,128,128]{2,1,0:T(8,128)S(1)}, f32[3,128,128]{2,1,0:T(8,128)S(1)}, u32[]{:S(2)}, u32[]{:S(2)}) collective-permute-start(f32[3,128,128]{2,1,0:T(8,128)S(1)} %collective-permute-done.12.refs_12_), channel_id=1, source_target_pairs={{0,8},{4,20},{8,0},{12,28},{16,24},{20,4},{24,16},{28,12},{1,9},{5... | collective-permute-start | bytes 589832 | tf_op jit(solution)/shard_map/ppermute | solution.py:327
  21.7 8.8 %collective-permute-start.1 = (f32[3,128,128]{2,1,0:T(8,128)S(1)}, f32[3,128,128]{2,1,0:T(8,128)S(1)}, u32[]{:S(2)}, u32[]{:S(2)}) collective-permute-start(f32[3,128,128]{2,1,0:T(8,128)S(1)} %collective-permute-done.refs_0_), channel_id=1, source_target_pairs={{0,8},{4,20},{8,0},{12,28},{16,24},{20,4},{24,16},{28,12},{1,9},{5... | collective-permute-start | bytes 589832 | tf_op jit(solution)/shard_map/ppermute | solution.py:327
  23.0 6.7 %collective-permute-start.7 = (f32[224,128]{1,0:T(8,128)S(1)}, f32[224,128]{1,0:T(8,128)S(1)}, u32[]{:S(2)}, u32[]{:S(2)}) collective-permute-start(f32[224,128]{1,0:T(8,128)S(1)} %collective-permute-done.5.refs_5_), channel_id=1, source_target_pairs={{0,8},{4,20},{8,0},{12,28},{16,24},{20,4},{24,16},{28,12},{1,9},{5... | collective-permute-start | bytes 344072 | tf_op jit(solution)/shard_map/ppermute | solution.py:327
  23.2 7.8 %collective-permute-start.14 = (f32[3,128,128]{2,1,0:T(8,128)S(1)}, f32[3,128,128]{2,1,0:T(8,128)S(1)}, u32[]{:S(2)}, u32[]{:S(2)}) collective-permute-start(f32[3,128,128]{2,1,0:T(8,128)S(1)} %collective-permute-done.12.refs_12_), channel_id=1, source_target_pairs={{0,4},{4,0},{8,12},{12,8},{16,20},{20,16},{24,28},{28,24},{1,5},{5... | collective-permute-start | bytes 589832 | tf_op jit(solution)/shard_map/ppermute | solution.py:272
  29.6 3.9 %collective-permute-start.2 = (f32[3,128,128]{2,1,0:T(8,128)S(1)}, f32[3,128,128]{2,1,0:T(8,128)S(1)}, u32[]{:S(2)}, u32[]{:S(2)}) collective-permute-start(f32[3,128,128]{2,1,0:T(8,128)S(1)} %collective-permute-done.refs_0_), channel_id=1, source_target_pairs={{0,4},{4,0},{8,12},{12,8},{16,20},{20,16},{24,28},{28,24},{1,5},{5... | collective-permute-start | bytes 589832 | tf_op jit(solution)/shard_map/ppermute | solution.py:272
  30.5 3.0 %collective-permute-start.15 = (f32[3,128,128]{2,1,0:T(8,128)S(1)}, f32[3,128,128]{2,1,0:T(8,128)S(1)}, u32[]{:S(2)}, u32[]{:S(2)}) collective-permute-start(f32[3,128,128]{2,1,0:T(8,128)S(1)} %collective-permute-done.13.refs_13_), channel_id=1, source_target_pairs={{0,4},{4,0},{8,12},{12,8},{16,20},{20,16},{24,28},{28,24},{1,5},{5... | collective-permute-start | bytes 589832 | tf_op jit(solution)/shard_map/ppermute | solution.py:272
  30.5 3.1 %collective-permute-start.3 = (f32[3,128,128]{2,1,0:T(8,128)S(1)}, f32[3,128,128]{2,1,0:T(8,128)S(1)}, u32[]{:S(2)}, u32[]{:S(2)}) collective-permute-start(f32[3,128,128]{2,1,0:T(8,128)S(1)} %collective-permute-done.1.refs_1_), channel_id=1, source_target_pairs={{0,4},{4,0},{8,12},{12,8},{16,20},{20,16},{24,28},{28,24},{1,5},{5... | collective-permute-start | bytes 589832 | tf_op jit(solution)/shard_map/ppermute | solution.py:272
  31.0 2.5 %collective-permute-start.11 = (f32[224,128]{1,0:T(8,128)S(1)}, f32[224,128]{1,0:T(8,128)S(1)}, u32[]{:S(2)}, u32[]{:S(2)}) collective-permute-start(f32[224,128]{1,0:T(8,128)S(1)} %collective-permute-done.7.refs_7_), channel_id=1, source_target_pairs={{0,4},{4,0},{8,12},{12,8},{16,20},{20,16},{24,28},{28,24},{1,5},{5... | collective-permute-start | bytes 344072 | tf_op jit(solution)/shard_map/ppermute | solution.py:272
  41.4 5.6 %collective-permute-start.18 = (f32[4,128,128]{2,1,0:T(8,128)S(1)}, f32[4,128,128]{2,1,0:T(8,128)S(1)}, u32[]{:S(2)}, u32[]{:S(2)}) collective-permute-start(f32[4,128,128]{2,1,0:T(8,128)S(1)} %shard_map.90), channel_id=1, source_target_pairs={{0,8},{4,20},{8,0},{12,28},{16,24},{20,4},{24,16},{28,12},{1,9},{5... | collective-permute-start | bytes 786440 | tf_op jit(solution)/shard_map/ppermute | solution.py:371
  41.5 8.3 %collective-permute-start.19 = (f32[4,128,128]{2,1,0:T(8,128)S(1)}, f32[4,128,128]{2,1,0:T(8,128)S(1)}, u32[]{:S(2)}, u32[]{:S(2)}) collective-permute-start(f32[4,128,128]{2,1,0:T(8,128)S(1)} %shard_map.91), channel_id=1, source_target_pairs={{0,8},{4,20},{8,0},{12,28},{16,24},{20,4},{24,16},{28,12},{1,9},{5... | collective-permute-start | bytes 786440 | tf_op jit(solution)/shard_map/ppermute | solution.py:371
  44.3 12.1 %collective-permute-start.17 = (f32[8,128,128]{2,1,0:T(8,128)S(1)}, f32[8,128,128]{2,1,0:T(8,128)S(1)}, u32[]{:S(2)}, u32[]{:S(2)}) collective-permute-start(f32[8,128,128]{2,1,0:T(8,128)S(1)} %shard_map.88), channel_id=1, source_target_pairs={{0,8},{4,20},{8,0},{12,28},{16,24},{20,4},{24,16},{28,12},{1,9},{5... | collective-permute-start | bytes 1572872 | tf_op jit(solution)/shard_map/ppermute | solution.py:376
  49.8 11.8 %collective-permute-start.20 = (f32[8,128,128]{2,1,0:T(8,128)S(1)}, f32[8,128,128]{2,1,0:T(8,128)S(1)}, u32[]{:S(2)}, u32[]{:S(2)}) collective-permute-start(f32[8,128,128]{2,1,0:T(8,128)S(1)} %maximum_add_fusion), channel_id=1, source_target_pairs={{0,16},{4,12},{8,24},{12,4},{16,0},{20,28},{24,8},{28,20},{1,17},{... | collective-permute-start | bytes 1572872 | tf_op jit(solution)/shard_map/ppermute | solution.py:376
  49.9 11.7 %copy-start = (f32[8,128,128]{2,1,0:T(8,128)S(1)}, f32[8,128,128]{2,1,0:T(8,128)}, u32[]{:S(2)}) copy-start(f32[8,128,128]{2,1,0:T(8,128)} %left_ref.1) | copy-start | bytes 1572868
